TPU v7x, 32 devices: a whole 2x2x4 slice. The times are simulated.
32 devices in a mesh: rep: 4 (over x, core), shard: 8 (over z, y).
Axes of the slice: x: 2, y: 2, z: 4, core: 2. Of those that a mesh axis runs over, the one named last changes fastest.
Arguments:
- tokens_in: bfloat16 [4, 2048, 768], P('rep', 'shard'), may hold values from -6 to 6
- segment_ids: int32 [4, 2048], P('rep'), may hold values from 0 to 15, never falling along the last dimension, each value on 1 to 1024 neighbouring positions
- w_qkv: bfloat16 [768, 2304], P('shard'), may hold values from -0.21875 to 0.21875
- w_out: bfloat16 [768, 768], P('shard'), may hold values from -2 to 2
- ln1_gain: bfloat16 [768], P('shard'), may hold values from 0.5 to 1.5
- ln1_bias: bfloat16 [768], P('shard'), may hold values from -3 to 3
- w_gate: bfloat16 [768, 3072], P('shard'), may hold values from -0.21875 to 0.21875
- w_up: bfloat16 [768, 3072], P('shard'), may hold values from -0.21875 to 0.21875
- w_down: bfloat16 [3072, 768], P('shard'), may hold values from -0.109375 to 0.109375
- ln2_gain: bfloat16 [768], P('shard'), may hold values from 0.5 to 1.5
- ln2_bias: bfloat16 [768], P('shard'), may hold values from -3 to 3
- out_cotangent: bfloat16 [4, 2048, 768], P('rep', 'shard'), may hold values from -6 to 6
Outputs:
- out: bfloat16 [4, 2048, 768], P('rep', 'shard')
- in_grad: float32 [4, 2048, 768], P('rep', 'shard')
- grad_w_qkv: float32 [768, 2304], P('shard')
- grad_w_out: float32 [768, 768], P('shard')
- grad_ln1_gain: float32 [768], P('shard')
- grad_ln1_bias: float32 [768], P('shard')
- grad_w_gate: float32 [768, 3072], P('shard')
- grad_w_up: float32 [768, 3072], P('shard')
- grad_w_down: float32 [3072, 768], P('shard')
- grad_ln2_gain: float32 [768], P('shard')
- grad_ln2_bias: float32 [768], P('shard')
Inputs may be any that keep to these rules, and one draw needn't show every extreme that they name: `segment_ids`: within each sequence the ids never fall; each of the 16 documents holds 1 to 1024 tokens and one holds exactly 1024.
All inputs are finite; a program needn't handle non-finite values.
Results may differ from a plain program's by a relative error of at most 0.023.
Values may be sent and summed in bfloat16 or wider, within the bound.
No kernel may reach another device: no remote copies, remote signals or barrier semaphores. Data moves between devices by JAX's collectives and lax.ppermute only.
A program may use at most 256 MiB of HBM per device.

v0:
```python
import jax
import jax.numpy as jnp
from jax import lax
from jax.sharding import PartitionSpec as P

D = 768
HEAD_DIM = 64
HEADS = 12


epsilon = 1e-05
rope_base = 1000.0


def rope_tables(start, count):
    positions = (start + jnp.arange(count, dtype=jnp.int32)).astype(jnp.float32)
    middle = HEAD_DIM // 2
    inverse = rope_base ** (-(2.0 * jnp.arange(middle).astype(jnp.float32)) / HEAD_DIM)
    angles = positions[:, None] * inverse[None, :]
    return (jnp.cos(angles)[:, None, :], jnp.sin(angles)[:, None, :])


def rotate(values_in, cosine, sine):
    middle = values_in.shape[-1] // 2
    first_half = values_in[..., :middle]
    second_half = values_in[..., middle:]
    return jnp.concatenate(
        [first_half * cosine - second_half * sine, second_half * cosine + first_half * sine],
        axis=-1,
    )


def rotate_back(upstream, cosine, sine):
    middle = upstream.shape[-1] // 2
    first_half = upstream[..., :middle]
    second_half = upstream[..., middle:]
    return jnp.concatenate(
        [first_half * cosine + second_half * sine, second_half * cosine - first_half * sine],
        axis=-1,
    )


def norm_forward(values_in, gain_vec, shift_vec):
    centred = values_in - jnp.mean(values_in, axis=-1, keepdims=True)
    variance = jnp.mean(centred * centred, axis=-1, keepdims=True)
    inverse_scale = lax.rsqrt(variance + epsilon)
    normed = centred * inverse_scale
    return (normed * gain_vec + shift_vec, normed, inverse_scale)


def norm_backward(upstream, normed, inverse_scale, gain_vec):
    scaled = upstream * gain_vec
    return inverse_scale * (
        scaled
        - jnp.mean(scaled, axis=-1, keepdims=True)
        - normed * jnp.mean(scaled * normed, axis=-1, keepdims=True)
    )


def fetch_attention(w_qkv, w_out, ln1_gain, ln1_bias):
    return (
        lax.all_gather(w_qkv, "shard", axis=0, tiled=True),
        lax.all_gather(w_out, "shard", axis=0, tiled=True),
        lax.all_gather(ln1_gain, "shard", axis=0, tiled=True),
        lax.all_gather(ln1_bias, "shard", axis=0, tiled=True),
    )


def fetch_feedforward(w_gate, w_up, w_down, ln2_gain, ln2_bias):
    return (
        lax.all_gather(w_gate, "shard", axis=0, tiled=True),
        lax.all_gather(w_up, "shard", axis=0, tiled=True),
        lax.all_gather(w_down, "shard", axis=0, tiled=True),
        lax.all_gather(ln2_gain, "shard", axis=0, tiled=True),
        lax.all_gather(ln2_bias, "shard", axis=0, tiled=True),
    )


def pair_columns(matrix, pair_index):
    width = 2 * HEAD_DIM
    return lax.dynamic_slice_in_dim(matrix, pair_index * width, width, 1).reshape(
        matrix.shape[0], 2, HEAD_DIM
    )


def pair_scores(pair_index, queries, key_rows, same_doc):
    scores = jnp.einsum(
        "qhd,khd->hqk",
        pair_columns(queries, pair_index),
        pair_columns(key_rows, pair_index),
        preferred_element_type=jnp.float32,
    ) * HEAD_DIM ** (-0.5)
    return jnp.where(same_doc[None], scores, -jnp.inf)


def attention_forward(queries, key_rows, value_rows, same_doc):

    def one_pair(pair_index):
        scores = pair_scores(pair_index, queries, key_rows, same_doc)
        row_max = jnp.max(scores, axis=-1, keepdims=True)
        expons = jnp.exp(scores - row_max)
        row_total = jnp.sum(expons, axis=-1, keepdims=True)
        weights_bf = (expons / row_total).astype(jnp.bfloat16)
        attended = jnp.einsum(
            "hqk,khd->qhd",
            weights_bf,
            pair_columns(value_rows, pair_index),
            preferred_element_type=jnp.float32,
        )
        return (
            attended.reshape(attended.shape[0], 2 * HEAD_DIM),
            (row_max + jnp.log(row_total))[..., 0],
        )

    attended, log_totals = lax.map(one_pair, jnp.arange(HEADS // 2, dtype=jnp.int32))
    return (jnp.transpose(attended, (1, 0, 2)).reshape(queries.shape[0], D), log_totals)


def attention_backward(queries, key_rows, value_rows, grad_attended, log_totals, same_doc):
    scale_factor = HEAD_DIM ** (-0.5)
    width = 2 * HEAD_DIM

    def one_pair(inputs):
        pair_index, pair_logs = inputs
        scores = pair_scores(pair_index, queries, key_rows, same_doc)
        weights = jnp.exp(scores - pair_logs[..., None])
        grad_pair = pair_columns(grad_attended, pair_index)
        grad_weights = jnp.einsum(
            "qhd,khd->hqk",
            grad_pair,
            pair_columns(value_rows, pair_index),
            preferred_element_type=jnp.float32,
        )
        row_delta = jnp.sum(weights * grad_weights, axis=-1, keepdims=True)
        grad_scores = (weights * (grad_weights - row_delta)).astype(jnp.bfloat16)
        grad_query = (
            jnp.einsum(
                "hqk,khd->qhd",
                grad_scores,
                pair_columns(key_rows, pair_index),
                preferred_element_type=jnp.float32,
            )
            * scale_factor
        )
        grad_key = (
            jnp.einsum(
                "hqk,qhd->khd",
                grad_scores,
                pair_columns(queries, pair_index),
                preferred_element_type=jnp.float32,
            )
            * scale_factor
        )
        grad_value = jnp.einsum(
            "hqk,qhd->khd",
            weights.astype(jnp.bfloat16),
            grad_pair,
            preferred_element_type=jnp.float32,
        )
        return (
            grad_query.reshape(-1, width),
            grad_key.reshape(-1, width),
            grad_value.reshape(-1, width),
        )

    pair_grads = lax.map(one_pair, (jnp.arange(HEADS // 2, dtype=jnp.int32), log_totals))
    return tuple(
        (
            jnp.transpose(pair_part, (1, 0, 2)).reshape(pair_part.shape[1], D)
            for pair_part in pair_grads
        )
    )


def per_device(
    tokens_in,
    segment_ids,
    w_qkv,
    w_out,
    ln1_gain,
    ln1_bias,
    w_gate,
    w_up,
    w_down,
    ln2_gain,
    ln2_bias,
    out_cotangent,
):
    inputs_bf = tokens_in.reshape(-1, D)
    token_count = inputs_bf.shape[0]
    doc_ids = segment_ids.reshape(-1)
    start = lax.axis_index("shard") * token_count
    own_docs = lax.dynamic_slice_in_dim(doc_ids, start, token_count)
    same_doc = own_docs[:, None] == doc_ids[None, :]
    cosine, sine = rope_tables(start, token_count)
    heads_shape = (token_count, HEADS, HEAD_DIM)
    qkv_full, out_full, gain_one, bias_one = fetch_attention(w_qkv, w_out, ln1_gain, ln1_bias)
    projected = jnp.dot(inputs_bf, qkv_full, preferred_element_type=jnp.float32)
    queries = (
        rotate(projected[:, :D].reshape(heads_shape), cosine, sine)
        .reshape(token_count, D)
        .astype(jnp.bfloat16)
    )
    own_keys = (
        rotate(projected[:, D : 2 * D].reshape(heads_shape), cosine, sine)
        .reshape(token_count, D)
        .astype(jnp.bfloat16)
    )
    own_values = projected[:, 2 * D :].astype(jnp.bfloat16)
    key_rows, value_rows = (
        lax.all_gather(own_keys, "shard", axis=0, tiled=True),
        lax.all_gather(own_values, "shard", axis=0, tiled=True),
    )
    attended, log_totals = attention_forward(queries, key_rows, value_rows, same_doc)
    attended_bf = attended.astype(jnp.bfloat16)
    branch = jnp.dot(attended_bf, out_full, preferred_element_type=jnp.float32)
    inputs_f = inputs_bf.astype(jnp.float32)
    first_out, first_normed, first_scale = norm_forward(
        inputs_f + branch, gain_one.astype(jnp.float32), bias_one.astype(jnp.float32)
    )
    gate_full, up_full, down_full, gain_two, bias_two = fetch_feedforward(
        w_gate, w_up, w_down, ln2_gain, ln2_bias
    )
    first_bf = first_out.astype(jnp.bfloat16)
    gate_act = jnp.dot(first_bf, gate_full, preferred_element_type=jnp.float32)
    up_act = jnp.dot(first_bf, up_full, preferred_element_type=jnp.float32)
    hidden_bf = (jax.nn.silu(gate_act) * up_act).astype(jnp.bfloat16)
    down_act = jnp.dot(hidden_bf, down_full, preferred_element_type=jnp.float32)
    result, second_normed, second_scale = norm_forward(
        first_out + down_act, gain_two.astype(jnp.float32), bias_two.astype(jnp.float32)
    )
    gate_full, up_full, down_full, gain_two, bias_two = fetch_feedforward(
        w_gate, w_up, w_down, ln2_gain, ln2_bias
    )
    upstream = out_cotangent.reshape(-1, D).astype(jnp.float32)
    grad_gain_two = jnp.sum(upstream * second_normed, axis=0)
    grad_bias_two = jnp.sum(upstream, axis=0)
    grad_second = norm_backward(upstream, second_normed, second_scale, gain_two.astype(jnp.float32))
    grad_down_bf = grad_second.astype(jnp.bfloat16)
    grad_down_w = jnp.einsum(
        "tf,td->fd", hidden_bf, grad_down_bf, preferred_element_type=jnp.float32
    )
    grad_hidden = jnp.einsum(
        "td,fd->tf", grad_down_bf, down_full, preferred_element_type=jnp.float32
    )
    sigmoid_gate = jax.nn.sigmoid(gate_act)
    grad_gate_bf = (
        grad_hidden * up_act * sigmoid_gate * (1.0 + gate_act * (1.0 - sigmoid_gate))
    ).astype(jnp.bfloat16)
    grad_up_bf = (grad_hidden * jax.nn.silu(gate_act)).astype(jnp.bfloat16)
    grad_gate_w = jnp.einsum(
        "td,tf->df", first_bf, grad_gate_bf, preferred_element_type=jnp.float32
    )
    grad_up_w = jnp.einsum("td,tf->df", first_bf, grad_up_bf, preferred_element_type=jnp.float32)
    grad_first = grad_second + jnp.einsum(
        "tf,df->td", grad_gate_bf, gate_full, preferred_element_type=jnp.float32
    )
    grad_first = grad_first + jnp.einsum(
        "tf,df->td", grad_up_bf, up_full, preferred_element_type=jnp.float32
    )
    qkv_full, out_full, gain_one, bias_one = fetch_attention(w_qkv, w_out, ln1_gain, ln1_bias)
    grad_gain_one = jnp.sum(grad_first * first_normed, axis=0)
    grad_bias_one = jnp.sum(grad_first, axis=0)
    grad_res = norm_backward(grad_first, first_normed, first_scale, gain_one.astype(jnp.float32))
    grad_branch_bf = grad_res.astype(jnp.bfloat16)
    grad_out_w = jnp.einsum(
        "tc,td->cd", attended_bf, grad_branch_bf, preferred_element_type=jnp.float32
    )
    grad_attended_bf = jnp.einsum(
        "td,cd->tc", grad_branch_bf, out_full, preferred_element_type=jnp.float32
    ).astype(jnp.bfloat16)
    grad_queries, grad_keys_all, grad_values_all = attention_backward(
        queries, key_rows, value_rows, grad_attended_bf, log_totals, same_doc
    )
    grad_keys, grad_values = (
        lax.psum_scatter(
            grad_keys_all.astype(jnp.bfloat16), "shard", scatter_dimension=0, tiled=True
        ).astype(jnp.float32),
        lax.psum_scatter(
            grad_values_all.astype(jnp.bfloat16), "shard", scatter_dimension=0, tiled=True
        ).astype(jnp.float32),
    )
    grad_projected = jnp.concatenate(
        [
            rotate_back(grad_queries.reshape(heads_shape), cosine, sine).reshape(token_count, D),
            rotate_back(grad_keys.reshape(heads_shape), cosine, sine).reshape(token_count, D),
            grad_values,
        ],
        axis=1,
    ).astype(jnp.bfloat16)
    grad_qkv_w = jnp.einsum(
        "td,tn->dn", inputs_bf, grad_projected, preferred_element_type=jnp.float32
    )
    grad_inputs = grad_res + jnp.einsum(
        "tn,dn->td", grad_projected, qkv_full, preferred_element_type=jnp.float32
    )
    (
        sum_qkv,
        sum_out,
        sum_gain_one,
        sum_bias_one,
        sum_gate,
        sum_up,
        sum_down,
        sum_gain_two,
        sum_bias_two,
    ) = (
        lax.psum_scatter(
            grad_qkv_w.astype(jnp.bfloat16), "shard", scatter_dimension=0, tiled=True
        ).astype(jnp.float32),
        lax.psum_scatter(
            grad_out_w.astype(jnp.bfloat16), "shard", scatter_dimension=0, tiled=True
        ).astype(jnp.float32),
        lax.psum_scatter(
            grad_gain_one.astype(jnp.bfloat16), "shard", scatter_dimension=0, tiled=True
        ).astype(jnp.float32),
        lax.psum_scatter(
            grad_bias_one.astype(jnp.bfloat16), "shard", scatter_dimension=0, tiled=True
        ).astype(jnp.float32),
        lax.psum_scatter(
            grad_gate_w.astype(jnp.bfloat16), "shard", scatter_dimension=0, tiled=True
        ).astype(jnp.float32),
        lax.psum_scatter(
            grad_up_w.astype(jnp.bfloat16), "shard", scatter_dimension=0, tiled=True
        ).astype(jnp.float32),
        lax.psum_scatter(
            grad_down_w.astype(jnp.bfloat16), "shard", scatter_dimension=0, tiled=True
        ).astype(jnp.float32),
        lax.psum_scatter(
            grad_gain_two.astype(jnp.bfloat16), "shard", scatter_dimension=0, tiled=True
        ).astype(jnp.float32),
        lax.psum_scatter(
            grad_bias_two.astype(jnp.bfloat16), "shard", scatter_dimension=0, tiled=True
        ).astype(jnp.float32),
    )
    totals = (
        lax.psum(sum_qkv.astype(jnp.bfloat16), "rep").astype(jnp.float32),
        lax.psum(sum_out.astype(jnp.bfloat16), "rep").astype(jnp.float32),
        lax.psum(sum_gain_one.astype(jnp.bfloat16), "rep").astype(jnp.float32),
        lax.psum(sum_bias_one.astype(jnp.bfloat16), "rep").astype(jnp.float32),
        lax.psum(sum_gate.astype(jnp.bfloat16), "rep").astype(jnp.float32),
        lax.psum(sum_up.astype(jnp.bfloat16), "rep").astype(jnp.float32),
        lax.psum(sum_down.astype(jnp.bfloat16), "rep").astype(jnp.float32),
        lax.psum(sum_gain_two.astype(jnp.bfloat16), "rep").astype(jnp.float32),
        lax.psum(sum_bias_two.astype(jnp.bfloat16), "rep").astype(jnp.float32),
    )
    return (
        result.astype(jnp.bfloat16).reshape(tokens_in.shape),
        grad_inputs.reshape(tokens_in.shape),
        totals[0],
        totals[1],
        totals[2],
        totals[3],
        totals[4],
        totals[5],
        totals[6],
        totals[7],
        totals[8],
    )


def solution(mesh):
    return jax.shard_map(
        per_device,
        mesh=mesh,
        in_specs=(
            P("rep", "shard", None),
            P("rep", None),
            P("shard", None),
            P("shard", None),
            P("shard"),
            P("shard"),
            P("shard", None),
            P("shard", None),
            P("shard", None),
            P("shard"),
            P("shard"),
            P("rep", "shard", None),
        ),
        out_specs=(
            P("rep", "shard", None),
            P("rep", "shard", None),
            P("shard", None),
            P("shard", None),
            P("shard"),
            P("shard"),
            P("shard", None),
            P("shard", None),
            P("shard", None),
            P("shard"),
            P("shard"),
        ),
        check_vma=False,
    )
```

profile of v0, /device:TPU:0, one launch (start us, length us, event | category | flops | bytes accessed | tf_op | source)
XLA Modules:
  0.0 1250.2 jit_solution(6899106883314646994)
XLA Ops:
  8.0 69.6 %all-gather.8.cloned.1.call-done = bf16[768,2304]{1,0:T(8,128)(2,1)} async-done(((bf16[96,2304]{1,0:T(8,128)(2,1)}), bf16[768,2304]{1,0:T(8,128)(2,1)}) %all-gather.8.cloned.1.call-update) | async-done | bytes 3538960 | tf_op jit(solution)/shard_map/all_gather | solution.py:62
  77.5 3.2 fusion.24
  90.3 20.1 %all-reduce.9 = (bf16[768]{0:T(1024)(128)(2,1)S(1)}, bf16[768]{0:T(1024)(128)(2,1)S(1)}, bf16[768]{0:T(1024)(128)(2,1)S(1)}) all-reduce(bf16[768]{0:T(1024)(128)(2,1)S(1)} %dynamic-update-slice.1, bf16[768]{0:T(1024)(128)(2,1)S(1)} %dynamic-update-slice, ...), channel_id=1, replica_groups=mesh['rep'=4,'shard'=8] {'shard'}, use_global_device_ids=true, to_apply=%add.1 | all-reduce | flops 2304 | bytes 9216
  112.3 28.6 %all-gather.10.cloned.1.call-done = bf16[2048,768]{1,0:T(8,128)(2,1)} async-done(((bf16[256,768]{1,0:T(8,128)(2,1)}), bf16[2048,768]{1,0:T(8,128)(2,1)}) %all-gather.10.cloned.1.call-update) | async-done | bytes 3145744 | tf_op jit(solution)/shard_map/all_gather | solution.py:212
  140.9 3.2 copy.42
  144.1 60.8 %all-gather.12.cloned.1.call-done = bf16[2048,768]{0,1:T(8,128)(2,1)} async-done(((bf16[256,768]{0,1:T(8,128)(2,1)}), bf16[2048,768]{0,1:T(8,128)(2,1)}) %all-gather.12.cloned.1.call-update) | async-done | bytes 3145744 | tf_op jit(solution)/shard_map/all_gather | solution.py:211
  205.4 50.5 %while.30 = (s32[]{:T(128)}, bf16[6,256,128]{1,2,0:T(8,128)(2,1)S(1)}, f32[6,2,256]{2,1,0:T(2,128)}, s32[6]{0:T(128)}, bf16[2048,768]{0,1:T(8,128)(2,1)S(1)}, /*...) while((s32[]{:T(128)}, ...), condition=%wide.region_3.4_spmd.clone.clone, body=%wide.region_0.3_spmd.clone.sunk.clone | while | flops 281542144 | bytes 18245292 | solution.py:115
  259.7 66.5 %all-gather.16.cloned.1.call-done = bf16[768,3072]{1,0:T(8,128)(2,1)} async-done(((bf16[96,3072]{1,0:T(8,128)(2,1)}), bf16[768,3072]{1,0:T(8,128)(2,1)}) %all-gather.16.cloned.1.call-update) | async-done | bytes 4718608 | tf_op jit(solution)/shard_map/all_gather | solution.py:71
  326.2 5.5 fusion.40
  331.7 74.3 %all-gather.18.cloned.1.call-done = bf16[768,3072]{1,0:T(8,128)(2,1)} async-done(((bf16[96,3072]{1,0:T(8,128)(2,1)}), bf16[768,3072]{1,0:T(8,128)(2,1)}) %all-gather.18.cloned.1.call-update) | async-done | bytes 4718608 | tf_op jit(solution)/shard_map/all_gather | solution.py:72
  406.0 7.2 multiply_convert_fusion.3
  413.1 72.7 %all-gather.20.cloned.1.call-done = bf16[3072,768]{1,0:T(8,128)(2,1)} async-done(((bf16[384,768]{1,0:T(8,128)(2,1)}), bf16[3072,768]{1,0:T(8,128)(2,1)}) %all-gather.20.cloned.1.call-update) | async-done | bytes 4718608 | tf_op jit(solution)/shard_map/all_gather | solution.py:73
  485.9 4.7 fusion.38
  491.8 5.7 multiply_convert_fusion.1
  504.0 70.1 %while.31 = (s32[]{:T(128)}, f32[6,256,128]{1,2,0:T(8,128)}, bf16[6,2048,128]{1,2,0:T(8,128)(2,1)}, bf16[6,2048,128]{1,2,0:T(8,128)(2,1)}, s32[6]{0:T(128)S(1)},...) while((s32[]{:T(128)}, f32[6,256,128]{1,2,0:T(8,128)}, ...), condition=%wide.region_14.15_spmd.clone.clone, body=%wide.region_12.14_spmd.clone.sunk.clone | while | flops 681606656 | bytes 40390856 | solution.py:166
  575.0 72.6 %reduce-scatter.10.cloned.1.call-done = bf16[256,768]{0,1:T(8,128)(2,1)} async-done(((bf16[2048,768]{0,1:T(8,128)(2,1)}), bf16[256,768]{0,1:T(8,128)(2,1)}) %reduce-scatter.10.cloned.1.call-update) | async-done | bytes 393232 | tf_op jit(solution)/shard_map/reduce_scatter | solution.py:276
  651.5 73.8 %reduce-scatter.12.cloned.1.call-done = bf16[256,768]{0,1:T(8,128)(2,1)} async-done(((bf16[2048,768]{0,1:T(8,128)(2,1)}), bf16[256,768]{0,1:T(8,128)(2,1)}) %reduce-scatter.12.cloned.1.call-update) | async-done | bytes 393232 | tf_op jit(solution)/shard_map/reduce_scatter | solution.py:279
  725.3 2.4 fusion.11
  727.8 4.0 copy.46
  732.9 2.5 convolution_convert_fusion.4
  735.8 4.5 convolution_convert_fusion
  741.3 5.0 convolution_convert_fusion.2
  746.4 5.1 convolution_convert_fusion.1
  751.6 59.0 %reduce-scatter.22.cloned.1.call-done = bf16[96,2304]{1,0:T(8,128)(2,1)} async-done(((bf16[768,2304]{1,0:T(8,128)(2,1)}), bf16[96,2304]{1,0:T(8,128)(2,1)}) %reduce-scatter.22.cloned.1.call-update) | async-done | bytes 442384
  812.6 66.3 %reduce-scatter.14.cloned.1.call-done = bf16[96,768]{1,0:T(8,128)(2,1)} async-done(((bf16[768,768]{1,0:T(8,128)(2,1)}), bf16[96,768]{1,0:T(8,128)(2,1)}) %reduce-scatter.14.cloned.1.call-update) | async-done | bytes 147472 | tf_op jit(solution)/shard_map/reduce_scatter | solution.py:311
  878.9 98.2 %reduce-scatter.20.cloned.1.call-done = bf16[384,768]{1,0:T(8,128)(2,1)} async-done(((bf16[3072,768]{1,0:T(8,128)(2,1)}), bf16[384,768]{1,0:T(8,128)(2,1)}) %reduce-scatter.20.cloned.1.call-update) | async-done | bytes 589840 | tf_op jit(solution)/shard_map/reduce_scatter | solution.py:326
  977.1 99.0 %reduce-scatter.16.cloned.1.call-done = bf16[96,3072]{1,0:T(8,128)(2,1)} async-done(((bf16[768,3072]{1,0:T(8,128)(2,1)}), bf16[96,3072]{1,0:T(8,128)(2,1)}) %reduce-scatter.16.cloned.1.call-update) | async-done | bytes 589840 | tf_op jit(solution)/shard_map/reduce_scatter | solution.py:320
  1076.1 98.8 %reduce-scatter.18.cloned.1.call-done = bf16[96,3072]{1,0:T(8,128)(2,1)} async-done(((bf16[768,3072]{1,0:T(8,128)(2,1)}), bf16[96,3072]{1,0:T(8,128)(2,1)}) %reduce-scatter.18.cloned.1.call-update) | async-done | bytes 589840 | tf_op jit(solution)/shard_map/reduce_scatter | solution.py:323
  1176.0 35.8 %all-reduce.8 = (bf16[768]{0:T(1024)(128)(2,1)S(1)}, bf16[768]{0:T(1024)(128)(2,1)S(1)}, bf16[768]{0:T(1024)(128)(2,1)S(1)}, bf16[768]{0:T(1024)(128)(2,1)S(1)}, bf16[768]{0:T(1024)(128)(2,1)S(1)}) all-reduce(bf16[768]{0:T(1024)(128)(2,1)S(1)} %dynamic-update-slice.3, ...), channel_id=1, replica_groups=mesh['rep'=4,'shard'=8] {'shard'}, use_global_device_ids=true, to_apply=%add.3 | all-reduce | flops 3840 | bytes 15360
  1212.1 6.3 all-reduce.10
  1221.3 4.1 fusion.13
  1225.4 10.8 all-reduce.14.cloned.1.call-done
  (358 shorter events, 155.5 us)
Async XLA Ops:
  7.2 70.3 %all-gather.8.cloned.1.call-start = ((), (), s32[]{:S(2)}) async-start(), calls=%async_computation.7 | async-start | bytes 3981312 | tf_op jit(solution)/shard_map/all_gather | solution.py:62
  7.9 133.0 %all-gather.10.cloned.1.call-start = ((), (), s32[]{:S(2)}) async-start(), calls=%async_computation.8 | async-start | bytes 3538944 | tf_op jit(solution)/shard_map/all_gather | solution.py:212
  81.6 123.3 %all-gather.12.cloned.1.call-start = ((), (), s32[]{:S(2)}) async-start(), calls=%async_computation.9 | async-start | bytes 3538944 | tf_op jit(solution)/shard_map/all_gather | solution.py:211
  84.6 27.0 %copy-start.15 = (s32[1,2048]{1,0:T(1,128)S(1)}, s32[1,2048]{1,0:T(1,128)}, u32[]{:S(2)}) copy-start(s32[1,2048]{1,0:T(1,128)} %param.17) | copy-start | bytes 24580
  85.7 170.3 %all-gather.14.cloned.1.call-start = ((), (), s32[]{:S(2)}) async-start(), calls=%async_computation.10 | async-start | bytes 1327104 | tf_op jit(solution)/shard_map/all_gather | solution.py:63
  86.2 240.0 %all-gather.16.cloned.1.call-start = ((), (), s32[]{:S(2)}) async-start(), calls=%async_computation.11 | async-start | bytes 5308416 | tf_op jit(solution)/shard_map/all_gather | solution.py:71
  86.8 319.2 %all-gather.18.cloned.1.call-start = ((), (), s32[]{:S(2)}) async-start(), calls=%async_computation.12 | async-start | bytes 5308416 | tf_op jit(solution)/shard_map/all_gather | solution.py:72
  87.4 398.5 %all-gather.20.cloned.1.call-start = ((), (), s32[]{:S(2)}) async-start(), calls=%async_computation.13 | async-start | bytes 5308416 | tf_op jit(solution)/shard_map/all_gather | solution.py:73
  88.1 559.4 %reduce-scatter.10.cloned.1.call-start = ((), (), s32[]{:S(2)}) async-start(), calls=%async_computation.14 | async-start | bytes 3538944 | tf_op jit(solution)/shard_map/reduce_scatter | solution.py:276
  259.7 146.3 %copy-start.6 = (bf16[256,768]{1,0:T(8,128)(2,1)}, bf16[256,768]{1,0:T(8,128)(2,1)S(1)}, u32[]{:S(2)}) copy-start(bf16[256,768]{1,0:T(8,128)(2,1)S(1)} %fusion.21) | copy-start | bytes 1179652
  490.6 7.0 copy-start
  490.6 7.0 copy-start.27
  490.9 6.7 copy-start.29
  490.9 6.7 slice-start
  490.9 8.3 slice-start.2
  491.8 7.4 slice-start.3
  574.1 74.5 %copy-start.21 = (f32[256,32]{0,1:T(8,128)S(1)}, f32[256,32]{0,1:T(8,128)}, u32[]{:S(2)}) copy-start(f32[256,32]{0,1:T(8,128)} %copy-done.20) | copy-start | bytes 98308
  574.1 74.5 %copy-start.23 = (f32[256,32]{0,1:T(8,128)S(1)}, f32[256,32]{0,1:T(8,128)}, u32[]{:S(2)}) copy-start(f32[256,32]{0,1:T(8,128)} %copy-done.22) | copy-start | bytes 98308
  574.2 151.2 %reduce-scatter.12.cloned.1.call-start = ((), (), s32[]{:S(2)}) async-start(), calls=%async_computation.15 | async-start | bytes 3538944 | tf_op jit(solution)/shard_map/reduce_scatter | solution.py:279
  574.9 235.7 %reduce-scatter.22.cloned.1.call-start = ((), (), s32[]{:S(2)}) async-start(), calls=%async_computation.20 | async-start | bytes 3981312
  731.9 147.1 %reduce-scatter.14.cloned.1.call-start = ((), (), s32[]{:S(2)}) async-start(), calls=%async_computation.16 | async-start | bytes 1327104 | tf_op jit(solution)/shard_map/reduce_scatter | solution.py:311
  735.4 241.7 %reduce-scatter.20.cloned.1.call-start = ((), (), s32[]{:S(2)}) async-start(), calls=%async_computation.19 | async-start | bytes 5308416 | tf_op jit(solution)/shard_map/reduce_scatter | solution.py:326
  740.3 335.8 %reduce-scatter.16.cloned.1.call-start = ((), (), s32[]{:S(2)}) async-start(), calls=%async_computation.17 | async-start | bytes 5308416 | tf_op jit(solution)/shard_map/reduce_scatter | solution.py:320
  746.3 428.6 %reduce-scatter.18.cloned.1.call-start = ((), (), s32[]{:S(2)}) async-start(), calls=%async_computation.18 | async-start | bytes 5308416 | tf_op jit(solution)/shard_map/reduce_scatter | solution.py:323
  751.5 423.6 %copy-start.48 = (bf16[96]{0:T(256)(128)(2,1)S(1)}, bf16[96]{0:T(256)(128)(2,1)}, u32[]{:S(2)}) copy-start(bf16[96]{0:T(256)(128)(2,1)} %param.26) | copy-start | bytes 580
  751.5 424.5 %copy-start.36 = (bf16[768]{0:T(1024)(128)(2,1)S(1)}, bf16[768]{0:T(1024)(128)(2,1)}, u32[]{:S(2)}) copy-start(bf16[768]{0:T(1024)(128)(2,1)} %get-tuple-element.266) | copy-start | bytes 4612
  751.5 424.5 %copy-start.40 = (bf16[768]{0:T(1024)(128)(2,1)S(1)}, bf16[768]{0:T(1024)(128)(2,1)}, u32[]{:S(2)}) copy-start(bf16[768]{0:T(1024)(128)(2,1)} %get-tuple-element.264) | copy-start | bytes 4612
  751.5 424.5 %copy-start.41 = (bf16[768]{0:T(1024)(128)(2,1)S(1)}, bf16[768]{0:T(1024)(128)(2,1)}, u32[]{:S(2)}) copy-start(bf16[768]{0:T(1024)(128)(2,1)} %get-tuple-element.269) | copy-start | bytes 4612
  751.5 469.8 %copy-start.18 = (bf16[256,12,64]{0,2,1:T(8,128)(2,1)S(1)}, bf16[256,12,64]{0,2,1:T(8,128)(2,1)}, u32[]{:S(2)}) copy-start(bf16[256,12,64]{0,2,1:T(8,128)(2,1)} %pad_maximum_fusion.5) | copy-start | bytes 1179652
  751.5 469.8 %copy-start.19 = (bf16[256,12,64]{0,2,1:T(8,128)(2,1)S(1)}, bf16[256,12,64]{0,2,1:T(8,128)(2,1)}, u32[]{:S(2)}) copy-start(bf16[256,12,64]{0,2,1:T(8,128)(2,1)} %pad_maximum_fusion.6) | copy-start | bytes 1179652
  751.5 469.8 %copy-start.44 = (bf16[256,768]{0,1:T(8,128)(2,1)S(1)}, bf16[256,768]{0,1:T(8,128)(2,1)}, u32[]{:S(2)}) copy-start(bf16[256,768]{0,1:T(8,128)(2,1)} %reduce-scatter.12.cloned.1.call-done) | copy-start | bytes 1179652
  751.5 484.6 %all-reduce.14.cloned.1.call-start = ((), (), s32[]{:S(2)}) async-start(), calls=%async_computation.21 | async-start | bytes 5013504 | tf_op jit(solution)/shard_map/psum | solution.py:337
  (37 other events, 128.0 us)
Sparse Core Ops, SparseCore 0:
  10.2 67.3 all-gather.7
  81.7 59.2 all-gather.9
  143.6 61.2 all-gather.11
  206.9 39.1 all-gather.13
  248.2 78.0 all-gather.15
  328.3 77.6 all-gather.17
  408.2 77.6 all-gather.19
  574.3 73.2 reduce-scatter.9
  651.2 74.1 reduce-scatter.11
  732.0 78.5 reduce-scatter.21
  814.5 64.3 reduce-scatter.13
  882.4 94.6 reduce-scatter.19
  980.8 95.2 reduce-scatter.15
  1079.6 95.2 reduce-scatter.17
  1178.1 58.0 all-reduce.13
where the time goes:
time: 1250 us
  waiting for transfers between devices  955 us (76%)
  matrix products  96.1 us (8%)
  local copies, waits for them, and re-layouts  75.7 us (6%)
  blocking collectives  62.2 us (5%)
  other arithmetic  36 us (3%)
  between operations  16.1 us (1%)
    reduce_scatter x1, waiting for transfers between devices, per_device(): lax.psum_scatter(grad_gate_w.astype(jnp.bfloat16), 'shard', scatter_dimen...  99 us
    reduce_scatter x1, waiting for transfers between devices, per_device(): lax.psum_scatter(grad_up_w.astype(jnp.bfloat16), 'shard', scatter_dimensi...  98.8 us
    reduce_scatter x1, waiting for transfers between devices, per_device(): lax.psum_scatter(grad_down_w.astype(jnp.bfloat16), 'shard', scatter_dimen...  98.2 us
    all_gather x1, waiting for transfers between devices, fetch_feedforward(): lax.all_gather(w_up, 'shard', axis=0, tiled=True)  74.3 us
    reduce_scatter x1, waiting for transfers between devices, per_device(): lax.psum_scatter(grad_values_all.astype(jnp.bfloat16), 'shard', scatter_d...  73.8 us
    all_gather x1, waiting for transfers between devices, fetch_feedforward(): lax.all_gather(w_down, 'shard', axis=0, tiled=True)  72.7 us
    reduce_scatter x1, waiting for transfers between devices, per_device(): lax.psum_scatter(grad_keys_all.astype(jnp.bfloat16), 'shard', scatter_dim...  72.6 us
    all_gather x1, waiting for transfers between devices, fetch_attention(): lax.all_gather(w_qkv, 'shard', axis=0, tiled=True)  69.6 us
  transfers between devices with their start and end apart: 15, of which 14 were waited for; matrix products, arithmetic and copies ran while one was open for 8% of the time, Pallas kernels for 0%

commit v1 on v0

--- a/solution.py
+++ b/solution.py
@@ -1,6 +1,8 @@
 import jax
 import jax.numpy as jnp
 from jax import lax
+from jax.experimental import pallas as pl
+from jax.experimental.pallas import tpu as pltpu
 from jax.sharding import PartitionSpec as P
 
 D = 768
@@ -359,9 +361,636 @@
     )
 
 
+BF = jnp.bfloat16
+F32 = jnp.float32
+AXES = ("rep", "shard")
+TILE = 256
+GROUP = 4
+OWN_HEADS = 3
+NARROW = OWN_HEADS * HEAD_DIM
+WIDE = 256
+LOG2E = 1.4426950408889634
+SCORE_FACTOR = HEAD_DIM ** (-0.5) * LOG2E
+MASKED = -1e30
+
+
+def moves(target):
+    pairs = []
+    for rep in range(4):
+        for shard in range(8):
+            goal = target(rep // 2, rep % 2, shard // 4, shard % 4)
+            if goal is not None:
+                x, c, h, j = goal
+                pairs.append((rep * 8 + shard, (2 * x + c) * 8 + 4 * h + j))
+    return pairs
+
+
+SPREAD = moves(lambda x, c, h, j: (x, h, c, j))
+OTHER_CORE = moves(lambda x, c, h, j: (x, 1 - c, h, j))
+OTHER_X = moves(lambda x, c, h, j: (1 - x, c, h, j))
+OTHER_HALF = moves(lambda x, c, h, j: (x, c, 1 - h, j))
+SQUARE = [moves(lambda x, c, h, j, k=k: (x, c, h, j ^ k)) for k in range(GROUP)]
+ROUND = [moves(lambda x, c, h, j, k=k: (x, c, h ^ c, j ^ k)) for k in range(GROUP)]
+OUT_FETCH = moves(lambda x, c, h, j: (x, j % 2, c, (4 * h + j) // 2))
+OUT_RETURN = moves(lambda x, c, h, j: (x, h, (2 * j + c) // 4, (2 * j + c) % 4))
+HOME_HALF = moves(lambda x, c, h, j: (x, c, 1 - h, j) if c != h else None)
+HOME_SQUARE = [
+    moves(lambda x, c, h, j, k=k: (x, c, h, j ^ k) if c == h else None) for k in range(GROUP)
+]
+HOME_X = moves(lambda x, c, h, j: (1 - x, c, h, j) if c == h else None)
+HOME_CORE = moves(lambda x, c, h, j: (x, 1 - c, h, j) if c == h else None)
+
+
+def send(value, pairs):
+    return lax.ppermute(value, AXES, pairs)
+
+
+def pick(flag, first, second):
+    return jnp.where(flag, second, first)
+
+
+def unmix(blocks, j):
+    bit0 = (j % 2) == 1
+    bit1 = (j // 2) == 1
+    b = blocks
+    b = [pick(bit0, b[0], b[1]), pick(bit0, b[1], b[0]), pick(bit0, b[2], b[3]), pick(bit0, b[3], b[2])]
+    return [pick(bit1, b[0], b[2]), pick(bit1, b[1], b[3]), pick(bit1, b[2], b[0]), pick(bit1, b[3], b[1])]
+
+
+def turned(values):
+    lane = lax.broadcasted_iota(jnp.int32, values.shape, 1) % HEAD_DIM
+    middle = HEAD_DIM // 2
+    return jnp.where(
+        lane < middle,
+        -pltpu.roll(values, WIDE - middle, 1),
+        pltpu.roll(values, middle, 1),
+    )
+
+
+def doubled(table):
+    return jnp.concatenate([table, table], axis=1)
+
+
+def project_kernel(x_ref, w_ref, cos_ref, sin_ref, q_ref, kv_ref):
+    projected = jnp.dot(x_ref[...], w_ref[...], preferred_element_type=F32)
+    cosine = doubled(cos_ref[...])
+    sine = doubled(sin_ref[...])
+    for index, ref in ((0, q_ref), (1, kv_ref)):
+        part = projected[:, index * WIDE : (index + 1) * WIDE]
+        ref[:, :WIDE] = (part * cosine + turned(part) * sine).astype(BF)
+    kv_ref[:, WIDE:] = projected[:, 2 * WIDE :].astype(BF)
+
+
+def project(x_rows, w_qkv, cosine, sine):
+    rows = x_rows.shape[0]
+    return pl.pallas_call(
+        project_kernel,
+        grid=(rows // TILE,),
+        in_specs=[
+            pl.BlockSpec((TILE, D), lambda i: (i, 0)),
+            pl.BlockSpec((D, 3 * WIDE), lambda i: (0, 0)),
+            pl.BlockSpec((TILE, 128), lambda i: (i, 0)),
+            pl.BlockSpec((TILE, 128), lambda i: (i, 0)),
+        ],
+        out_specs=[
+            pl.BlockSpec((TILE, WIDE), lambda i: (i, 0)),
+            pl.BlockSpec((TILE, 2 * WIDE), lambda i: (i, 0)),
+        ],
+        out_shape=[
+            jax.ShapeDtypeStruct((rows, WIDE), BF),
+            jax.ShapeDtypeStruct((rows, 2 * WIDE), BF),
+        ],
+        name="project",
+    )(x_rows, w_qkv, cosine, sine)
+
+
+def head_only(values, head):
+    lane = lax.broadcasted_iota(jnp.int32, values.shape, 1) // HEAD_DIM
+    return jnp.where(lane == head, values, jnp.zeros_like(values))
+
+
+def share_document(ids_ref, q_tile, kv_tile):
+    q_first = ids_ref[q_tile * TILE]
+    q_last = ids_ref[q_tile * TILE + TILE - 1]
+    k_first = ids_ref[kv_tile * TILE]
+    k_last = ids_ref[kv_tile * TILE + TILE - 1]
+    return jnp.logical_and(k_first <= q_last, q_first <= k_last)
+
+
+def contract(left, right, left_dim, right_dim):
+    return lax.dot_general(
+        left, right, (((left_dim,), (right_dim,)), ((), ())), preferred_element_type=F32
+    )
+
+
+def attend_kernel(
+    ids_ref, row_ids_ref, col_ids_ref, q_ref, own_ref, other_ref, out_ref, log_ref,
+    v_turned, max_ref, total_ref, acc_ref,
+):
+    q_tile = pl.program_id(0)
+    own_tiles = own_ref.shape[0] // TILE
+
+    @pl.when(q_tile == 0)
+    def _():
+        for base, ref in ((0, own_ref), (own_tiles, other_ref)):
+            for tile in range(own_tiles):
+                v_turned[base + tile] = jnp.transpose(
+                    ref[pl.ds(tile * TILE, TILE), WIDE:]
+                )[:NARROW]
+
+    queries = q_ref[...]
+    per_head = [head_only(queries, head) for head in range(OWN_HEADS)]
+    q_ids = row_ids_ref[0]
+    max_ref[...] = jnp.full(max_ref.shape, MASKED, F32)
+    total_ref[...] = jnp.zeros(total_ref.shape, F32)
+    acc_ref[...] = jnp.zeros(acc_ref.shape, F32)
+
+    for base, ref in ((0, own_ref), (own_tiles, other_ref)):
+
+        def one_tile(tile, carry, base=base, ref=ref):
+            @pl.when(share_document(ids_ref, q_tile, base + tile))
+            def _():
+                start = pl.multiple_of(tile * TILE, TILE)
+                keys = ref[pl.ds(start, TILE), :WIDE]
+                same = (
+                    col_ids_ref[pl.ds(pl.multiple_of((base + tile) * TILE, TILE), TILE), :] == q_ids
+                )
+                for head in range(OWN_HEADS):
+                    scores = contract(keys, per_head[head], 1, 1) * SCORE_FACTOR
+                    scores = jnp.where(same, scores, MASKED)
+                    old_max = max_ref[head : head + 1, :]
+                    new_max = jnp.maximum(old_max, jnp.max(scores, axis=0, keepdims=True))
+                    shrink = jnp.exp2(old_max - new_max)
+                    expons = jnp.exp2(scores - new_max)
+                    max_ref[head : head + 1, :] = new_max
+                    total_ref[head : head + 1, :] = total_ref[
+                        head : head + 1, :
+                    ] * shrink + jnp.sum(expons, axis=0, keepdims=True)
+                    rows = slice(head * HEAD_DIM, (head + 1) * HEAD_DIM)
+                    acc_ref[rows, :] = acc_ref[rows, :] * shrink + jnp.dot(
+                        v_turned[base + tile, rows, :],
+                        expons.astype(BF),
+                        preferred_element_type=F32,
+                    )
+
+            return carry
+
+        lax.fori_loop(0, own_tiles, one_tile, 0)
+
+    parts = []
+    for head in range(OWN_HEADS):
+        rows = slice(head * HEAD_DIM, (head + 1) * HEAD_DIM)
+        parts.append(acc_ref[rows, :] / total_ref[head : head + 1, :])
+    parts.append(jnp.zeros((WIDE - NARROW, TILE), F32))
+    out_ref[...] = jnp.transpose(jnp.concatenate(parts, axis=0)).astype(BF)
+    row = lax.broadcasted_iota(jnp.int32, log_ref.shape, 0)
+    log_ref[...] = jnp.where(
+        row < OWN_HEADS,
+        max_ref[...] + jnp.log2(jnp.where(row < OWN_HEADS, total_ref[...], 1.0)),
+        0.0,
+    )
+
+
+def attend(ids, row_ids, col_ids, queries, kv_own, kv_other):
+    rows = queries.shape[0]
+    whole = lambda array: pl.BlockSpec(array.shape, lambda i, ids: (0,) * array.ndim)
+    return pl.pallas_call(
+        attend_kernel,
+        grid_spec=pltpu.PrefetchScalarGridSpec(
+            num_scalar_prefetch=1,
+            grid=(rows // TILE,),
+            in_specs=[
+                pl.BlockSpec((1, 1, TILE), lambda i, ids: (i, 0, 0)),
+                whole(col_ids),
+                pl.BlockSpec((TILE, WIDE), lambda i, ids: (i, 0)),
+                whole(kv_own),
+                whole(kv_other),
+            ],
+            out_specs=[
+                pl.BlockSpec((TILE, WIDE), lambda i, ids: (i, 0)),
+                pl.BlockSpec((8, TILE), lambda i, ids: (0, i)),
+            ],
+            scratch_shapes=[
+                pltpu.VMEM((2 * rows // TILE, NARROW, TILE), BF),
+                pltpu.VMEM((8, TILE), F32),
+                pltpu.VMEM((8, TILE), F32),
+                pltpu.VMEM((NARROW, TILE), F32),
+            ],
+        ),
+        out_shape=[
+            jax.ShapeDtypeStruct((rows, WIDE), BF),
+            jax.ShapeDtypeStruct((8, rows), F32),
+        ],
+        name="attend",
+    )(ids, row_ids, col_ids, queries, kv_own, kv_other)
+
+
+def attend_back_kernel(
+    ids_ref, row_ids_ref, col_ids_ref, q_ref, up_ref, out_ref, log_ref, own_ref, other_ref,
+    cos_ref, sin_ref, dq_ref, own_grad_ref, other_grad_ref,
+    k_turned, acc_ref, key_acc, value_acc,
+):
+    q_tile = pl.program_id(0)
+    own_tiles = own_ref.shape[0] // TILE
+
+    @pl.when(q_tile == 0)
+    def _():
+        for base, ref in ((0, own_ref), (own_tiles, other_ref)):
+            for tile in range(own_tiles):
+                k_turned[base + tile] = jnp.transpose(
+                    ref[pl.ds(tile * TILE, TILE), :WIDE]
+                )[:NARROW]
+        key_acc[...] = jnp.zeros(key_acc.shape, F32)
+        value_acc[...] = jnp.zeros(value_acc.shape, F32)
+
+    queries = q_ref[...]
+    upstream = up_ref[...]
+    q_heads = [head_only(queries, head) for head in range(OWN_HEADS)]
+    up_heads = [head_only(upstream, head) for head in range(OWN_HEADS)]
+    products = upstream.astype(F32) * out_ref[...].astype(F32)
+    lane_head = lax.broadcasted_iota(jnp.int32, (8, WIDE), 1) // HEAD_DIM
+    selector = (lane_head == lax.broadcasted_iota(jnp.int32, (8, WIDE), 0)).astype(F32)
+    deltas = lax.dot_general(
+        selector, products, (((1,), (1,)), ((), ())),
+        precision=lax.Precision.HIGHEST, preferred_element_type=F32,
+    )
+    q_ids = row_ids_ref[0]
+    acc_ref[...] = jnp.zeros(acc_ref.shape, F32)
+
+    for base, ref in ((0, own_ref), (own_tiles, other_ref)):
+
+        def one_tile(tile, carry, base=base, ref=ref):
+            @pl.when(share_document(ids_ref, q_tile, base + tile))
+            def _():
+                start = pl.multiple_of(tile * TILE, TILE)
+                place = pl.ds(pl.multiple_of((base + tile) * TILE, TILE), TILE)
+                keys = ref[pl.ds(start, TILE), :WIDE]
+                values = ref[pl.ds(start, TILE), WIDE:]
+                same = col_ids_ref[place, :] == q_ids
+                for head in range(OWN_HEADS):
+                    scores = contract(keys, q_heads[head], 1, 1) * SCORE_FACTOR
+                    weights = jnp.where(
+                        same, jnp.exp2(scores - log_ref[head : head + 1, :]), 0.0
+                    )
+                    grad_weights = contract(values, up_heads[head], 1, 1)
+                    grad_scores = (
+                        weights * (grad_weights - deltas[head : head + 1, :])
+                    ).astype(BF)
+                    value_acc[place, :] += jnp.dot(
+                        weights.astype(BF), up_heads[head], preferred_element_type=F32
+                    )
+                    key_acc[place, :] += jnp.dot(
+                        grad_scores, q_heads[head], preferred_element_type=F32
+                    )
+                    rows = slice(head * HEAD_DIM, (head + 1) * HEAD_DIM)
+                    acc_ref[rows, :] += jnp.dot(
+                        k_turned[base + tile, rows, :], grad_scores, preferred_element_type=F32
+                    )
+
+            return carry
+
+        lax.fori_loop(0, own_tiles, one_tile, 0)
+
+    factor = HEAD_DIM ** (-0.5)
+    grad_query = jnp.transpose(
+        jnp.concatenate([acc_ref[...], jnp.zeros((WIDE - NARROW, TILE), F32)], axis=0)
+    )
+    grad_query = grad_query * factor
+    dq_ref[...] = (
+        grad_query * doubled(cos_ref[...]) - turned(grad_query) * doubled(sin_ref[...])
+    ).astype(BF)
+
+    @pl.when(q_tile == pl.num_programs(0) - 1)
+    def _():
+        rows = own_grad_ref.shape[0]
+        own_grad_ref[:, :WIDE] = key_acc[:rows, :] * factor
+        own_grad_ref[:, WIDE:] = value_acc[:rows, :]
+        other_grad_ref[:, :WIDE] = (key_acc[rows:, :] * factor).astype(BF)
+        other_grad_ref[:, WIDE:] = value_acc[rows:, :].astype(BF)
+
+
+def attend_back(
+    ids, row_ids, col_ids, queries, upstream, attended, logs, kv_own, kv_other, cosine, sine
+):
+    rows = queries.shape[0]
+    whole = lambda array: pl.BlockSpec(array.shape, lambda i, ids: (0,) * array.ndim)
+    tiled = lambda width: pl.BlockSpec((TILE, width), lambda i, ids: (i, 0))
+    return pl.pallas_call(
+        attend_back_kernel,
+        grid_spec=pltpu.PrefetchScalarGridSpec(
+            num_scalar_prefetch=1,
+            grid=(rows // TILE,),
+            in_specs=[
+                pl.BlockSpec((1, 1, TILE), lambda i, ids: (i, 0, 0)),
+                whole(col_ids),
+                tiled(WIDE),
+                tiled(WIDE),
+                tiled(WIDE),
+                pl.BlockSpec((8, TILE), lambda i, ids: (0, i)),
+                whole(kv_own),
+                whole(kv_other),
+                tiled(128),
+                tiled(128),
+            ],
+            out_specs=[
+                tiled(WIDE),
+                pl.BlockSpec((rows, 2 * WIDE), lambda i, ids: (0, 0)),
+                pl.BlockSpec((rows, 2 * WIDE), lambda i, ids: (0, 0)),
+            ],
+            scratch_shapes=[
+                pltpu.VMEM((2 * rows // TILE, NARROW, TILE), BF),
+                pltpu.VMEM((NARROW, TILE), F32),
+                pltpu.VMEM((2 * rows, WIDE), F32),
+                pltpu.VMEM((2 * rows, WIDE), F32),
+            ],
+        ),
+        out_shape=[
+            jax.ShapeDtypeStruct((rows, WIDE), BF),
+            jax.ShapeDtypeStruct((rows, 2 * WIDE), F32),
+            jax.ShapeDtypeStruct((rows, 2 * WIDE), BF),
+        ],
+        name="attend_back",
+    )(ids, row_ids, col_ids, queries, upstream, attended, logs, kv_own, kv_other, cosine, sine)
+
+
+def join_grads_kernel(dq_ref, own_ref, got_ref, cos_ref, sin_ref, out_ref):
+    out_ref[:, :WIDE] = dq_ref[...]
+    total = own_ref[...] + got_ref[...].astype(F32)
+    keys = total[:, :WIDE]
+    out_ref[:, WIDE : 2 * WIDE] = (
+        keys * doubled(cos_ref[...]) - turned(keys) * doubled(sin_ref[...])
+    ).astype(BF)
+    out_ref[:, 2 * WIDE :] = total[:, WIDE:].astype(BF)
+
+
+def join_grads(grad_queries, own, got, cosine, sine):
+    rows = grad_queries.shape[0]
+    tiled = lambda width: pl.BlockSpec((TILE, width), lambda i: (i, 0))
+    return pl.pallas_call(
+        join_grads_kernel,
+        grid=(rows // TILE,),
+        in_specs=[tiled(WIDE), tiled(2 * WIDE), tiled(2 * WIDE), tiled(128), tiled(128)],
+        out_specs=tiled(3 * WIDE),
+        out_shape=jax.ShapeDtypeStruct((rows, 3 * WIDE), BF),
+        name="join_grads",
+    )(grad_queries, own, got, cosine, sine)
+
+
+def gather_square(block):
+    return [block] + [send(block, SQUARE[k]) for k in range(1, GROUP)]
+
+
+def reduce_square(left, weight, weight_dim):
+    got = []
+    for k in (3, 1, 2):
+        part = contract(left[k * TILE : (k + 1) * TILE], weight, 1, weight_dim)
+        got.append(send(part.astype(BF), SQUARE[k]))
+    total = contract(left[:TILE], weight, 1, weight_dim)
+    for part in got:
+        total = total + part.astype(F32)
+    return total
+
+
+def per_device_clustered(
+    tokens_in,
+    segment_ids,
+    w_qkv,
+    w_out,
+    ln1_gain,
+    ln1_bias,
+    w_gate,
+    w_up,
+    w_down,
+    ln2_gain,
+    ln2_bias,
+    out_cotangent,
+):
+    rep = lax.axis_index("rep")
+    shard = lax.axis_index("shard")
+    x, c = rep // 2, rep % 2
+    h, j = shard // 4, shard % 4
+    core_is_one = c == 1
+    half_is_one = h == 1
+    x_is_one = x == 1
+    at_home = c == h
+    token_count = tokens_in.shape[1]
+    length = segment_ids.shape[1]
+    rows_d = w_qkv.shape[0]
+    rows_f = w_down.shape[0]
+    slice_f = 2 * rows_f
+    group_rows = GROUP * token_count
+
+    inputs_bf = send(tokens_in.reshape(token_count, D), SPREAD)
+    doc_ids = send(segment_ids, SPREAD).reshape(2, GROUP, token_count)
+
+    def by_target(rows_of_targets):
+        return [lax.dynamic_index_in_dim(rows_of_targets, j ^ k, 0, False) for k in range(GROUP)]
+
+    def fetch_columns(targets):
+        mine = [send(part, ROUND[k]) for k, part in enumerate(by_target(targets))]
+        mine = jnp.stack(mine)
+        other = send(mine, OTHER_CORE)
+        away = c != h
+        low = pick(away, mine, other)
+        high = pick(away, other, mine)
+        return jnp.concatenate([jnp.stack(unmix(low, j)), jnp.stack(unmix(high, j))], axis=0)
+
+    vectors = jnp.stack([ln1_gain, ln1_bias, ln2_gain, ln2_bias], axis=1)
+    qkv_targets = jnp.transpose(w_qkv.reshape(rows_d, 3, GROUP, NARROW), (2, 0, 1, 3)).reshape(
+        GROUP, rows_d, 3 * NARROW
+    )
+    qkv_targets = jnp.concatenate(
+        [qkv_targets, jnp.broadcast_to(vectors[None], (GROUP, rows_d, 4))], axis=2
+    )
+    qkv_got = fetch_columns(qkv_targets)
+    vectors_full = jnp.transpose(qkv_got[:, :, 3 * NARROW :].reshape(D, 4)).astype(F32)
+    gain_one, bias_one, gain_two, bias_two = (vectors_full[i] for i in range(4))
+    qkv_own = jnp.pad(
+        qkv_got[:, :, : 3 * NARROW].reshape(D, 3, NARROW), ((0, 0), (0, 0), (0, WIDE - NARROW))
+    ).reshape(D, 3 * WIDE)
+
+    out_got = send(w_out, OUT_FETCH)
+    out_other = send(out_got, OTHER_CORE)
+    out_own = jnp.concatenate(
+        [
+            pick(core_is_one, out_got, out_other),
+            pick(core_is_one, out_other, out_got),
+            jnp.zeros((WIDE - NARROW, D), BF),
+        ],
+        axis=0,
+    )
+
+    half_f = rows_f // 2
+    down_mine = send(lax.dynamic_slice_in_dim(w_down, c * half_f, half_f, 0), OTHER_HALF)
+    down_other = send(down_mine, OTHER_CORE)
+    down_far = jnp.concatenate(
+        [pick(core_is_one, down_mine, down_other), pick(core_is_one, down_other, down_mine)], axis=0
+    )
+    down_own = jnp.concatenate(
+        [pick(half_is_one, w_down, down_far), pick(half_is_one, down_far, w_down)], axis=0
+    )
+
+    def column_targets(weight):
+        return jnp.transpose(weight.reshape(rows_d, 2, GROUP, rows_f), (2, 0, 1, 3)).reshape(
+            GROUP, rows_d, slice_f
+        )
+
+    gate_up_got = fetch_columns(
+        jnp.concatenate([column_targets(w_gate), column_targets(w_up)], axis=2)
+    )
+    gate_up_own = gate_up_got.reshape(D, 2 * slice_f)
+
+    tile_index = j ^ jnp.arange(GROUP, dtype=jnp.int32)
+    first_row = (c * GROUP + tile_index) * token_count
+    positions = (
+        first_row[:, None] + jnp.arange(token_count, dtype=jnp.int32)[None, :]
+    ).reshape(group_rows).astype(F32)
+    middle = HEAD_DIM // 2
+    exponents = jnp.arange(128, dtype=jnp.int32) % middle
+    inverse = rope_base ** (-(2.0 * exponents.astype(F32)) / HEAD_DIM)
+    angles = positions[:, None] * inverse[None, :]
+    cosine, sine = jnp.cos(angles), jnp.sin(angles)
+    mixed = jnp.stack(unmix([doc_ids[:, k] for k in range(GROUP)], j), axis=1)
+    ids = jnp.concatenate(
+        [pick(core_is_one, mixed[0], mixed[1]), pick(core_is_one, mixed[1], mixed[0])], axis=0
+    )
+    flat_ids = ids.reshape(length)
+    row_ids = ids.reshape(length // TILE, 1, TILE)
+    col_ids = flat_ids[:, None]
+
+    x_rows = jnp.concatenate(gather_square(inputs_bf), axis=0)
+    queries, kv_own = project(x_rows, qkv_own, cosine, sine)
+    kv_other = send(kv_own, OTHER_CORE)
+    attended, logs = attend(flat_ids, row_ids, col_ids, queries, kv_own, kv_other)
+    branch = reduce_square(attended, out_own, 0)
+    first_out, first_normed, first_scale = norm_forward(
+        inputs_bf.astype(F32) + branch, gain_one, bias_one
+    )
+
+    first_rows = jnp.concatenate(gather_square(first_out.astype(BF)), axis=0)
+    acts = contract(first_rows, gate_up_own, 1, 0)
+    gate_act, up_act = acts[:, :slice_f], acts[:, slice_f:]
+    hidden_bf = (jax.nn.silu(gate_act) * up_act).astype(BF)
+    down_act = reduce_square(hidden_bf, down_own, 0)
+    result, second_normed, second_scale = norm_forward(first_out + down_act, gain_two, bias_two)
+    result_home = send(result.astype(BF), SPREAD)
+
+    upstream = send(out_cotangent.reshape(token_count, D), SPREAD).astype(F32)
+    grad_gain_two = jnp.sum(upstream * second_normed, axis=0)
+    grad_bias_two = jnp.sum(upstream, axis=0)
+    grad_second = norm_backward(upstream, second_normed, second_scale, gain_two)
+    grad_down_rows = jnp.concatenate(gather_square(grad_second.astype(BF)), axis=0)
+    grad_hidden = contract(grad_down_rows, down_own, 1, 1)
+    sigmoid_gate = jax.nn.sigmoid(gate_act)
+    grad_gate_bf = (
+        grad_hidden * up_act * sigmoid_gate * (1.0 + gate_act * (1.0 - sigmoid_gate))
+    ).astype(BF)
+    grad_up_bf = (grad_hidden * (gate_act * sigmoid_gate)).astype(BF)
+    grad_acts = jnp.concatenate([grad_gate_bf, grad_up_bf], axis=1)
+    grad_first = grad_second + reduce_square(grad_acts, gate_up_own, 1)
+    grad_gain_one = jnp.sum(grad_first * first_normed, axis=0)
+    grad_bias_one = jnp.sum(grad_first, axis=0)
+    grad_res = norm_backward(grad_first, first_normed, first_scale, gain_one)
+
+    grad_branch_rows = jnp.concatenate(gather_square(grad_res.astype(BF)), axis=0)
+    grad_attended = contract(grad_branch_rows, out_own, 1, 1).astype(BF)
+    grad_queries, kv_grad_own, kv_grad_away = attend_back(
+        flat_ids, row_ids, col_ids, queries, grad_attended, attended, logs, kv_own, kv_other,
+        cosine, sine,
+    )
+    kv_grad_got = send(kv_grad_away, OTHER_CORE)
+    grad_projected = join_grads(grad_queries, kv_grad_own, kv_grad_got, cosine, sine)
+    grad_inputs = grad_res + reduce_square(grad_projected, qkv_own, 1)
+    grad_inputs_home = send(grad_inputs.astype(BF), SPREAD).astype(F32)
+
+    quarter = rows_d // 2
+
+    def rows_for_home(partial):
+        partial = partial.astype(BF)
+        keep = pick(core_is_one, partial[0], partial[1]).astype(F32)
+        away = pick(core_is_one, partial[1], partial[0])
+        total = keep + send(away, OTHER_CORE).astype(F32)
+        total = total.astype(BF).reshape(-1, 2, quarter, total.shape[-1])
+        keep = pick(x_is_one, total[:, 0], total[:, 1]).astype(F32)
+        away = pick(x_is_one, total[:, 1], total[:, 0])
+        total = keep + send(away, OTHER_X).astype(F32)
+        total_bf = total.astype(BF)
+        return (total + send(total_bf, HOME_HALF).astype(F32)).astype(BF)
+
+    def both_x(mine, axis):
+        got = send(mine, HOME_X)
+        return jnp.stack(
+            [pick(x_is_one, mine, got), pick(x_is_one, got, mine)], axis=axis
+        )
+
+    def both_cores(mine):
+        return pick(at_home, send(mine, HOME_CORE), mine).astype(F32)
+
+    def to_row_owner(mine):
+        parts = by_target(mine)
+        return unmix([parts[0]] + [send(parts[k], HOME_SQUARE[k]) for k in range(1, GROUP)], j)
+
+    grad_down_part = contract(hidden_bf, grad_down_rows, 0, 0).reshape(2, rows_f, D)
+    down_mine = rows_for_home(grad_down_part)
+    grad_w_down = both_cores(both_x(down_mine, 1)).reshape(rows_f, D)
+
+    grad_gate_up_part = contract(first_rows, grad_acts, 0, 0).reshape(2, D // 2, 2 * slice_f)
+    gate_up_mine = rows_for_home(grad_gate_up_part)
+    gate_up_mine = jnp.stack(to_row_owner(gate_up_mine), axis=1)
+    gate_up_all = both_cores(both_x(gate_up_mine, 0)).reshape(rows_d, GROUP, 2, 2, rows_f)
+    gate_up_all = jnp.transpose(gate_up_all, (2, 0, 3, 1, 4)).reshape(2, rows_d, w_gate.shape[1])
+    grad_w_gate, grad_w_up = gate_up_all[0], gate_up_all[1]
+
+    grad_out_part = contract(attended, grad_branch_rows, 0, 0)[:NARROW].astype(BF)
+    grad_out_part = grad_out_part.reshape(2, 2, quarter, D)
+    keep = pick(core_is_one, grad_out_part[0], grad_out_part[1]).astype(F32)
+    away = pick(core_is_one, grad_out_part[1], grad_out_part[0])
+    out_total = (keep + send(away, OTHER_CORE).astype(F32)).astype(BF)
+    keep = pick(x_is_one, out_total[0], out_total[1]).astype(F32)
+    away = pick(x_is_one, out_total[1], out_total[0])
+    out_total = (keep + send(away, OTHER_X).astype(F32)).astype(BF)
+    out_total = (out_total.astype(F32) + send(out_total, OTHER_HALF).astype(F32)).astype(BF)
+    out_mine = send(out_total, OUT_RETURN)
+    out_got = send(out_mine, OTHER_X)
+    grad_w_out = jnp.concatenate(
+        [pick(x_is_one, out_mine, out_got), pick(x_is_one, out_got, out_mine)], axis=0
+    ).astype(F32)
+
+    grad_qkv_part = contract(x_rows, grad_projected, 0, 0).reshape(D, 3, WIDE)[:, :, :NARROW]
+    vector_part = jnp.stack([grad_gain_one, grad_bias_one, grad_gain_two, grad_bias_two], axis=1)
+    grad_qkv_part = jnp.concatenate([grad_qkv_part.reshape(D, 3 * NARROW), vector_part], axis=1)
+    qkv_mine = rows_for_home(grad_qkv_part.reshape(2, D // 2, 3 * NARROW + 4))
+    qkv_parts = to_row_owner(qkv_mine)
+    vector_sum = sum(part[:, 3 * NARROW :].astype(F32) for part in qkv_parts)
+    columns = jnp.stack([part[:, : 3 * NARROW] for part in qkv_parts], axis=1)
+    columns = columns.reshape(quarter, GROUP, 3, NARROW)
+    columns = jnp.transpose(columns, (0, 2, 1, 3)).reshape(quarter, 3 * D)
+    qkv_all = jnp.concatenate([columns, vector_sum.astype(BF)], axis=1)
+    qkv_all = both_cores(both_x(qkv_all, 0)).reshape(rows_d, 3 * D + 4)
+    grad_w_qkv = qkv_all[:, : 3 * D]
+    vector_grads = jnp.transpose(qkv_all[:, 3 * D :])
+
+    return (
+        result_home.reshape(tokens_in.shape),
+        grad_inputs_home.reshape(tokens_in.shape),
+        grad_w_qkv,
+        grad_w_out,
+        vector_grads[0],
+        vector_grads[1],
+        grad_w_gate,
+        grad_w_up,
+        grad_w_down,
+        vector_grads[2],
+        vector_grads[3],
+    )
+
+
 def solution(mesh):
+    sizes = dict(mesh.shape)
+    clustered = (sizes["rep"], sizes["shard"]) == (4, 8)
+    plan = per_device_clustered if clustered else per_device
     return jax.shard_map(
-        per_device,
+        plan,
         mesh=mesh,
         in_specs=(
             P("rep", "shard", None),

time: 1250 us -> 477 us (0.38)
  waiting for transfers between devices: 955 us -> 151 us
  starting transfers between devices: 0.86 us -> 144 us
  blocking collectives: 62.2 us -> 0 us
  matrix products: 96.1 us -> 37.5 us
  Pallas kernels: 0 us -> 48.3 us
  local copies, waits for them, and re-layouts: 75.7 us -> 50.1 us
  between operations: 16.1 us -> 2.89 us
    reduce_scatter x6 -> x0, waiting for transfers between devices: 509 us -> none  [the longest x1 99 us: per_device(): lax.psum_scatter(grad_gate_w.astype(jnp.bfloat16), 'shard', scatter_dimen...]
    all_gather x7 -> x0, waiting for transfers between devices: 373 us -> none  [the longest x1 74.3 us: fetch_feedforward(): lax.all_gather(w_up, 'shard', axis=0, tiled=True)]
    ppermute x0 -> x71, waiting for transfers between devices: none -> 151 us  [send(): return lax.ppermute(value, AXES, pairs)]
    ppermute x0 -> x71, starting transfers between devices: none -> 144 us  [send(): return lax.ppermute(value, AXES, pairs)]
    unnamed x16 -> x0, waiting for transfers between devices: 62.8 us -> none
    dot_general x57 -> x23, matrix products: 96.1 us -> 37.5 us  [contract(): lax.dot_general(left, right, (((left_dim,), (right_dim,)), ((), ())), pre...]
    unnamed x2 -> x0, blocking collectives: 55.9 us -> none
    pallas_call x0 -> x4, Pallas kernels: none -> 48.3 us  [the longest x1 24.3 us: attend_back(): pl.pallas_call(attend_back_kernel, grid_spec=pltpu.PrefetchScalarGridSpec...]
  transfers between devices with their start and end apart: 15 -> 71, of which waited for: 14 -> 32; matrix products, arithmetic and copies ran while one was open for 8% -> 17% of each run, Pallas kernels for 0% -> 7%
where the time goes in v1:
time: 477 us; the launch traced here: 468 us
  waiting for transfers between devices  151 us (32%)
  starting transfers between devices  144 us (30%)
  local copies, waits for them, and re-layouts  50.1 us (11%)
  Pallas kernels  48.3 us (10%)
  matrix products  37.5 us (8%)
  other arithmetic  34.2 us (7%)
    ppermute x71, waiting for transfers between devices, send(): return lax.ppermute(value, AXES, pairs)  151 us
    ppermute x71, starting transfers between devices, send(): return lax.ppermute(value, AXES, pairs)  144 us
    dot_general x23, matrix products, contract(): lax.dot_general(left, right, (((left_dim,), (right_dim,)), ((), ())), pre...  37.5 us
    pallas_call x1, Pallas kernels, attend_back(): pl.pallas_call(attend_back_kernel, grid_spec=pltpu.PrefetchScalarGridSpec...  24.3 us
    unnamed x160, local copies, waits for them, and re-layouts  14.7 us
    pallas_call x1, Pallas kernels, attend(): pl.pallas_call(attend_kernel, grid_spec=pltpu.PrefetchScalarGridSpec(num_...  14 us
    select_n x18, other arithmetic, pick(): return jnp.where(flag, second, first)  11.1 us
  transfers between devices with their start and end apart: 71, of which 32 were waited for; matrix products, arithmetic and copies ran while one was open for 17% of the time, Pallas kernels for 7%

profile of v1, /device:TPU:0, one launch (start us, length us, event | category | flops | bytes accessed | tf_op | source)
XLA Modules:
  0.0 468.1 jit_solution(1712381264015563739)
XLA Ops:
  24.5 7.9 %collective-permute-start.20 = (bf16[96,1536]{1,0:T(8,128)(2,1)S(1)}, bf16[96,1536]{1,0:T(8,128)(2,1)S(1)}, u32[]{:S(2)}, u32[]{:S(2)}) collective-permute-start(bf16[96,1536]{1,0:T(8,128)(2,1)S(1)} %get-tuple-element.56), channel_id=1, source_target_pairs={{0,1},{1,0},{2,3},{3,2},{4,5},{5,4},{6,7},{7,6},{8,13},{9,12},{10,... | collective-permute-start | bytes 884744 | tf_op jit(solution)/shard_map/ppermute | solution.py:405
  39.5 4.5 collective-permute-start
  44.0 25.3 %collective-permute-start.9 = (bf16[4,96,580]{2,1,0:T(8,128)(2,1)S(1)}, bf16[4,96,580]{2,1,0:T(8,128)(2,1)S(1)}, u32[]{:S(2)}, u32[]{:S(2)}) collective-permute-start(bf16[4,96,580]{2,1,0:T(8,128)(2,1)S(1)} %pad_maximum_fusion.11), channel_id=1, source_target_pairs={{0,8},{1,9},{2,10},{3,11},{4,12},{5,13},{6,14},{7,15},{8,0},{9,1},... | collective-permute-start | bytes 1336328 | tf_op jit(solution)/shard_map/ppermute | solution.py:405
  71.0 12.6 %collective-permute-start.25 = (bf16[192,768]{1,0:T(8,128)(2,1)}, bf16[192,768]{1,0:T(8,128)(2,1)S(1)}, u32[]{:S(2)}, u32[]{:S(2)}) collective-permute-start(bf16[192,768]{1,0:T(8,128)(2,1)} %collective-permute-done.24), channel_id=1, source_target_pairs={{0,8},{1,9},{2,10},{3,11},{4,12},{5,13},{6,14},{7,15},{8,0},{9,1},... | collective-permute-start | bytes 884744 | tf_op jit(solution)/shard_map/ppermute | solution.py:405
  100.4 5.0 %collective-permute-done.4 = bf16[256,768]{1,0:T(8,128)(2,1)} collective-permute-done((bf16[256,768]{1,0:T(8,128)(2,1)}, bf16[256,768]{1,0:T(8,128)(2,1)}, u32[]{:S(2)}, u32[]{:S(2)}) %collective-permute-start.4) | collective-permute-done | bytes 393248 | tf_op jit(solution)/shard_map/ppermute | solution.py:405
  107.6 5.5 %project.1 = (bf16[1024,256]{1,0:T(8,128)(2,1)}, bf16[1024,512]{1,0:T(8,128)(2,1)}) custom-call(bf16[1024,768]{1,0:T(8,128)(2,1)} %copy-done.9, bf16[768,768]{1,0:T(8,128)(2,1)} %copy.131.w_ref, f32[1024,128]{1,0:T(8,128)} %get-tuple-element.103.cos_ref, f32[1024,128]{1,0:T(8,128)} %get-tuple-element.102.sin_ref), custom_call_target="tpu_custom_call" | custom-call | tf_op jit(solution)/shard_map/project/pallas_call | solution.py:446
  116.1 14.0 %attend.1 = (bf16[1024,256]{1,0:T(8,128)(2,1)}, f32[8,1024]{1,0:T(8,128)}) custom-call(s32[2048]{0:T(1024)} %bitcast.308, s32[8,1,256]{2,1,0:T(1,128)} %reshape.295.row_ids_ref, s32[2048,1]{1,0:T(8,128)} %bitcast.271, bf16[1024,256]{1,0:T(8,128)(2,1)} %get-tuple-element.18.q_ref, bf16[1024,512]{1,0:T(8,128)(2,1)} %get-tuple-element.19.own_ref, ...), custom_call_target="tpu_custom_call" | custom-call | tf_op jit(solution)/shard_map/attend/pallas_call | solution.py:557
  137.1 9.1 %collective-permute-done.13 = bf16[256,768]{1,0:T(8,128)(2,1)S(1)} collective-permute-done((bf16[256,768]{1,0:T(8,128)(2,1)S(1)}, bf16[256,768]{1,0:T(8,128)(2,1)S(1)}, u32[]{:S(2)}, u32[]{:S(2)}) %collective-permute-start.13) | collective-permute-done | bytes 393248 | tf_op jit(solution)/shard_map/ppermute | solution.py:405
  146.2 7.5 %collective-permute-done.14 = bf16[256,768]{1,0:T(8,128)(2,1)S(1)} collective-permute-done((bf16[256,768]{1,0:T(8,128)(2,1)S(1)}, bf16[256,768]{1,0:T(8,128)(2,1)S(1)}, u32[]{:S(2)}, u32[]{:S(2)}) %collective-permute-start.14) | collective-permute-done | bytes 393248 | tf_op jit(solution)/shard_map/ppermute | solution.py:405
  159.4 7.5 %collective-permute-done.16 = bf16[256,768]{1,0:T(8,128)(2,1)S(1)} collective-permute-done((bf16[256,768]{1,0:T(8,128)(2,1)S(1)}, bf16[256,768]{1,0:T(8,128)(2,1)S(1)}, u32[]{:S(2)}, u32[]{:S(2)}) %collective-permute-start.16) | collective-permute-done | bytes 393248 | tf_op jit(solution)/shard_map/ppermute | solution.py:405
  169.2 7.3 %collective-permute-done.18 = bf16[256,768]{1,0:T(8,128)(2,1)S(1)} collective-permute-done((bf16[256,768]{1,0:T(8,128)(2,1)S(1)}, bf16[256,768]{1,0:T(8,128)(2,1)S(1)}, u32[]{:S(2)}, u32[]{:S(2)}) %collective-permute-start.18) | collective-permute-done | bytes 393248 | tf_op jit(solution)/shard_map/ppermute | solution.py:405
  188.3 12.8 %collective-permute-done.26 = bf16[256,768]{1,0:T(8,128)(2,1)S(1)} collective-permute-done((bf16[256,768]{1,0:T(8,128)(2,1)S(1)}, bf16[256,768]{1,0:T(8,128)(2,1)S(1)}, u32[]{:S(2)}, u32[]{:S(2)}) %collective-permute-start.26) | collective-permute-done | bytes 393248 | tf_op jit(solution)/shard_map/ppermute | solution.py:405
  203.3 4.2 collective-permute-done.28
  217.3 4.7 collective-permute-done.31
  223.4 6.2 %collective-permute-done.33 = bf16[256,768]{1,0:T(8,128)(2,1)} collective-permute-done((bf16[256,768]{1,0:T(8,128)(2,1)}, bf16[256,768]{1,0:T(8,128)(2,1)}, u32[]{:S(2)}, u32[]{:S(2)}) %collective-permute-start.33) | collective-permute-done | bytes 393248 | tf_op jit(solution)/shard_map/ppermute | solution.py:405
  229.6 5.7 %multiply_convert_fusion = (bf16[1024,768]{1,0:T(8,128)(2,1)S(1)}, bf16[1024,768]{1,0:T(8,128)(2,1)S(1)}) fusion(f32[1024,1536]{1,0:T(8,128)} %copy-done.4, bf16[384,768]{1,0:T(8,128)(2,1)} %get-tuple-element.52, bf16[384,768]{1,0:T(8,128)(2,1)} %get-tuple-element.51, bf16[256,768]{1,0:T(8,128)(2,1)} %collective-permute-done.33, ...), kind=kOutput, calls=%fused_computation.10 | convolution fusion | flops 1226833920 | bytes 12189696 | tf_op jit(solution)/shard_map/dot_general | solution.py:481
  244.4 6.4 %collective-permute-done.34 = bf16[256,768]{1,0:T(8,128)(2,1)S(1)} collective-permute-done((bf16[256,768]{1,0:T(8,128)(2,1)S(1)}, bf16[256,768]{1,0:T(8,128)(2,1)S(1)}, u32[]{:S(2)}, u32[]{:S(2)}) %collective-permute-start.34) | collective-permute-done | bytes 393248 | tf_op jit(solution)/shard_map/ppermute | solution.py:405
  250.8 3.9 collective-permute-done.35
  265.0 4.7 collective-permute-done.37
  271.8 6.9 %collective-permute-done.39 = bf16[256,768]{1,0:T(8,128)(2,1)S(1)} collective-permute-done((bf16[256,768]{1,0:T(8,128)(2,1)S(1)}, bf16[256,768]{1,0:T(8,128)(2,1)S(1)}, u32[]{:S(2)}, u32[]{:S(2)}) %collective-permute-start.39) | collective-permute-done | bytes 393248 | tf_op jit(solution)/shard_map/ppermute | solution.py:405
  283.9 4.6 collective-permute-start.29
  294.0 12.3 %collective-permute-done.55 = bf16[48,768]{1,0:T(8,128)(2,1)S(1)} collective-permute-done((bf16[48,768]{1,0:T(8,128)(2,1)S(1)}, bf16[48,768]{1,0:T(8,128)(2,1)S(1)}, u32[]{:S(2)}, u32[]{:S(2)}) %collective-permute-start.55) | collective-permute-done | bytes 73760 | tf_op jit(solution)/shard_map/ppermute | solution.py:405
  310.1 24.3 %attend_back.1 = (bf16[1024,256]{1,0:T(8,128)(2,1)}, f32[1024,512]{1,0:T(8,128)}, bf16[1024,512]{1,0:T(8,128)(2,1)}) custom-call(s32[2048]{0:T(1024)} %bitcast.309, s32[8,1,256]{2,1,0:T(1,128)} %reshape.295.row_ids_ref, s32[2048,1]{1,0:T(8,128)} %bitcast.272, bf16[1024,256]{1,0:T(8,128)(2,1)} %get-tuple-element.18.q_ref, ...), custom_call_target="tpu_custom_call" | custom-call | tf_op jit(solution)/shard_map/attend_back/pallas_call | solution.py:678
  339.0 3.9 collective-permute-start.69
  346.4 4.3 collective-permute-done.69
  353.9 6.2 %collective-permute-done.59 = bf16[4,48,1536]{2,1,0:T(8,128)(2,1)S(1)} collective-permute-done((bf16[4,48,1536]{2,1,0:T(8,128)(2,1)S(1)}, bf16[4,48,1536]{2,1,0:T(8,128)(2,1)S(1)}, u32[]{:S(2)}, u32[]{:S(2)}) %collective-permute-start.59) | collective-permute-done | bytes 589856 | tf_op jit(solution)/shard_map/ppermute | solution.py:405
  363.4 4.5 join_grads.1
  385.9 4.6 collective-permute-done.41
  390.5 7.3 %collective-permute-done.42 = bf16[256,768]{1,0:T(8,128)(2,1)S(1)} collective-permute-done((bf16[256,768]{1,0:T(8,128)(2,1)S(1)}, bf16[256,768]{1,0:T(8,128)(2,1)S(1)}, u32[]{:S(2)}, u32[]{:S(2)}) %collective-permute-start.42) | collective-permute-done | bytes 393248 | tf_op jit(solution)/shard_map/ppermute | solution.py:405
  418.3 6.7 %collective-permute-done.47 = bf16[4,48,580]{2,1,0:T(8,128)(2,1)S(1)} collective-permute-done((bf16[4,48,580]{2,1,0:T(8,128)(2,1)S(1)}, bf16[4,48,580]{2,1,0:T(8,128)(2,1)S(1)}, u32[]{:S(2)}, u32[]{:S(2)}) %collective-permute-start.47) | collective-permute-done | bytes 222752 | tf_op jit(solution)/shard_map/ppermute | solution.py:405
  427.4 5.1 %collective-permute-start.49 = (bf16[48,580]{0,1:T(8,128)(2,1)S(1)}, bf16[48,580]{0,1:T(8,128)(2,1)}, u32[]{:S(2)}, u32[]{:S(2)}) collective-permute-start(bf16[48,580]{0,1:T(8,128)(2,1)S(1)} %bitcast.305), channel_id=1, source_target_pairs={{0,2},{1,3},{2,0},{3,1},{12,14},{13,15},{14,12},{15,13},{16,18},{1... | collective-permute-start | bytes 167048 | tf_op jit(solution)/shard_map/ppermute | solution.py:405
  446.2 4.5 collective-permute-done.51
  (450 shorter events, 215.2 us)
Async XLA Ops:
  4.2 18.7 %collective-permute-start.5 = (bf16[96,580]{1,0:T(8,128)(2,1)}, bf16[96,580]{1,0:T(8,128)(2,1)S(1)}, u32[]{:S(2)}, u32[]{:S(2)}) collective-permute-start(bf16[96,580]{1,0:T(8,128)(2,1)} %bitcast.9), channel_id=1, source_target_pairs={{0,0},{1,1},{2,2},{3,3},{4,4},{5,5},{6,6},{7,7},{8,12},{9,13},{10,... | collective-permute-start | bytes 334088 | tf_op jit(solution)/shard_map/ppermute | solution.py:405
  6.5 18.0 %collective-permute-start.6 = (bf16[96,580]{1,0:T(8,128)(2,1)}, bf16[96,580]{1,0:T(8,128)(2,1)S(1)}, u32[]{:S(2)}, u32[]{:S(2)}) collective-permute-start(bf16[96,580]{1,0:T(8,128)(2,1)} %bitcast.11), channel_id=1, source_target_pairs={{0,1},{1,0},{2,3},{3,2},{4,5},{5,4},{6,7},{7,6},{8,13},{9,12},{10,... | collective-permute-start | bytes 334088 | tf_op jit(solution)/shard_map/ppermute | solution.py:405
  10.3 22.1 %collective-permute-start.7 = (bf16[96,580]{1,0:T(8,128)(2,1)}, bf16[96,580]{1,0:T(8,128)(2,1)S(1)}, u32[]{:S(2)}, u32[]{:S(2)}) collective-permute-start(bf16[96,580]{1,0:T(8,128)(2,1)} %bitcast.13), channel_id=1, source_target_pairs={{0,2},{1,3},{2,0},{3,1},{4,6},{5,7},{6,4},{7,5},{8,14},{9,15},{10,... | collective-permute-start | bytes 334088 | tf_op jit(solution)/shard_map/ppermute | solution.py:405
  12.7 21.2 %collective-permute-start.8 = (bf16[96,580]{1,0:T(8,128)(2,1)}, bf16[96,580]{1,0:T(8,128)(2,1)S(1)}, u32[]{:S(2)}, u32[]{:S(2)}) collective-permute-start(bf16[96,580]{1,0:T(8,128)(2,1)} %bitcast.15), channel_id=1, source_target_pairs={{0,3},{1,2},{2,1},{3,0},{4,7},{5,6},{6,5},{7,4},{8,15},{9,14},{10,... | collective-permute-start | bytes 334088 | tf_op jit(solution)/shard_map/ppermute | solution.py:405
  24.5 19.4 %collective-permute-start.20 = (bf16[96,1536]{1,0:T(8,128)(2,1)S(1)}, bf16[96,1536]{1,0:T(8,128)(2,1)S(1)}, u32[]{:S(2)}, u32[]{:S(2)}) collective-permute-start(bf16[96,1536]{1,0:T(8,128)(2,1)S(1)} %get-tuple-element.56), channel_id=1, source_target_pairs={{0,1},{1,0},{2,3},{3,2},{4,5},{5,4},{6,7},{7,6},{8,13},{9,12},{10,... | collective-permute-start | bytes 884744 | tf_op jit(solution)/shard_map/ppermute | solution.py:405
  32.4 36.9 %collective-permute-start.21 = (bf16[96,1536]{1,0:T(8,128)(2,1)}, bf16[96,1536]{1,0:T(8,128)(2,1)S(1)}, u32[]{:S(2)}, u32[]{:S(2)}) collective-permute-start(bf16[96,1536]{1,0:T(8,128)(2,1)} %get-tuple-element.55), channel_id=1, source_target_pairs={{0,2},{1,3},{2,0},{3,1},{4,6},{5,7},{6,4},{7,5},{8,14},{9,15},{10,... | collective-permute-start | bytes 884744 | tf_op jit(solution)/shard_map/ppermute | solution.py:405
  33.9 35.5 %collective-permute-start.22 = (bf16[96,1536]{1,0:T(8,128)(2,1)}, bf16[96,1536]{1,0:T(8,128)(2,1)S(1)}, u32[]{:S(2)}, u32[]{:S(2)}) collective-permute-start(bf16[96,1536]{1,0:T(8,128)(2,1)} %get-tuple-element.54), channel_id=1, source_target_pairs={{0,3},{1,2},{2,1},{3,0},{4,7},{5,6},{6,5},{7,4},{8,15},{9,14},{10,... | collective-permute-start | bytes 884744 | tf_op jit(solution)/shard_map/ppermute | solution.py:405
  36.5 34.5 %collective-permute-start.24 = (bf16[192,768]{1,0:T(8,128)(2,1)S(1)}, bf16[192,768]{1,0:T(8,128)(2,1)}, u32[]{:S(2)}, u32[]{:S(2)}) collective-permute-start(bf16[192,768]{1,0:T(8,128)(2,1)S(1)} %constant_dynamic-slice_fusion.4), channel_id=1, source_target_pairs={{0,4},{1,5},{2,6},{3,7},{4,0},{5,1},{6,2},{7,3},{8,12},{9,13},{10,... | collective-permute-start | bytes 884744 | tf_op jit(solution)/shard_map/ppermute | solution.py:405
  39.5 44.9 %collective-permute-start = (bf16[256,768]{1,0:T(8,128)(2,1)}, bf16[256,768]{1,0:T(8,128)(2,1)}, u32[]{:S(2)}, u32[]{:S(2)}) collective-permute-start(bf16[256,768]{1,0:T(8,128)(2,1)} %bitcast.317), channel_id=1, source_target_pairs={{0,0},{1,1},{2,2},{3,3},{4,8},{5,9},{6,10},{7,11},{8,4},{9,5},{10,... | collective-permute-start | bytes 1179656 | tf_op jit(solution)/shard_map/ppermute | solution.py:405
  44.0 42.3 %collective-permute-start.9 = (bf16[4,96,580]{2,1,0:T(8,128)(2,1)S(1)}, bf16[4,96,580]{2,1,0:T(8,128)(2,1)S(1)}, u32[]{:S(2)}, u32[]{:S(2)}) collective-permute-start(bf16[4,96,580]{2,1,0:T(8,128)(2,1)S(1)} %pad_maximum_fusion.11), channel_id=1, source_target_pairs={{0,8},{1,9},{2,10},{3,11},{4,12},{5,13},{6,14},{7,15},{8,0},{9,1},... | collective-permute-start | bytes 1336328 | tf_op jit(solution)/shard_map/ppermute | solution.py:405
  70.6 42.5 %collective-permute-start.23 = (bf16[4,96,1536]{2,1,0:T(8,128)(2,1)}, bf16[4,96,1536]{2,1,0:T(8,128)(2,1)}, u32[]{:S(2)}, u32[]{:S(2)}) collective-permute-start(bf16[4,96,1536]{2,1,0:T(8,128)(2,1)} %pad_maximum_fusion.5), channel_id=1, source_target_pairs={{0,8},{1,9},{2,10},{3,11},{4,12},{5,13},{6,14},{7,15},{8,0},{9,1},... | collective-permute-start | bytes 3538952 | tf_op jit(solution)/shard_map/ppermute | solution.py:405
  71.0 24.9 %collective-permute-start.25 = (bf16[192,768]{1,0:T(8,128)(2,1)}, bf16[192,768]{1,0:T(8,128)(2,1)S(1)}, u32[]{:S(2)}, u32[]{:S(2)}) collective-permute-start(bf16[192,768]{1,0:T(8,128)(2,1)} %collective-permute-done.24), channel_id=1, source_target_pairs={{0,8},{1,9},{2,10},{3,11},{4,12},{5,13},{6,14},{7,15},{8,0},{9,1},... | collective-permute-start | bytes 884744 | tf_op jit(solution)/shard_map/ppermute | solution.py:405
  86.3 19.1 %collective-permute-start.4 = (bf16[256,768]{1,0:T(8,128)(2,1)}, bf16[256,768]{1,0:T(8,128)(2,1)}, u32[]{:S(2)}, u32[]{:S(2)}) collective-permute-start(bf16[256,768]{1,0:T(8,128)(2,1)} %collective-permute-done), channel_id=1, source_target_pairs={{0,3},{1,2},{2,1},{3,0},{4,7},{5,6},{6,5},{7,4},{8,11},{9,10},{10,... | collective-permute-start | bytes 1179656 | tf_op jit(solution)/shard_map/ppermute | solution.py:405
  133.5 20.2 %collective-permute-start.14 = (bf16[256,768]{1,0:T(8,128)(2,1)S(1)}, bf16[256,768]{1,0:T(8,128)(2,1)S(1)}, u32[]{:S(2)}, u32[]{:S(2)}) collective-permute-start(bf16[256,768]{1,0:T(8,128)(2,1)S(1)} %convolution_convert_fusion.15), channel_id=1, source_target_pairs={{0,1},{1,0},{2,3},{3,2},{4,5},{5,4},{6,7},{7,6},{8,9},{9,8},{10,11... | collective-permute-start | bytes 1179656 | tf_op jit(solution)/shard_map/ppermute | solution.py:405
  135.2 18.5 %collective-permute-start.15 = (bf16[256,768]{1,0:T(8,128)(2,1)S(1)}, bf16[256,768]{1,0:T(8,128)(2,1)S(1)}, u32[]{:S(2)}, u32[]{:S(2)}) collective-permute-start(bf16[256,768]{1,0:T(8,128)(2,1)S(1)} %convolution_convert_fusion.14), channel_id=1, source_target_pairs={{0,2},{1,3},{2,0},{3,1},{4,6},{5,7},{6,4},{7,5},{8,10},{9,11},{10,... | collective-permute-start | bytes 1179656 | tf_op jit(solution)/shard_map/ppermute | solution.py:405
  157.5 19.0 %collective-permute-start.18 = (bf16[256,768]{1,0:T(8,128)(2,1)S(1)}, bf16[256,768]{1,0:T(8,128)(2,1)S(1)}, u32[]{:S(2)}, u32[]{:S(2)}) collective-permute-start(bf16[256,768]{1,0:T(8,128)(2,1)S(1)} %fusion.26), channel_id=1, source_target_pairs={{0,3},{1,2},{2,1},{3,0},{4,7},{5,6},{6,5},{7,4},{8,11},{9,10},{10,... | collective-permute-start | bytes 1179656 | tf_op jit(solution)/shard_map/ppermute | solution.py:405
  185.2 18.2 %collective-permute-start.27 = (bf16[256,768]{1,0:T(8,128)(2,1)S(1)}, bf16[256,768]{1,0:T(8,128)(2,1)S(1)}, u32[]{:S(2)}, u32[]{:S(2)}) collective-permute-start(bf16[256,768]{1,0:T(8,128)(2,1)S(1)} %convolution_convert_fusion.12), channel_id=1, source_target_pairs={{0,1},{1,0},{2,3},{3,2},{4,5},{5,4},{6,7},{7,6},{8,9},{9,8},{10,11... | collective-permute-start | bytes 1179656 | tf_op jit(solution)/shard_map/ppermute | solution.py:405
  186.8 20.7 %collective-permute-start.28 = (bf16[256,768]{1,0:T(8,128)(2,1)S(1)}, bf16[256,768]{1,0:T(8,128)(2,1)S(1)}, u32[]{:S(2)}, u32[]{:S(2)}) collective-permute-start(bf16[256,768]{1,0:T(8,128)(2,1)S(1)} %convolution_convert_fusion.11), channel_id=1, source_target_pairs={{0,2},{1,3},{2,0},{3,1},{4,6},{5,7},{6,4},{7,5},{8,10},{9,11},{10,... | collective-permute-start | bytes 1179656 | tf_op jit(solution)/shard_map/ppermute | solution.py:405
  187.5 21.1 %collective-permute-start.30 = (bf16[256,768]{1,0:T(8,128)(2,1)S(1)}, bf16[256,768]{1,0:T(8,128)(2,1)S(1)}, u32[]{:S(2)}, u32[]{:S(2)}) collective-permute-start(bf16[256,768]{1,0:T(8,128)(2,1)S(1)} %bitcast.318), channel_id=1, source_target_pairs={{0,0},{1,1},{2,2},{3,3},{4,8},{5,9},{6,10},{7,11},{8,4},{9,5},{10,... | collective-permute-start | bytes 1179656 | tf_op jit(solution)/shard_map/ppermute | solution.py:405
  211.1 18.5 %collective-permute-start.33 = (bf16[256,768]{1,0:T(8,128)(2,1)}, bf16[256,768]{1,0:T(8,128)(2,1)}, u32[]{:S(2)}, u32[]{:S(2)}) collective-permute-start(bf16[256,768]{1,0:T(8,128)(2,1)} %fusion.77), channel_id=1, source_target_pairs={{0,3},{1,2},{2,1},{3,0},{4,7},{5,6},{6,5},{7,4},{8,11},{9,10},{10,... | collective-permute-start | bytes 1179656 | tf_op jit(solution)/shard_map/ppermute | solution.py:405
  244.3 20.4 %collective-permute-start.66 = (bf16[384,768]{1,0:T(8,128)(2,1)S(1)}, bf16[384,768]{1,0:T(8,128)(2,1)S(1)}, u32[]{:S(2)}, u32[]{:S(2)}) collective-permute-start(bf16[384,768]{1,0:T(8,128)(2,1)S(1)} %broadcast_select_fusion.5), channel_id=1, source_target_pairs={{0,8},{1,9},{2,10},{3,11},{4,12},{5,13},{6,14},{7,15},{8,0},{9,1},... | collective-permute-start | bytes 1769480 | tf_op jit(solution)/shard_map/ppermute | solution.py:405
  260.3 18.4 %collective-permute-start.39 = (bf16[256,768]{1,0:T(8,128)(2,1)S(1)}, bf16[256,768]{1,0:T(8,128)(2,1)S(1)}, u32[]{:S(2)}, u32[]{:S(2)}) collective-permute-start(bf16[256,768]{1,0:T(8,128)(2,1)S(1)} %get-tuple-element.40), channel_id=1, source_target_pairs={{0,3},{1,2},{2,1},{3,0},{4,7},{5,6},{6,5},{7,4},{8,11},{9,10},{10,... | collective-permute-start | bytes 1179656 | tf_op jit(solution)/shard_map/ppermute | solution.py:405
  283.8 59.1 %collective-permute-start.58 = (bf16[384,1536]{1,0:T(8,128)(2,1)}, bf16[384,1536]{1,0:T(8,128)(2,1)}, u32[]{:S(2)}, u32[]{:S(2)}) collective-permute-start(bf16[384,1536]{1,0:T(8,128)(2,1)} %broadcast_select_fusion.2), channel_id=1, source_target_pairs={{0,8},{1,9},{2,10},{3,11},{4,12},{5,13},{6,14},{7,15},{8,0},{9,1},... | collective-permute-start | bytes 3538952 | tf_op jit(solution)/shard_map/ppermute | solution.py:405
  283.9 53.9 %collective-permute-start.29 = (bf16[256,768]{1,0:T(8,128)(2,1)}, bf16[256,768]{1,0:T(8,128)(2,1)}, u32[]{:S(2)}, u32[]{:S(2)}) collective-permute-start(bf16[256,768]{1,0:T(8,128)(2,1)} %get-tuple-element.65), channel_id=1, source_target_pairs={{0,0},{1,1},{2,2},{3,3},{4,8},{5,9},{6,10},{7,11},{8,4},{9,5},{10,... | collective-permute-start | bytes 1179656 | tf_op jit(solution)/shard_map/ppermute | solution.py:405
  292.7 45.2 %collective-permute-start.68 = (bf16[4,48,768]{2,1,0:T(8,128)(2,1)}, bf16[4,48,768]{2,1,0:T(8,128)(2,1)}, u32[]{:S(2)}, u32[]{:S(2)}) collective-permute-start(bf16[4,48,768]{2,1,0:T(8,128)(2,1)} %fusion.29), channel_id=1, source_target_pairs={{4,0},{5,1},{6,2},{7,3},{8,12},{9,13},{10,14},{11,15},{20,16},{21,... | collective-permute-start | bytes 884744 | tf_op jit(solution)/shard_map/ppermute | solution.py:405
  306.3 31.6 %collective-permute-start.56 = (bf16[48,768]{1,0:T(8,128)(2,1)S(1)}, bf16[48,768]{1,0:T(8,128)(2,1)}, u32[]{:S(2)}, u32[]{:S(2)}) collective-permute-start(bf16[48,768]{1,0:T(8,128)(2,1)S(1)} %add_convert_fusion.6), channel_id=1, source_target_pairs={{0,0},{1,2},{2,4},{3,6},{4,8},{5,10},{6,12},{7,14},{8,1},{9,3},{10... | collective-permute-start | bytes 221192 | tf_op jit(solution)/shard_map/ppermute | solution.py:405
  334.3 28.1 %collective-permute-start.40 = (bf16[1024,512]{1,0:T(8,128)(2,1)}, bf16[1024,512]{1,0:T(8,128)(2,1)S(1)}, u32[]{:S(2)}, u32[]{:S(2)}) collective-permute-start(bf16[1024,512]{1,0:T(8,128)(2,1)} %get-tuple-element.24), channel_id=1, source_target_pairs={{0,8},{1,9},{2,10},{3,11},{4,12},{5,13},{6,14},{7,15},{8,0},{9,1},... | collective-permute-start | bytes 3145736 | tf_op jit(solution)/shard_map/ppermute | solution.py:405
  351.8 32.0 %collective-permute-start.70 = (bf16[4,2,48,768]{3,2,0,1:T(8,128)(2,1)}, bf16[4,2,48,768]{3,2,0,1:T(8,128)(2,1)}, u32[]{:S(2)}, u32[]{:S(2)}) collective-permute-start(bf16[4,2,48,768]{3,2,0,1:T(8,128)(2,1)} %pad_maximum_fusion.10), channel_id=1, source_target_pairs={{0,8},{1,9},{2,10},{3,11},{12,4},{13,5},{14,6},{15,7},{16,24},{17,... | collective-permute-start | bytes 1769480 | tf_op jit(solution)/shard_map/ppermute | solution.py:405
  361.1 41.5 %collective-permute-start.60 = (bf16[4,48,1536]{2,1,0:T(8,128)(2,1)}, bf16[4,48,1536]{2,1,0:T(8,128)(2,1)}, u32[]{:S(2)}, u32[]{:S(2)}) collective-permute-start(bf16[4,48,1536]{2,1,0:T(8,128)(2,1)} %fusion.7), channel_id=1, source_target_pairs={{4,0},{5,1},{6,2},{7,3},{8,12},{9,13},{10,14},{11,15},{20,16},{21,... | collective-permute-start | bytes 1769480 | tf_op jit(solution)/shard_map/ppermute | solution.py:405
  378.3 19.6 %collective-permute-start.42 = (bf16[256,768]{1,0:T(8,128)(2,1)S(1)}, bf16[256,768]{1,0:T(8,128)(2,1)S(1)}, u32[]{:S(2)}, u32[]{:S(2)}) collective-permute-start(bf16[256,768]{1,0:T(8,128)(2,1)S(1)} %copy-done.68), channel_id=1, source_target_pairs={{0,1},{1,0},{2,3},{3,2},{4,5},{5,4},{6,7},{7,6},{8,9},{9,8},{10,11... | collective-permute-start | bytes 1179656 | tf_op jit(solution)/shard_map/ppermute | solution.py:405
  379.3 18.6 %collective-permute-start.43 = (bf16[256,768]{1,0:T(8,128)(2,1)S(1)}, bf16[256,768]{1,0:T(8,128)(2,1)S(1)}, u32[]{:S(2)}, u32[]{:S(2)}) collective-permute-start(bf16[256,768]{1,0:T(8,128)(2,1)S(1)} %copy-done.67), channel_id=1, source_target_pairs={{0,2},{1,3},{2,0},{3,1},{4,6},{5,7},{6,4},{7,5},{8,10},{9,11},{10,... | collective-permute-start | bytes 1179656 | tf_op jit(solution)/shard_map/ppermute | solution.py:405
  399.4 45.8 %collective-permute-start.44 = (bf16[256,768]{1,0:T(8,128)(2,1)S(1)}, bf16[256,768]{1,0:T(8,128)(2,1)S(1)}, u32[]{:S(2)}, u32[]{:S(2)}) collective-permute-start(bf16[256,768]{1,0:T(8,128)(2,1)S(1)} %fusion.6), channel_id=1, source_target_pairs={{0,0},{1,1},{2,2},{3,3},{4,8},{5,9},{6,10},{7,11},{8,4},{9,5},{10,... | collective-permute-start | bytes 1179656 | tf_op jit(solution)/shard_map/ppermute | solution.py:405
  (112 other events, 1176.7 us)

commit v2 on v1

--- a/solution.py
+++ b/solution.py
@@ -1,3 +1,5 @@
+import math
+
 import jax
 import jax.numpy as jnp
 from jax import lax
@@ -374,6 +376,11 @@
 MASKED = -1e30
 
 
+def cost(flops, *arrays):
+    moved = sum(math.prod(array.shape) * array.dtype.itemsize for array in arrays)
+    return pl.CostEstimate(flops=flops, transcendentals=0, bytes_accessed=moved)
+
+
 def moves(target):
     pairs = []
     for rep in range(4):
@@ -390,7 +397,7 @@
 OTHER_X = moves(lambda x, c, h, j: (1 - x, c, h, j))
 OTHER_HALF = moves(lambda x, c, h, j: (x, c, 1 - h, j))
 SQUARE = [moves(lambda x, c, h, j, k=k: (x, c, h, j ^ k)) for k in range(GROUP)]
-ROUND = [moves(lambda x, c, h, j, k=k: (x, c, h ^ c, j ^ k)) for k in range(GROUP)]
+ROUND = [moves(lambda x, c, h, j, i=i: (x, c, h ^ c, j ^ (2 * x + i))) for i in range(2)]
 OUT_FETCH = moves(lambda x, c, h, j: (x, j % 2, c, (4 * h + j) // 2))
 OUT_RETURN = moves(lambda x, c, h, j: (x, h, (2 * j + c) // 4, (2 * j + c) % 4))
 HOME_HALF = moves(lambda x, c, h, j: (x, c, 1 - h, j) if c != h else None)
@@ -460,6 +467,7 @@
             jax.ShapeDtypeStruct((rows, WIDE), BF),
             jax.ShapeDtypeStruct((rows, 2 * WIDE), BF),
         ],
+        cost_estimate=cost(2 * rows * w_qkv.size, x_rows, w_qkv, x_rows, cosine, sine),
         name="project",
     )(x_rows, w_qkv, cosine, sine)
 
@@ -581,6 +589,9 @@
             jax.ShapeDtypeStruct((rows, WIDE), BF),
             jax.ShapeDtypeStruct((8, rows), F32),
         ],
+        cost_estimate=cost(
+            4 * OWN_HEADS * WIDE * rows * 2 * rows, queries, kv_own, kv_other, queries
+        ),
         name="attend",
     )(ids, row_ids, col_ids, queries, kv_own, kv_other)
 
@@ -709,6 +720,9 @@
             jax.ShapeDtypeStruct((rows, 2 * WIDE), F32),
             jax.ShapeDtypeStruct((rows, 2 * WIDE), BF),
         ],
+        cost_estimate=cost(
+            10 * OWN_HEADS * WIDE * rows * 2 * rows, queries, kv_own, kv_other, queries
+        ),
         name="attend_back",
     )(ids, row_ids, col_ids, queries, upstream, attended, logs, kv_own, kv_other, cosine, sine)
 
@@ -732,19 +746,274 @@
         in_specs=[tiled(WIDE), tiled(2 * WIDE), tiled(2 * WIDE), tiled(128), tiled(128)],
         out_specs=tiled(3 * WIDE),
         out_shape=jax.ShapeDtypeStruct((rows, 3 * WIDE), BF),
+        cost_estimate=cost(8 * own.size, own, own, got, grad_queries),
         name="join_grads",
     )(grad_queries, own, got, cosine, sine)
 
 
+def after(value, *others):
+    return lax.optimization_barrier((value,) + others)[0]
+
+
+def join(*values):
+    return lax.optimization_barrier(values)
+
+
+def pack_qkv_kernel(target_ref, w_ref, vectors_ref, *refs):
+    packed = refs[-1]
+    for target in range(GROUP):
+        for part in range(3):
+            start = part * D + target * NARROW
+            packed[target, :, part * NARROW : (part + 1) * NARROW] = w_ref[
+                :, start : start + NARROW
+            ]
+        packed[target, :, 3 * NARROW :] = vectors_ref[...]
+    for index, ref in enumerate(refs[:-1]):
+        ref[...] = packed[target_ref[index]]
+
+
+def pack_qkv(targets, w_qkv, vectors):
+    rows = w_qkv.shape[0]
+    width = 3 * NARROW + vectors.shape[1]
+    return pl.pallas_call(
+        pack_qkv_kernel,
+        in_specs=[
+            pl.BlockSpec(memory_space=pltpu.SMEM),
+            pl.BlockSpec(memory_space=pltpu.VMEM),
+            pl.BlockSpec(memory_space=pltpu.VMEM),
+        ],
+        out_specs=[pl.BlockSpec(memory_space=pltpu.VMEM)] * 2,
+        out_shape=[jax.ShapeDtypeStruct((rows, width), BF)] * 2,
+        scratch_shapes=[pltpu.VMEM((GROUP, rows, width), BF)],
+        name="pack_qkv",
+    )(targets, w_qkv, vectors)
+
+
+def pack_gate_up_kernel(target_ref, gate_ref, up_ref, *refs):
+    packed = refs[-1]
+    width = packed.shape[2] // 4
+    for target in range(GROUP):
+        for index in range(4):
+            source = (gate_ref, up_ref)[index // 2]
+            start = (index % 2 * GROUP + target) * width
+            packed[target, :, index * width : (index + 1) * width] = source[
+                :, start : start + width
+            ]
+    for index, ref in enumerate(refs[:-1]):
+        ref[...] = packed[target_ref[index]]
+
+
+def pack_gate_up(targets, w_gate, w_up):
+    rows = w_gate.shape[0]
+    width = 2 * w_gate.shape[1] // GROUP
+    return pl.pallas_call(
+        pack_gate_up_kernel,
+        in_specs=[
+            pl.BlockSpec(memory_space=pltpu.SMEM),
+            pl.BlockSpec(memory_space=pltpu.VMEM),
+            pl.BlockSpec(memory_space=pltpu.VMEM),
+        ],
+        out_specs=[pl.BlockSpec(memory_space=pltpu.VMEM)] * 2,
+        out_shape=[jax.ShapeDtypeStruct((rows, width), BF)] * 2,
+        scratch_shapes=[pltpu.VMEM((GROUP, rows, width), BF)],
+        name="pack_gate_up",
+    )(targets, w_gate, w_up)
+
+
+def unpack_qkv_kernel(place_ref, near_ref, far_ref, out_ref, vectors_ref):
+    zeros = jnp.zeros((near_ref.shape[1], WIDE - NARROW), BF)
+    for index in range(2 * GROUP):
+        source = (near_ref, far_ref)[index // GROUP]
+        place = place_ref[index]
+        for part in range(3):
+            out_ref[place, :, part * WIDE : part * WIDE + NARROW] = source[
+                index % GROUP, :, part * NARROW : (part + 1) * NARROW
+            ]
+            out_ref[place, :, part * WIDE + NARROW : (part + 1) * WIDE] = zeros
+        vectors_ref[place] = source[index % GROUP, :, 3 * NARROW :]
+
+
+def unpack_qkv(places, near, far):
+    _, rows, width = near.shape
+    return pl.pallas_call(
+        unpack_qkv_kernel,
+        in_specs=[
+            pl.BlockSpec(memory_space=pltpu.SMEM),
+            pl.BlockSpec(memory_space=pltpu.VMEM),
+            pl.BlockSpec(memory_space=pltpu.VMEM),
+        ],
+        out_specs=[pl.BlockSpec(memory_space=pltpu.VMEM)] * 2,
+        out_shape=[
+            jax.ShapeDtypeStruct((2 * GROUP, rows, 3 * WIDE), BF),
+            jax.ShapeDtypeStruct((2 * GROUP, rows, width - 3 * NARROW), BF),
+        ],
+        name="unpack_qkv",
+    )(places, near, far)
+
+
+def unpack_kernel(place_ref, near_ref, far_ref, out_ref):
+    first = pl.program_id(0) < GROUP
+    out_ref[...] = jnp.where(first, near_ref[...], far_ref[...])
+
+
+def unpack(places, near, far):
+    count, rows, width = near.shape
+    return pl.pallas_call(
+        unpack_kernel,
+        grid_spec=pltpu.PrefetchScalarGridSpec(
+            num_scalar_prefetch=1,
+            grid=(2 * count,),
+            in_specs=[
+                pl.BlockSpec((1, rows, width), lambda i, p: (jnp.minimum(i, count - 1), 0, 0)),
+                pl.BlockSpec((1, rows, width), lambda i, p: (jnp.maximum(i - count, 0), 0, 0)),
+            ],
+            out_specs=pl.BlockSpec((1, rows, width), lambda i, p: (p[i], 0, 0)),
+        ),
+        out_shape=jax.ShapeDtypeStruct((2 * count, rows, width), BF),
+        name="unpack",
+    )(places, near, far)
+
+
+def split_feed_kernel(x_ref, down_ref, down_got_ref, gate_up_ref, gate_up_got_ref, keep_ref, away_ref):
+    mine = x_ref[0]
+    width = down_ref.shape[-1]
+    for block in range(GROUP):
+        for side, ref in ((mine, keep_ref), (1 - mine, away_ref)):
+            ref[block] = (
+                down_ref[block, side] + down_got_ref[block, side].astype(F32)
+            ).astype(BF)
+            total = gate_up_ref[block, side] + gate_up_got_ref[block, side].astype(F32)
+            ref[GROUP + block] = total[:, :width].astype(BF)
+            ref[2 * GROUP + block] = total[:, width:].astype(BF)
+
+
+def whole_call(kernel, name, shapes, scalars, *arrays):
+    return pl.pallas_call(
+        kernel,
+        in_specs=[pl.BlockSpec(memory_space=pltpu.SMEM)]
+        + [pl.BlockSpec(memory_space=pltpu.VMEM)] * len(arrays),
+        out_specs=[pl.BlockSpec(memory_space=pltpu.VMEM)] * len(shapes),
+        out_shape=[jax.ShapeDtypeStruct(shape, dtype) for shape, dtype in shapes],
+        cost_estimate=cost(sum(a.size for a in arrays), *arrays, *arrays),
+        name=name,
+    )(scalars, *arrays)
+
+
+def square_feed_kernel(index_ref, mine_ref, got_ref, kept_ref, *send_refs):
+    for k in range(GROUP):
+        target = index_ref[k]
+        for part in range(2):
+            slot = (part + 1) * GROUP + target
+            block = mine_ref[slot] + got_ref[slot]
+            if k == 0:
+                kept_ref[GROUP + part] = block
+            else:
+                send_refs[k - 1][part] = block
+        kept_ref[k] = mine_ref[k] + got_ref[k]
+
+
+def join_feed_kernel(index_ref, kept_ref, *refs):
+    out_ref = refs[-1]
+    for k in range(GROUP):
+        out_ref[k] = kept_ref[k]
+        for part in range(2):
+            slot = (part + 1) * GROUP + index_ref[k]
+            out_ref[slot] = kept_ref[GROUP + part] if k == 0 else refs[k - 1][part]
+
+
+def finish_feed_kernel(flag_ref, own_ref, other_ref, far_own_ref, far_other_ref, down_ref, gate_ref, up_ref):
+    mine, at_home = flag_ref[0], flag_ref[1] == 1
+    rows = own_ref.shape[1]
+    half = own_ref.shape[2] // 2
+    for slot in range(3 * GROUP):
+        for near, far, side in ((own_ref, far_own_ref, mine), (other_ref, far_other_ref, 1 - mine)):
+            block = jnp.where(at_home, near[slot], far[slot]).astype(F32)
+            if slot < GROUP:
+                down_ref[slot, side] = block
+            else:
+                ref = gate_ref if slot < 2 * GROUP else up_ref
+                start = slot % GROUP * half
+                width = GROUP * half
+                ref[side, :, start : start + half] = block[:, :half]
+                ref[side, :, width + start : width + start + half] = block[:, half:]
+
+
+def split_cores_kernel(c_ref, part_ref, vectors_ref, away_ref):
+    rows = part_ref.shape[1]
+    away_ref[:rows] = part_ref[1 - c_ref[0]].astype(BF)
+    away_ref[rows:] = jnp.zeros((16, part_ref.shape[2]), BF)
+    away_ref[rows : rows + 8] = vectors_ref[...].astype(BF)
+
+
+def split_x_kernel(flag_ref, part_ref, vectors_ref, got_ref, keep_ref, away_ref):
+    core, mine = flag_ref[0], flag_ref[1]
+    rows = part_ref.shape[1]
+    step = rows // (2 * GROUP)
+    for block in range(GROUP):
+        for side, ref in ((mine, keep_ref), (1 - mine, away_ref)):
+            place = pl.ds(pl.multiple_of((2 * block + side) * step, step), step)
+            ref[block * step : (block + 1) * step] = (
+                part_ref[core, place] + got_ref[place].astype(F32)
+            ).astype(BF)
+    for ref in (keep_ref, away_ref):
+        ref[GROUP * step :] = got_ref[rows:]
+        ref[GROUP * step : GROUP * step + 8] = (
+            vectors_ref[...] + got_ref[rows : rows + 8].astype(F32)
+        ).astype(BF)
+
+
+def square_qkv_kernel(index_ref, mine_ref, got_ref, *refs):
+    step = (mine_ref.shape[0] - 16) // GROUP
+    vectors = mine_ref[GROUP * step :] + got_ref[GROUP * step :]
+    for k in range(GROUP):
+        place = pl.ds(pl.multiple_of(index_ref[k] * step, step), step)
+        refs[k][:step] = mine_ref[place] + got_ref[place]
+        refs[k][step:] = vectors
+
+
+def join_qkv_kernel(index_ref, *refs):
+    out_ref = refs[-1]
+    step = refs[0].shape[0] - 16
+    vectors = refs[0][step:].astype(F32)
+    for k in range(GROUP):
+        place = pl.ds(pl.multiple_of(index_ref[k] * step, step), step)
+        out_ref[place] = refs[k][:step]
+        if k:
+            vectors += refs[k][step:].astype(F32)
+    out_ref[GROUP * step :] = vectors.astype(BF)
+
+
+def finish_qkv_kernel(flag_ref, own_ref, other_ref, far_own_ref, far_other_ref, out_ref, vectors_ref):
+    mine, at_home = flag_ref[0], flag_ref[1] == 1
+    step = (own_ref.shape[0] - 16) // GROUP
+    for block in range(GROUP):
+        rows = slice(block * step, (block + 1) * step)
+        for near, far, side in ((own_ref, far_own_ref, mine), (other_ref, far_other_ref, 1 - mine)):
+            values = jnp.where(at_home, near[rows], far[rows]).astype(F32)
+            for part in range(3):
+                start = part * D + block * NARROW
+                out_ref[side, :, start : start + NARROW] = values[
+                    :, part * WIDE : part * WIDE + NARROW
+                ]
+    rows = slice(GROUP * step, GROUP * step + 8)
+    vectors_ref[...] = jnp.where(at_home, own_ref[rows], far_own_ref[rows]).astype(F32)
+
+
 def gather_square(block):
     return [block] + [send(block, SQUARE[k]) for k in range(1, GROUP)]
 
 
-def reduce_square(left, weight, weight_dim):
-    got = []
-    for k in (3, 1, 2):
-        part = contract(left[k * TILE : (k + 1) * TILE], weight, 1, weight_dim)
-        got.append(send(part.astype(BF), SQUARE[k]))
+def square_parts(left, weight, weight_dim):
+    return [
+        contract(left[k * TILE : (k + 1) * TILE], weight, 1, weight_dim).astype(BF)
+        for k in range(1, GROUP)
+    ]
+
+
+def reduce_square(left, weight, weight_dim, parts=None):
+    if parts is None:
+        parts = square_parts(left, weight, weight_dim)
+    got = [send(part, SQUARE[k + 1]) for k, part in enumerate(parts)]
     total = contract(left[:TILE], weight, 1, weight_dim)
     for part in got:
         total = total + part.astype(F32)
@@ -783,62 +1052,22 @@
     inputs_bf = send(tokens_in.reshape(token_count, D), SPREAD)
     doc_ids = send(segment_ids, SPREAD).reshape(2, GROUP, token_count)
 
-    def by_target(rows_of_targets):
-        return [lax.dynamic_index_in_dim(rows_of_targets, j ^ k, 0, False) for k in range(GROUP)]
-
-    def fetch_columns(targets):
-        mine = [send(part, ROUND[k]) for k, part in enumerate(by_target(targets))]
-        mine = jnp.stack(mine)
-        other = send(mine, OTHER_CORE)
-        away = c != h
-        low = pick(away, mine, other)
-        high = pick(away, other, mine)
-        return jnp.concatenate([jnp.stack(unmix(low, j)), jnp.stack(unmix(high, j))], axis=0)
+    by_x = jnp.stack([2 * x, 2 * x + 1, 2 - 2 * x, 3 - 2 * x]) ^ j
+    targets = by_x[:2]
+    places = jnp.concatenate([GROUP * (h ^ c) + by_x, GROUP * (1 - (h ^ c)) + by_x])
 
     vectors = jnp.stack([ln1_gain, ln1_bias, ln2_gain, ln2_bias], axis=1)
-    qkv_targets = jnp.transpose(w_qkv.reshape(rows_d, 3, GROUP, NARROW), (2, 0, 1, 3)).reshape(
-        GROUP, rows_d, 3 * NARROW
-    )
-    qkv_targets = jnp.concatenate(
-        [qkv_targets, jnp.broadcast_to(vectors[None], (GROUP, rows_d, 4))], axis=2
-    )
-    qkv_got = fetch_columns(qkv_targets)
-    vectors_full = jnp.transpose(qkv_got[:, :, 3 * NARROW :].reshape(D, 4)).astype(F32)
-    gain_one, bias_one, gain_two, bias_two = (vectors_full[i] for i in range(4))
-    qkv_own = jnp.pad(
-        qkv_got[:, :, : 3 * NARROW].reshape(D, 3, NARROW), ((0, 0), (0, 0), (0, WIDE - NARROW))
-    ).reshape(D, 3 * WIDE)
-
-    out_got = send(w_out, OUT_FETCH)
-    out_other = send(out_got, OTHER_CORE)
-    out_own = jnp.concatenate(
-        [
-            pick(core_is_one, out_got, out_other),
-            pick(core_is_one, out_other, out_got),
-            jnp.zeros((WIDE - NARROW, D), BF),
-        ],
-        axis=0,
-    )
-
-    half_f = rows_f // 2
-    down_mine = send(lax.dynamic_slice_in_dim(w_down, c * half_f, half_f, 0), OTHER_HALF)
-    down_other = send(down_mine, OTHER_CORE)
-    down_far = jnp.concatenate(
-        [pick(core_is_one, down_mine, down_other), pick(core_is_one, down_other, down_mine)], axis=0
-    )
-    down_own = jnp.concatenate(
-        [pick(half_is_one, w_down, down_far), pick(half_is_one, down_far, w_down)], axis=0
-    )
-
-    def column_targets(weight):
-        return jnp.transpose(weight.reshape(rows_d, 2, GROUP, rows_f), (2, 0, 1, 3)).reshape(
-            GROUP, rows_d, slice_f
-        )
-
-    gate_up_got = fetch_columns(
-        jnp.concatenate([column_targets(w_gate), column_targets(w_up)], axis=2)
-    )
-    gate_up_own = gate_up_got.reshape(D, 2 * slice_f)
+    qkv_packed = pack_qkv(targets, w_qkv, vectors)
+    qkv_mine = after(
+        jnp.stack([send(part, ROUND[i]) for i, part in enumerate(qkv_packed)]), inputs_bf
+    )
+    x_tiles = gather_square(inputs_bf)
+    qkv_near = jnp.concatenate([qkv_mine, send(qkv_mine, OTHER_X)], axis=0)
+    qkv_far = send(qkv_near, OTHER_CORE)
+    qkv_own, vectors_got = unpack_qkv(places, qkv_near, qkv_far)
+    qkv_own = qkv_own.reshape(D, 3 * WIDE)
+    x_rows = jnp.concatenate(x_tiles, axis=0)
+    x_rows, qkv_own, vectors_got, w_out = join(x_rows, qkv_own, vectors_got, w_out)
 
     tile_index = j ^ jnp.arange(GROUP, dtype=jnp.int32)
     first_row = (c * GROUP + tile_index) * token_count
@@ -858,26 +1087,71 @@
     row_ids = ids.reshape(length // TILE, 1, TILE)
     col_ids = flat_ids[:, None]
 
-    x_rows = jnp.concatenate(gather_square(inputs_bf), axis=0)
+    part_f = rows_f // 4
+    gate_up_packed = pack_gate_up(targets, w_gate, w_up)
+    down_sent = lax.dynamic_slice_in_dim(w_down, (2 * c + x) * part_f, part_f, 0)
+
     queries, kv_own = project(x_rows, qkv_own, cosine, sine)
     kv_other = send(kv_own, OTHER_CORE)
+    kv_other, w_out, down_sent, *gate_up_packed = join(kv_other, w_out, down_sent, *gate_up_packed)
     attended, logs = attend(flat_ids, row_ids, col_ids, queries, kv_own, kv_other)
-    branch = reduce_square(attended, out_own, 0)
+    out_got = send(w_out, OUT_FETCH)
+    gate_up_first = [send(part, ROUND[i]) for i, part in enumerate(gate_up_packed)]
+    down_mine = send(down_sent, OTHER_HALF)
+    attended, logs, out_got, down_mine, *gate_up_first = join(
+        attended, logs, out_got, down_mine, *gate_up_first
+    )
+    out_other = send(out_got, OTHER_CORE)
+    out_own = jnp.concatenate(
+        [
+            pick(core_is_one, out_got, out_other),
+            pick(core_is_one, out_other, out_got),
+            jnp.zeros((WIDE - NARROW, D), BF),
+        ],
+        axis=0,
+    )
+
+    branch_parts = square_parts(attended, out_own, 0)
+    gate_up_mine, down_mine, *branch_parts = join(
+        jnp.stack(gate_up_first), down_mine, *branch_parts
+    )
+    gate_up_second = send(gate_up_mine, OTHER_X)
+    down_got = send(down_mine, OTHER_X)
+    branch = reduce_square(attended, out_own, 0, branch_parts)
+    vectors_full = jnp.transpose(vectors_got.reshape(D, 4)).astype(F32)
+    gain_one, bias_one, gain_two, bias_two = (vectors_full[i] for i in range(4))
     first_out, first_normed, first_scale = norm_forward(
         inputs_bf.astype(F32) + branch, gain_one, bias_one
     )
-
-    first_rows = jnp.concatenate(gather_square(first_out.astype(BF)), axis=0)
+    first_bf, gate_up_second, down_got, out_cotangent = join(
+        first_out.astype(BF), gate_up_second, down_got, out_cotangent
+    )
+
+    first_tiles = gather_square(first_bf)
+    gate_up_near = jnp.concatenate([gate_up_mine, gate_up_second], axis=0)
+    gate_up_far = send(gate_up_near, OTHER_CORE)
+    gate_up_own = unpack(places, gate_up_near, gate_up_far).reshape(D, 2 * slice_f)
+    down_pair = jnp.concatenate(
+        [pick(x_is_one, down_mine, down_got), pick(x_is_one, down_got, down_mine)], axis=0
+    )
+    down_other = send(down_pair, OTHER_CORE)
+    down_far = jnp.concatenate(
+        [pick(core_is_one, down_pair, down_other), pick(core_is_one, down_other, down_pair)], axis=0
+    )
+    down_own = jnp.concatenate(
+        [pick(half_is_one, w_down, down_far), pick(half_is_one, down_far, w_down)], axis=0
+    )
+    first_rows = jnp.concatenate(first_tiles, axis=0)
     acts = contract(first_rows, gate_up_own, 1, 0)
     gate_act, up_act = acts[:, :slice_f], acts[:, slice_f:]
     hidden_bf = (jax.nn.silu(gate_act) * up_act).astype(BF)
+    cotangent = send(after(out_cotangent, hidden_bf).reshape(token_count, D), SPREAD)
     down_act = reduce_square(hidden_bf, down_own, 0)
     result, second_normed, second_scale = norm_forward(first_out + down_act, gain_two, bias_two)
-    result_home = send(result.astype(BF), SPREAD)
-
-    upstream = send(out_cotangent.reshape(token_count, D), SPREAD).astype(F32)
-    grad_gain_two = jnp.sum(upstream * second_normed, axis=0)
-    grad_bias_two = jnp.sum(upstream, axis=0)
+
+    upstream = cotangent.astype(F32)
+    grad_gain_two = jnp.sum(upstream * second_normed, axis=0, keepdims=True)
+    grad_bias_two = jnp.sum(upstream, axis=0, keepdims=True)
     grad_second = norm_backward(upstream, second_normed, second_scale, gain_two)
     grad_down_rows = jnp.concatenate(gather_square(grad_second.astype(BF)), axis=0)
     grad_hidden = contract(grad_down_rows, down_own, 1, 1)
@@ -887,99 +1161,140 @@
     ).astype(BF)
     grad_up_bf = (grad_hidden * (gate_act * sigmoid_gate)).astype(BF)
     grad_acts = jnp.concatenate([grad_gate_bf, grad_up_bf], axis=1)
-    grad_first = grad_second + reduce_square(grad_acts, gate_up_own, 1)
-    grad_gain_one = jnp.sum(grad_first * first_normed, axis=0)
-    grad_bias_one = jnp.sum(grad_first, axis=0)
+    first_parts = square_parts(grad_acts, gate_up_own, 1)
+
+    quarter = rows_d // 2
+    step_square = jnp.arange(GROUP, dtype=jnp.int32) ^ j
+    x_flag = x.reshape(1)
+    home_flags = jnp.stack([x, at_home.astype(jnp.int32)])
+
+    def over_cores(partial):
+        keep = pick(core_is_one, partial[0], partial[1])
+        away = pick(core_is_one, partial[1], partial[0])
+        return keep, send(away.astype(BF), OTHER_CORE)
+
+    by_x_rows = (GROUP, 2, quarter)
+    gate_up_keep, gate_up_got = over_cores(
+        contract(first_rows, after(grad_acts, *first_parts), 0, 0).reshape(
+            2, D // 2, 2 * slice_f
+        )
+    )
+    down_keep, down_got = over_cores(
+        contract(hidden_bf, after(grad_down_rows, *first_parts), 0, 0).reshape(2, rows_f, D)
+    )
+    bundle_shape = ((3 * GROUP, quarter, D), BF)
+    feed_keep, feed_away = whole_call(
+        split_feed_kernel, "split_feed", [bundle_shape] * 2, x_flag,
+        down_keep.reshape(by_x_rows + (D,)), down_got.reshape(by_x_rows + (D,)),
+        gate_up_keep.reshape(by_x_rows + (2 * slice_f,)),
+        gate_up_got.reshape(by_x_rows + (2 * slice_f,)),
+    )
+    grad_first = grad_second + reduce_square(grad_acts, gate_up_own, 1, first_parts)
+    grad_first, feed_away = join(grad_first, feed_away)
+    feed_got = send(feed_away, OTHER_X)
+    grad_gain_one = jnp.sum(grad_first * first_normed, axis=0, keepdims=True)
+    grad_bias_one = jnp.sum(grad_first, axis=0, keepdims=True)
     grad_res = norm_backward(grad_first, first_normed, first_scale, gain_one)
 
     grad_branch_rows = jnp.concatenate(gather_square(grad_res.astype(BF)), axis=0)
     grad_attended = contract(grad_branch_rows, out_own, 1, 1).astype(BF)
+    out_keep, out_got = over_cores(
+        contract(attended, grad_branch_rows, 0, 0)[:NARROW].reshape(2, rows_d, D)
+    )
+    grad_attended, feed_got, out_got = join(grad_attended, feed_got, out_got)
+    feed_mine = feed_keep + feed_got
+    out_total = (out_keep + out_got.astype(F32)).astype(BF)
+    grad_attended, feed_mine, out_total, result_bf = join(
+        grad_attended, feed_mine, out_total, result.astype(BF)
+    )
     grad_queries, kv_grad_own, kv_grad_away = attend_back(
         flat_ids, row_ids, col_ids, queries, grad_attended, attended, logs, kv_own, kv_other,
         cosine, sine,
     )
+    feed_home = send(feed_mine, HOME_HALF)
+    out_far = send(out_total, OTHER_X)
+    result_home = send(result_bf, SPREAD)
+    grad_queries, kv_grad_own, kv_grad_away, feed_home, out_far, result_home = join(
+        grad_queries, kv_grad_own, kv_grad_away, feed_home, out_far, result_home
+    )
     kv_grad_got = send(kv_grad_away, OTHER_CORE)
     grad_projected = join_grads(grad_queries, kv_grad_own, kv_grad_got, cosine, sine)
-    grad_inputs = grad_res + reduce_square(grad_projected, qkv_own, 1)
-    grad_inputs_home = send(grad_inputs.astype(BF), SPREAD).astype(F32)
-
-    quarter = rows_d // 2
-
-    def rows_for_home(partial):
-        partial = partial.astype(BF)
-        keep = pick(core_is_one, partial[0], partial[1]).astype(F32)
-        away = pick(core_is_one, partial[1], partial[0])
-        total = keep + send(away, OTHER_CORE).astype(F32)
-        total = total.astype(BF).reshape(-1, 2, quarter, total.shape[-1])
-        keep = pick(x_is_one, total[:, 0], total[:, 1]).astype(F32)
-        away = pick(x_is_one, total[:, 1], total[:, 0])
-        total = keep + send(away, OTHER_X).astype(F32)
-        total_bf = total.astype(BF)
-        return (total + send(total_bf, HOME_HALF).astype(F32)).astype(BF)
-
-    def both_x(mine, axis):
-        got = send(mine, HOME_X)
-        return jnp.stack(
-            [pick(x_is_one, mine, got), pick(x_is_one, got, mine)], axis=axis
-        )
-
-    def both_cores(mine):
-        return pick(at_home, send(mine, HOME_CORE), mine).astype(F32)
-
-    def to_row_owner(mine):
-        parts = by_target(mine)
-        return unmix([parts[0]] + [send(parts[k], HOME_SQUARE[k]) for k in range(1, GROUP)], j)
-
-    grad_down_part = contract(hidden_bf, grad_down_rows, 0, 0).reshape(2, rows_f, D)
-    down_mine = rows_for_home(grad_down_part)
-    grad_w_down = both_cores(both_x(down_mine, 1)).reshape(rows_f, D)
-
-    grad_gate_up_part = contract(first_rows, grad_acts, 0, 0).reshape(2, D // 2, 2 * slice_f)
-    gate_up_mine = rows_for_home(grad_gate_up_part)
-    gate_up_mine = jnp.stack(to_row_owner(gate_up_mine), axis=1)
-    gate_up_all = both_cores(both_x(gate_up_mine, 0)).reshape(rows_d, GROUP, 2, 2, rows_f)
-    gate_up_all = jnp.transpose(gate_up_all, (2, 0, 3, 1, 4)).reshape(2, rows_d, w_gate.shape[1])
-    grad_w_gate, grad_w_up = gate_up_all[0], gate_up_all[1]
-
-    grad_out_part = contract(attended, grad_branch_rows, 0, 0)[:NARROW].astype(BF)
-    grad_out_part = grad_out_part.reshape(2, 2, quarter, D)
-    keep = pick(core_is_one, grad_out_part[0], grad_out_part[1]).astype(F32)
-    away = pick(core_is_one, grad_out_part[1], grad_out_part[0])
-    out_total = (keep + send(away, OTHER_CORE).astype(F32)).astype(BF)
-    keep = pick(x_is_one, out_total[0], out_total[1]).astype(F32)
-    away = pick(x_is_one, out_total[1], out_total[0])
-    out_total = (keep + send(away, OTHER_X).astype(F32)).astype(BF)
-    out_total = (out_total.astype(F32) + send(out_total, OTHER_HALF).astype(F32)).astype(BF)
-    out_mine = send(out_total, OUT_RETURN)
-    out_got = send(out_mine, OTHER_X)
-    grad_w_out = jnp.concatenate(
-        [pick(x_is_one, out_mine, out_got), pick(x_is_one, out_got, out_mine)], axis=0
-    ).astype(F32)
-
-    grad_qkv_part = contract(x_rows, grad_projected, 0, 0).reshape(D, 3, WIDE)[:, :, :NARROW]
-    vector_part = jnp.stack([grad_gain_one, grad_bias_one, grad_gain_two, grad_bias_two], axis=1)
-    grad_qkv_part = jnp.concatenate([grad_qkv_part.reshape(D, 3 * NARROW), vector_part], axis=1)
-    qkv_mine = rows_for_home(grad_qkv_part.reshape(2, D // 2, 3 * NARROW + 4))
-    qkv_parts = to_row_owner(qkv_mine)
-    vector_sum = sum(part[:, 3 * NARROW :].astype(F32) for part in qkv_parts)
-    columns = jnp.stack([part[:, : 3 * NARROW] for part in qkv_parts], axis=1)
-    columns = columns.reshape(quarter, GROUP, 3, NARROW)
-    columns = jnp.transpose(columns, (0, 2, 1, 3)).reshape(quarter, 3 * D)
-    qkv_all = jnp.concatenate([columns, vector_sum.astype(BF)], axis=1)
-    qkv_all = both_cores(both_x(qkv_all, 0)).reshape(rows_d, 3 * D + 4)
-    grad_w_qkv = qkv_all[:, : 3 * D]
-    vector_grads = jnp.transpose(qkv_all[:, 3 * D :])
+
+    input_parts = square_parts(grad_projected, qkv_own, 1)
+    grad_projected, x_rows, *input_parts = join(grad_projected, x_rows, *input_parts)
+    qkv_part = contract(x_rows, grad_projected, 0, 0).reshape(2, D // 2, 3 * WIDE)
+    vector_part = jnp.concatenate(
+        [grad_gain_one, grad_bias_one, grad_gain_two, grad_bias_two]
+        + [jnp.zeros((4, D), F32)], axis=0
+    )
+    moved_rows = D // 4 + 16
+    (qkv_away,) = whole_call(
+        split_cores_kernel, "split_cores", [((D // 2 + 16, 3 * WIDE), BF)], c.reshape(1),
+        qkv_part, vector_part,
+    )
+    qkv_away, feed_mine, feed_home = join(qkv_away, feed_mine, feed_home)
+    qkv_got = send(qkv_away, OTHER_CORE)
+    feed_kept, *feed_sends = whole_call(
+        square_feed_kernel, "square_feed",
+        [((GROUP + 2, quarter, D), BF)] + [((2, quarter, D), BF)] * 3,
+        step_square, feed_mine, feed_home,
+    )
+    qkv_got, *feed_sends = join(qkv_got, *feed_sends)
+    feed_gots = [send(part, HOME_SQUARE[k + 1]) for k, part in enumerate(feed_sends)]
+    qkv_keep, qkv_away = whole_call(
+        split_x_kernel, "split_x", [((moved_rows, 3 * WIDE), BF)] * 2, jnp.stack([c, x]),
+        qkv_part, vector_part, qkv_got,
+    )
+    qkv_away, *feed_gots = join(qkv_away, *feed_gots)
+    qkv_got = send(qkv_away, OTHER_X)
+    (feed_bundle,) = whole_call(
+        join_feed_kernel, "join_feed", [bundle_shape], step_square, feed_kept, *feed_gots
+    )
+    grad_inputs = grad_res + reduce_square(grad_projected, qkv_own, 1, input_parts)
+    inputs_back, feed_bundle, qkv_got, out_total, out_far = join(
+        grad_inputs.astype(BF), feed_bundle, qkv_got, out_total, out_far
+    )
+    grad_inputs_home = send(inputs_back, SPREAD)
+    feed_other = send(feed_bundle, HOME_X)
+    feed_far = send(feed_bundle, HOME_CORE)
+    qkv_mine = qkv_keep + qkv_got
+    qkv_home = send(qkv_mine, HOME_HALF)
+    out_total = (out_total.astype(F32) + out_far.astype(F32)).astype(BF)
+    out_got = send(out_total, OTHER_HALF)
+    qkv_home, out_got, feed_other, feed_far = join(qkv_home, out_got, feed_other, feed_far)
+    feed_far_other = send(feed_other, HOME_CORE)
+    qkv_sends = whole_call(
+        square_qkv_kernel, "square_qkv", [((quarter + 16, 3 * WIDE), BF)] * GROUP,
+        step_square, qkv_mine, qkv_home,
+    )
+    qkv_sends, out_total, feed_far_other = join(qkv_sends, out_total + out_got, feed_far_other)
+    qkv_gots = [qkv_sends[0]] + [send(qkv_sends[k], HOME_SQUARE[k]) for k in range(1, GROUP)]
+    grad_w_out = send(out_total, OUT_RETURN)
+    grad_w_down, grad_w_gate, grad_w_up = whole_call(
+        finish_feed_kernel, "finish_feed",
+        [(by_x_rows + (D,), F32)] + [((2, quarter, w_gate.shape[1]), F32)] * 2,
+        home_flags, feed_bundle, feed_other, feed_far, feed_far_other,
+    )
+    (qkv_bundle,) = whole_call(
+        join_qkv_kernel, "join_qkv", [((moved_rows, 3 * WIDE), BF)], step_square, *qkv_gots
+    )
+    qkv_other = send(qkv_bundle, HOME_X)
+    grad_w_qkv, vector_grads = whole_call(
+        finish_qkv_kernel, "finish_qkv", [((2, quarter, 3 * D), F32), ((8, D), F32)],
+        home_flags, qkv_bundle, qkv_other, send(qkv_bundle, HOME_CORE), send(qkv_other, HOME_CORE),
+    )
+    vector_grads = lax.dynamic_slice_in_dim(vector_grads, shard * rows_d, rows_d, 1)
 
     return (
         result_home.reshape(tokens_in.shape),
-        grad_inputs_home.reshape(tokens_in.shape),
-        grad_w_qkv,
-        grad_w_out,
+        grad_inputs_home.astype(F32).reshape(tokens_in.shape),
+        grad_w_qkv.reshape(w_qkv.shape),
+        grad_w_out.astype(F32),
         vector_grads[0],
         vector_grads[1],
-        grad_w_gate,
-        grad_w_up,
-        grad_w_down,
+        grad_w_gate.reshape(w_gate.shape),
+        grad_w_up.reshape(w_up.shape),
+        grad_w_down.reshape(w_down.shape),
         vector_grads[2],
         vector_grads[3],
     )

time: 477 us -> 429 us (0.90)
  Pallas kernels: 48.3 us -> 91.3 us
  local copies, waits for them, and re-layouts: 50.1 us -> 15.3 us
  starting transfers between devices: 144 us -> 112 us
  waiting for transfers between devices: 151 us -> 136 us
  other arithmetic: 34.2 us -> 28.9 us
    pallas_call x0 -> x13, Pallas kernels: none -> 37.1 us  [the longest x9 23.8 us: whole_call(): pl.pallas_call(kernel, in_specs=[pl.BlockSpec(memory_space=pltpu.SMEM)] +...]
    ppermute x71 -> x67, starting transfers between devices: 144 us -> 112 us  [send(): return lax.ppermute(value, AXES, pairs)]
    ppermute x71 -> x67, waiting for transfers between devices: 151 us -> 136 us  [send(): return lax.ppermute(value, AXES, pairs)]
    reshape x12 -> x0, local copies, waits for them, and re-layouts: 8.77 us -> none  [the longest x2 2.43 us: per_device_clustered(): w_qkv.reshape(rows_d, 3, GROUP, NARROW)]
    slice x12 -> x0, local copies, waits for them, and re-layouts: 7.71 us -> none  [the longest x3 3.96 us: per_device_clustered(): grad_w_gate, grad_w_up = (gate_up_all[0], gate_up_all[1])]
    unnamed x160 -> x114, local copies, waits for them, and re-layouts: 14.7 us -> 9.64 us
    select_n x18 -> x8, other arithmetic: 11.1 us -> 7.63 us  [pick(): return jnp.where(flag, second, first)]
  transfers between devices with their start and end apart: 71 -> 67, of which waited for: 32 -> 29; matrix products, arithmetic and copies ran while one was open for 17% -> 11% of each run, Pallas kernels for 7% -> 15%
where the time goes in v2:
time: 429 us; the launch traced here: 422 us
  waiting for transfers between devices  136 us (32%)
  starting transfers between devices  112 us (26%)
  Pallas kernels  91.3 us (21%)
  matrix products  36 us (8%)
  other arithmetic  28.9 us (7%)
  local copies, waits for them, and re-layouts  15.3 us (4%)
    ppermute x67, waiting for transfers between devices, send(): return lax.ppermute(value, AXES, pairs)  136 us
    ppermute x67, starting transfers between devices, send(): return lax.ppermute(value, AXES, pairs)  112 us
    dot_general x23, matrix products, contract(): lax.dot_general(left, right, (((left_dim,), (right_dim,)), ((), ())), pre...  36 us
    pallas_call x1, Pallas kernels, attend_back(): pl.pallas_call(attend_back_kernel, grid_spec=pltpu.PrefetchScalarGridSpec...  28.2 us
    pallas_call x9, Pallas kernels, whole_call(): pl.pallas_call(kernel, in_specs=[pl.BlockSpec(memory_space=pltpu.SMEM)] +...  23.8 us
    pallas_call x1, Pallas kernels, attend(): pl.pallas_call(attend_kernel, grid_spec=pltpu.PrefetchScalarGridSpec(num_...  16.1 us
    unnamed x114, local copies, waits for them, and re-layouts  9.64 us
  transfers between devices with their start and end apart: 67, of which 29 were waited for; matrix products, arithmetic and copies ran while one was open for 11% of the time, Pallas kernels for 15%

profile of v2, /device:TPU:0, one launch (start us, length us, event | category | flops | bytes accessed | tf_op | source)
XLA Modules:
  0.0 421.6 jit_solution(2145441560522397524)
XLA Ops:
  12.4 10.1 %collective-permute-start.7 = (bf16[2,96,580]{2,1,0:T(8,128)(2,1)S(1)}, bf16[2,96,580]{2,1,0:T(8,128)(2,1)S(1)}, u32[]{:S(2)}, u32[]{:S(2)}) collective-permute-start(bf16[2,96,580]{2,1,0:T(8,128)(2,1)S(1)} %pad_maximum_fusion.10), channel_id=1, source_target_pairs={{0,16},{1,17},{2,18},{3,19},{4,20},{5,21},{6,22},{7,23},{8,24},{9,... | collective-permute-start | bytes 668168 | tf_op jit(solution)/shard_map/ppermute | solution.py:412
  35.5 7.7 %collective-permute-done.3 = bf16[256,768]{1,0:T(8,128)(2,1)S(1)} collective-permute-done((bf16[256,768]{1,0:T(8,128)(2,1)S(1)}, bf16[256,768]{1,0:T(8,128)(2,1)S(1)}, u32[]{:S(2)}, u32[]{:S(2)}) %collective-permute-start.3) | collective-permute-done | bytes 393248 | tf_op jit(solution)/shard_map/ppermute | solution.py:412
  47.7 5.4 %project.1 = (bf16[1024,256]{1,0:T(8,128)(2,1)}, bf16[1024,512]{1,0:T(8,128)(2,1)}) custom-call(bf16[1024,768]{1,0:T(8,128)(2,1)} %pad_maximum_fusion.1.x_ref, bf16[768,768]{1,0:T(8,128)(2,1)} %bitcast.86, f32[1024,128]{1,0:T(8,128)} %get-tuple-element.257.cos_ref, f32[1024,128]{1,0:T(8,128)} %get-tuple-element.256.sin_ref), custom_call_target="tpu_custom_call" | custom-call | flops 1207959552 | bytes 5373952 | tf_op jit(solution)/shard_map/project/pallas_call | solution.py:453
  61.7 6.0 %collective-permute-start.11 = (bf16[96,768]{1,0:T(8,128)(2,1)S(1)}, bf16[96,768]{1,0:T(8,128)(2,1)}, u32[]{:S(2)}, u32[]{:S(2)}) collective-permute-start(bf16[96,768]{1,0:T(8,128)(2,1)S(1)} %constant_dynamic-slice_fusion.1), channel_id=1, source_target_pairs={{0,4},{1,5},{2,6},{3,7},{4,0},{5,1},{6,2},{7,3},{8,12},{9,13},{10,... | collective-permute-start | bytes 442376 | tf_op jit(solution)/shard_map/ppermute | solution.py:412
  71.9 16.1 %attend.1 = (bf16[1024,256]{1,0:T(8,128)(2,1)}, f32[8,1024]{1,0:T(8,128)}) custom-call(s32[2048]{0:T(1024)} %bitcast.103, s32[8,1,256]{2,1,0:T(1,128)} %reshape.184.row_ids_ref, s32[2048,1]{1,0:T(8,128)} %bitcast.92, bf16[1024,256]{1,0:T(8,128)(2,1)} %get-tuple-element.122.q_ref, bf16[1024,512]{1,0:T(8,128)(2,1)} %get-tuple-element.123.own_ref, ...), custom_call_target="tpu_custom_call" | custom-call | flops 6442450944 | bytes 3145728 | tf_op jit(solution)/shard_map/attend/pallas_call | solution.py:565
  88.1 4.9 %collective-permute-start.14 = (bf16[96,768]{1,0:T(8,128)(2,1)S(1)}, bf16[96,768]{1,0:T(8,128)(2,1)S(1)}, u32[]{:S(2)}, u32[]{:S(2)}) collective-permute-start(bf16[96,768]{1,0:T(8,128)(2,1)S(1)} %collective-permute-done.10), channel_id=1, source_target_pairs={{0,8},{1,9},{2,10},{3,11},{4,12},{5,13},{6,14},{7,15},{8,0},{9,1},... | collective-permute-start | bytes 442376 | tf_op jit(solution)/shard_map/ppermute | solution.py:412
  103.7 6.9 %collective-permute-done.17 = bf16[256,768]{1,0:T(8,128)(2,1)} collective-permute-done((bf16[256,768]{1,0:T(8,128)(2,1)}, bf16[256,768]{1,0:T(8,128)(2,1)}, u32[]{:S(2)}, u32[]{:S(2)}) %collective-permute-start.17) | collective-permute-done | bytes 393248 | tf_op jit(solution)/shard_map/ppermute | solution.py:412
  110.6 5.9 %collective-permute-done.16 = bf16[256,768]{1,0:T(8,128)(2,1)} collective-permute-done((bf16[256,768]{1,0:T(8,128)(2,1)}, bf16[256,768]{1,0:T(8,128)(2,1)}, u32[]{:S(2)}, u32[]{:S(2)}) %collective-permute-start.16) | collective-permute-done | bytes 393248 | tf_op jit(solution)/shard_map/ppermute | solution.py:412
  132.0 3.4 collective-permute-done.20
  136.8 8.2 %collective-permute-done.22 = bf16[256,768]{1,0:T(8,128)(2,1)S(1)} collective-permute-done((bf16[256,768]{1,0:T(8,128)(2,1)}, bf16[256,768]{1,0:T(8,128)(2,1)S(1)}, u32[]{:S(2)}, u32[]{:S(2)}) %collective-permute-start.22) | collective-permute-done | bytes 393248 | tf_op jit(solution)/shard_map/ppermute | solution.py:412
  145.0 6.7 %unpack.1 = bf16[8,96,1536]{2,1,0:T(8,128)(2,1)} custom-call(s32[8]{0:T(128)} %pad_add_fusion.2.place_ref, bf16[4,96,1536]{2,1,0:T(8,128)(2,1)} %copy-done.2, bf16[4,96,1536]{2,1,0:T(8,128)(2,1)} %collective-permute-done.23.far_ref), custom_call_target="tpu_custom_call" | custom-call | tf_op jit(solution)/shard_map/unpack/pallas_call | solution.py:861
  151.7 4.3 %fusion.61 = f32[1024,1536]{1,0:T(8,128)S(1)} fusion(bf16[1024,768]{1,0:T(8,128)(2,1)S(1)} %constant_dynamic-update-slice_fusion.2, bf16[768,1536]{1,0:T(8,128)(2,1)} %bitcast.77), kind=kOutput, calls=%fused_computation.172 | convolution fusion | flops 2415919104 | bytes 10223616 | tf_op jit(solution)/shard_map/dot_general | solution.py:489
  163.1 12.8 %collective-permute-done.27 = bf16[256,768]{1,0:T(8,128)(2,1)S(1)} collective-permute-done((bf16[256,768]{1,0:T(8,128)(2,1)S(1)}, bf16[256,768]{1,0:T(8,128)(2,1)S(1)}, u32[]{:S(2)}, u32[]{:S(2)}) %collective-permute-start.27) | collective-permute-done | bytes 393248 | tf_op jit(solution)/shard_map/ppermute | solution.py:412
  175.9 5.6 %collective-permute-done.26 = bf16[256,768]{1,0:T(8,128)(2,1)S(1)} collective-permute-done((bf16[256,768]{1,0:T(8,128)(2,1)S(1)}, bf16[256,768]{1,0:T(8,128)(2,1)S(1)}, u32[]{:S(2)}, u32[]{:S(2)}) %collective-permute-start.26) | collective-permute-done | bytes 393248 | tf_op jit(solution)/shard_map/ppermute | solution.py:412
  188.1 9.4 %collective-permute-done.31 = bf16[256,768]{1,0:T(8,128)(2,1)S(1)} collective-permute-done((bf16[256,768]{1,0:T(8,128)(2,1)S(1)}, bf16[256,768]{1,0:T(8,128)(2,1)S(1)}, u32[]{:S(2)}, u32[]{:S(2)}) %collective-permute-start.31) | collective-permute-done | bytes 393248 | tf_op jit(solution)/shard_map/ppermute | solution.py:412
  197.5 5.7 %collective-permute-done.30 = bf16[256,768]{1,0:T(8,128)(2,1)S(1)} collective-permute-done((bf16[256,768]{1,0:T(8,128)(2,1)S(1)}, bf16[256,768]{1,0:T(8,128)(2,1)S(1)}, u32[]{:S(2)}, u32[]{:S(2)}) %collective-permute-start.30) | collective-permute-done | bytes 393248 | tf_op jit(solution)/shard_map/ppermute | solution.py:412
  221.2 7.4 %collective-permute-done.33 = bf16[256,768]{1,0:T(8,128)(2,1)S(1)} collective-permute-done((bf16[256,768]{1,0:T(8,128)(2,1)S(1)}, bf16[256,768]{1,0:T(8,128)(2,1)S(1)}, u32[]{:S(2)}, u32[]{:S(2)}) %collective-permute-start.33) | collective-permute-done | bytes 393248 | tf_op jit(solution)/shard_map/ppermute | solution.py:412
  230.8 4.0 split_feed.1
  239.4 9.4 %collective-permute-done.39 = bf16[256,768]{1,0:T(8,128)(2,1)S(1)} collective-permute-done((bf16[256,768]{1,0:T(8,128)(2,1)S(1)}, bf16[256,768]{1,0:T(8,128)(2,1)S(1)}, u32[]{:S(2)}, u32[]{:S(2)}) %collective-permute-start.39) | collective-permute-done | bytes 393248 | tf_op jit(solution)/shard_map/ppermute | solution.py:412
  248.8 7.4 %collective-permute-done.38 = bf16[256,768]{1,0:T(8,128)(2,1)S(1)} collective-permute-done((bf16[256,768]{1,0:T(8,128)(2,1)S(1)}, bf16[256,768]{1,0:T(8,128)(2,1)S(1)}, u32[]{:S(2)}, u32[]{:S(2)}) %collective-permute-start.38) | collective-permute-done | bytes 393248 | tf_op jit(solution)/shard_map/ppermute | solution.py:412
  262.8 28.2 %attend_back.1 = (bf16[1024,256]{1,0:T(8,128)(2,1)}, f32[1024,512]{1,0:T(8,128)}, bf16[1024,512]{1,0:T(8,128)(2,1)}) custom-call(s32[2048]{0:T(1024)} %bitcast.104, s32[8,1,256]{2,1,0:T(1,128)} %reshape.184.row_ids_ref, s32[2048,1]{1,0:T(8,128)} %bitcast.93, bf16[1024,256]{1,0:T(8,128)(2,1)} %get-tuple-element.122.q_ref, ...), custom_call_target="tpu_custom_call" | custom-call | flops 16106127360 | bytes 3145728 | tf_op jit(solution)/shard_map/attend_back/pallas_call | solution.py:689
  298.4 4.6 %join_grads.1 = bf16[1024,768]{1,0:T(8,128)(2,1)} custom-call(bf16[1024,256]{1,0:T(8,128)(2,1)} %get-tuple-element.168.dq_ref, f32[1024,512]{1,0:T(8,128)} %get-tuple-element.169.own_ref, bf16[1024,512]{1,0:T(8,128)(2,1)} %copy-done.11, f32[1024,128]{1,0:T(8,128)} %get-tuple-element.257.cos_ref, f32[1024,128]{1,0:T(8,128)} %get-tuple-element.256.sin_ref), custom_call_target="tpu_custom_call" | custom-call | flops 4194304 | bytes 5767168 | tf_op jit(solution)/shard_map/join_grads/pallas_call | solution.py:743
  321.9 3.4 collective-permute-start.50
  327.2 10.5 %collective-permute-done.50.refs_0_ = bf16[2,48,768]{2,1,0:T(8,128)(2,1)S(1)} collective-permute-done((bf16[2,48,768]{2,1,0:T(8,128)(2,1)}, bf16[2,48,768]{2,1,0:T(8,128)(2,1)S(1)}, u32[]{:S(2)}, u32[]{:S(2)}) %collective-permute-start.50) | collective-permute-done | bytes 147488 | tf_op jit(solution)/shard_map/ppermute | solution.py:412
  346.0 3.7 collective-permute-start.53
  354.9 3.9 collective-permute-start.57
  363.5 3.6 collective-permute-start.56
  367.1 10.5 %collective-permute-done.56 = bf16[96,768]{1,0:T(8,128)(2,1)S(1)} collective-permute-done((bf16[96,768]{1,0:T(8,128)(2,1)S(1)}, bf16[96,768]{1,0:T(8,128)(2,1)S(1)}, u32[]{:S(2)}, u32[]{:S(2)}) %collective-permute-start.56) | collective-permute-done | bytes 147488 | tf_op jit(solution)/shard_map/ppermute | solution.py:412
  381.7 3.4 collective-permute-start.60
  387.0 3.9 collective-permute-start.62
  402.6 3.6 collective-permute-done.63.other_ref
  411.1 4.0 finish_feed.1
  (330 shorter events, 189.0 us)
Async XLA Ops:
  12.4 16.4 %collective-permute-start.7 = (bf16[2,96,580]{2,1,0:T(8,128)(2,1)S(1)}, bf16[2,96,580]{2,1,0:T(8,128)(2,1)S(1)}, u32[]{:S(2)}, u32[]{:S(2)}) collective-permute-start(bf16[2,96,580]{2,1,0:T(8,128)(2,1)S(1)} %pad_maximum_fusion.10), channel_id=1, source_target_pairs={{0,16},{1,17},{2,18},{3,19},{4,20},{5,21},{6,22},{7,23},{8,24},{9,... | collective-permute-start | bytes 668168 | tf_op jit(solution)/shard_map/ppermute | solution.py:412
  22.5 20.6 %collective-permute-start.3 = (bf16[256,768]{1,0:T(8,128)(2,1)S(1)}, bf16[256,768]{1,0:T(8,128)(2,1)S(1)}, u32[]{:S(2)}, u32[]{:S(2)}) collective-permute-start(bf16[256,768]{1,0:T(8,128)(2,1)S(1)} %collective-permute-done.1), channel_id=1, source_target_pairs={{0,2},{1,3},{2,0},{3,1},{4,6},{5,7},{6,4},{7,5},{8,10},{9,11},{10,... | collective-permute-start | bytes 1179656 | tf_op jit(solution)/shard_map/ppermute | solution.py:412
  24.8 18.4 %collective-permute-start.2 = (bf16[256,768]{1,0:T(8,128)(2,1)S(1)}, bf16[256,768]{1,0:T(8,128)(2,1)S(1)}, u32[]{:S(2)}, u32[]{:S(2)}) collective-permute-start(bf16[256,768]{1,0:T(8,128)(2,1)S(1)} %collective-permute-done.1), channel_id=1, source_target_pairs={{0,1},{1,0},{2,3},{3,2},{4,5},{5,4},{6,7},{7,6},{8,9},{9,8},{10,11... | collective-permute-start | bytes 1179656 | tf_op jit(solution)/shard_map/ppermute | solution.py:412
  61.0 27.0 %collective-permute-start.10 = (bf16[96,768]{1,0:T(8,128)(2,1)S(1)}, bf16[96,768]{1,0:T(8,128)(2,1)S(1)}, u32[]{:S(2)}, u32[]{:S(2)}) collective-permute-start(bf16[96,768]{1,0:T(8,128)(2,1)S(1)} %copy-done.46), channel_id=1, source_target_pairs={{0,0},{1,8},{2,1},{3,9},{4,2},{5,10},{6,3},{7,11},{8,4},{9,12},{10... | collective-permute-start | bytes 442376 | tf_op jit(solution)/shard_map/ppermute | solution.py:412
  61.7 26.4 %collective-permute-start.11 = (bf16[96,768]{1,0:T(8,128)(2,1)S(1)}, bf16[96,768]{1,0:T(8,128)(2,1)}, u32[]{:S(2)}, u32[]{:S(2)}) collective-permute-start(bf16[96,768]{1,0:T(8,128)(2,1)S(1)} %constant_dynamic-slice_fusion.1), channel_id=1, source_target_pairs={{0,4},{1,5},{2,6},{3,7},{4,0},{5,1},{6,2},{7,3},{8,12},{9,13},{10,... | collective-permute-start | bytes 442376 | tf_op jit(solution)/shard_map/ppermute | solution.py:412
  67.7 20.4 %collective-permute-start.12 = (bf16[96,1536]{1,0:T(8,128)(2,1)}, bf16[96,1536]{1,0:T(8,128)(2,1)S(1)}, u32[]{:S(2)}, u32[]{:S(2)}) collective-permute-start(bf16[96,1536]{1,0:T(8,128)(2,1)} %get-tuple-element.132), channel_id=1, source_target_pairs={{0,0},{1,1},{2,2},{3,3},{4,4},{5,5},{6,6},{7,7},{8,12},{9,13},{10,... | collective-permute-start | bytes 884744 | tf_op jit(solution)/shard_map/ppermute | solution.py:412
  69.5 18.6 %collective-permute-start.13 = (bf16[96,1536]{1,0:T(8,128)(2,1)}, bf16[96,1536]{1,0:T(8,128)(2,1)S(1)}, u32[]{:S(2)}, u32[]{:S(2)}) collective-permute-start(bf16[96,1536]{1,0:T(8,128)(2,1)} %get-tuple-element.133), channel_id=1, source_target_pairs={{0,1},{1,0},{2,3},{3,2},{4,5},{5,4},{6,7},{7,6},{8,13},{9,12},{10,... | collective-permute-start | bytes 884744 | tf_op jit(solution)/shard_map/ppermute | solution.py:412
  97.3 19.1 %collective-permute-start.16 = (bf16[256,768]{1,0:T(8,128)(2,1)}, bf16[256,768]{1,0:T(8,128)(2,1)}, u32[]{:S(2)}, u32[]{:S(2)}) collective-permute-start(bf16[256,768]{1,0:T(8,128)(2,1)} %convolution_convert_fusion.11), channel_id=1, source_target_pairs={{0,2},{1,3},{2,0},{3,1},{4,6},{5,7},{6,4},{7,5},{8,10},{9,11},{10,... | collective-permute-start | bytes 1179656 | tf_op jit(solution)/shard_map/ppermute | solution.py:412
  98.3 20.1 %collective-permute-start.15 = (bf16[256,768]{1,0:T(8,128)(2,1)}, bf16[256,768]{1,0:T(8,128)(2,1)}, u32[]{:S(2)}, u32[]{:S(2)}) collective-permute-start(bf16[256,768]{1,0:T(8,128)(2,1)} %convolution_convert_fusion.12), channel_id=1, source_target_pairs={{0,1},{1,0},{2,3},{3,2},{4,5},{5,4},{6,7},{7,6},{8,9},{9,8},{10,11... | collective-permute-start | bytes 1179656 | tf_op jit(solution)/shard_map/ppermute | solution.py:412
  101.6 19.9 %collective-permute-start.18 = (bf16[2,96,1536]{2,1,0:T(8,128)(2,1)S(1)}, bf16[2,96,1536]{2,1,0:T(8,128)(2,1)S(1)}, u32[]{:S(2)}, u32[]{:S(2)}) collective-permute-start(bf16[2,96,1536]{2,1,0:T(8,128)(2,1)S(1)} %pad_maximum_fusion.5), channel_id=1, source_target_pairs={{0,16},{1,17},{2,18},{3,19},{4,20},{5,21},{6,22},{7,23},{8,24},{9,... | collective-permute-start | bytes 1769480 | tf_op jit(solution)/shard_map/ppermute | solution.py:412
  101.6 19.9 %collective-permute-start.19 = (bf16[96,768]{1,0:T(8,128)(2,1)}, bf16[96,768]{1,0:T(8,128)(2,1)S(1)}, u32[]{:S(2)}, u32[]{:S(2)}) collective-permute-start(bf16[96,768]{1,0:T(8,128)(2,1)} %collective-permute-done.11), channel_id=1, source_target_pairs={{0,16},{1,17},{2,18},{3,19},{4,20},{5,21},{6,22},{7,23},{8,24},{9,... | collective-permute-start | bytes 442376 | tf_op jit(solution)/shard_map/ppermute | solution.py:412
  121.6 23.4 %collective-permute-start.23 = (bf16[4,96,1536]{2,1,0:T(8,128)(2,1)S(1)}, bf16[4,96,1536]{2,1,0:T(8,128)(2,1)}, u32[]{:S(2)}, u32[]{:S(2)}) collective-permute-start(bf16[4,96,1536]{2,1,0:T(8,128)(2,1)S(1)} %constant_dynamic-update-slice_fusion.6.near_ref), channel_id=1, source_target_pairs={{0,8},{1,9},{2,10},{3,11},{4,12},{5,13},{6,14},{7,15},{8,0},{9,1},... | collective-permute-start | bytes 3538952 | tf_op jit(solution)/shard_map/ppermute | solution.py:412
  124.8 20.2 %collective-permute-start.22 = (bf16[256,768]{1,0:T(8,128)(2,1)}, bf16[256,768]{1,0:T(8,128)(2,1)S(1)}, u32[]{:S(2)}, u32[]{:S(2)}) collective-permute-start(bf16[256,768]{1,0:T(8,128)(2,1)} %fusion.21), channel_id=1, source_target_pairs={{0,3},{1,2},{2,1},{3,0},{4,7},{5,6},{6,5},{7,4},{8,11},{9,10},{10,... | collective-permute-start | bytes 1179656 | tf_op jit(solution)/shard_map/ppermute | solution.py:412
  158.7 17.3 %collective-permute-start.27 = (bf16[256,768]{1,0:T(8,128)(2,1)S(1)}, bf16[256,768]{1,0:T(8,128)(2,1)S(1)}, u32[]{:S(2)}, u32[]{:S(2)}) collective-permute-start(bf16[256,768]{1,0:T(8,128)(2,1)S(1)} %convolution_convert_fusion.7), channel_id=1, source_target_pairs={{0,3},{1,2},{2,1},{3,0},{4,7},{5,6},{6,5},{7,4},{8,11},{9,10},{10,... | collective-permute-start | bytes 1179656 | tf_op jit(solution)/shard_map/ppermute | solution.py:412
  159.1 22.4 %collective-permute-start.26 = (bf16[256,768]{1,0:T(8,128)(2,1)S(1)}, bf16[256,768]{1,0:T(8,128)(2,1)S(1)}, u32[]{:S(2)}, u32[]{:S(2)}) collective-permute-start(bf16[256,768]{1,0:T(8,128)(2,1)S(1)} %convolution_convert_fusion.8), channel_id=1, source_target_pairs={{0,2},{1,3},{2,0},{3,1},{4,6},{5,7},{6,4},{7,5},{8,10},{9,11},{10,... | collective-permute-start | bytes 1179656 | tf_op jit(solution)/shard_map/ppermute | solution.py:412
  160.8 20.7 %collective-permute-start.25 = (bf16[256,768]{1,0:T(8,128)(2,1)S(1)}, bf16[256,768]{1,0:T(8,128)(2,1)S(1)}, u32[]{:S(2)}, u32[]{:S(2)}) collective-permute-start(bf16[256,768]{1,0:T(8,128)(2,1)S(1)} %convolution_convert_fusion.9), channel_id=1, source_target_pairs={{0,1},{1,0},{2,3},{3,2},{4,5},{5,4},{6,7},{7,6},{8,9},{9,8},{10,11... | collective-permute-start | bytes 1179656 | tf_op jit(solution)/shard_map/ppermute | solution.py:412
  162.2 20.3 %collective-permute-start.28 = (bf16[256,768]{1,0:T(8,128)(2,1)S(1)}, bf16[256,768]{1,0:T(8,128)(2,1)S(1)}, u32[]{:S(2)}, u32[]{:S(2)}) collective-permute-start(bf16[256,768]{1,0:T(8,128)(2,1)S(1)} %bitcast.116), channel_id=1, source_target_pairs={{0,0},{1,1},{2,2},{3,3},{4,8},{5,9},{6,10},{7,11},{8,4},{9,5},{10,... | collective-permute-start | bytes 1179656 | tf_op jit(solution)/shard_map/ppermute | solution.py:412
  185.1 18.2 %collective-permute-start.30 = (bf16[256,768]{1,0:T(8,128)(2,1)S(1)}, bf16[256,768]{1,0:T(8,128)(2,1)S(1)}, u32[]{:S(2)}, u32[]{:S(2)}) collective-permute-start(bf16[256,768]{1,0:T(8,128)(2,1)S(1)} %get-tuple-element.240), channel_id=1, source_target_pairs={{0,2},{1,3},{2,0},{3,1},{4,6},{5,7},{6,4},{7,5},{8,10},{9,11},{10,... | collective-permute-start | bytes 1179656 | tf_op jit(solution)/shard_map/ppermute | solution.py:412
  209.9 18.7 %collective-permute-start.33 = (bf16[256,768]{1,0:T(8,128)(2,1)S(1)}, bf16[256,768]{1,0:T(8,128)(2,1)S(1)}, u32[]{:S(2)}, u32[]{:S(2)}) collective-permute-start(bf16[256,768]{1,0:T(8,128)(2,1)S(1)} %convolution_convert_fusion.5), channel_id=1, source_target_pairs={{0,2},{1,3},{2,0},{3,1},{4,6},{5,7},{6,4},{7,5},{8,10},{9,11},{10,... | collective-permute-start | bytes 1179656 | tf_op jit(solution)/shard_map/ppermute | solution.py:412
  211.1 17.5 %collective-permute-start.32 = (bf16[256,768]{1,0:T(8,128)(2,1)S(1)}, bf16[256,768]{1,0:T(8,128)(2,1)S(1)}, u32[]{:S(2)}, u32[]{:S(2)}) collective-permute-start(bf16[256,768]{1,0:T(8,128)(2,1)S(1)} %convolution_convert_fusion.6), channel_id=1, source_target_pairs={{0,1},{1,0},{2,3},{3,2},{4,5},{5,4},{6,7},{7,6},{8,9},{9,8},{10,11... | collective-permute-start | bytes 1179656 | tf_op jit(solution)/shard_map/ppermute | solution.py:412
  237.5 18.7 %collective-permute-start.38 = (bf16[256,768]{1,0:T(8,128)(2,1)S(1)}, bf16[256,768]{1,0:T(8,128)(2,1)S(1)}, u32[]{:S(2)}, u32[]{:S(2)}) collective-permute-start(bf16[256,768]{1,0:T(8,128)(2,1)S(1)} %get-tuple-element.231), channel_id=1, source_target_pairs={{0,2},{1,3},{2,0},{3,1},{4,6},{5,7},{6,4},{7,5},{8,10},{9,11},{10,... | collective-permute-start | bytes 1179656 | tf_op jit(solution)/shard_map/ppermute | solution.py:412
  238.8 17.5 %collective-permute-start.37 = (bf16[256,768]{1,0:T(8,128)(2,1)S(1)}, bf16[256,768]{1,0:T(8,128)(2,1)S(1)}, u32[]{:S(2)}, u32[]{:S(2)}) collective-permute-start(bf16[256,768]{1,0:T(8,128)(2,1)S(1)} %get-tuple-element.231), channel_id=1, source_target_pairs={{0,1},{1,0},{2,3},{3,2},{4,5},{5,4},{6,7},{7,6},{8,9},{9,8},{10,11... | collective-permute-start | bytes 1179656 | tf_op jit(solution)/shard_map/ppermute | solution.py:412
  239.4 20.6 %collective-permute-start.40 = (bf16[12,48,768]{2,1,0:T(8,128)(2,1)S(1)}, bf16[12,48,768]{2,1,0:T(8,128)(2,1)S(1)}, u32[]{:S(2)}, u32[]{:S(2)}) collective-permute-start(bf16[12,48,768]{2,1,0:T(8,128)(2,1)S(1)} %copy-done.44), channel_id=1, source_target_pairs={{0,16},{1,17},{2,18},{3,19},{4,20},{5,21},{6,22},{7,23},{8,24},{9,... | collective-permute-start | bytes 2654216 | tf_op jit(solution)/shard_map/ppermute | solution.py:412
  260.3 30.7 %collective-permute-start.42 = (bf16[12,48,768]{2,1,0:T(8,128)(2,1)S(1)}, bf16[12,48,768]{2,1,0:T(8,128)(2,1)S(1)}, u32[]{:S(2)}, u32[]{:S(2)}) collective-permute-start(bf16[12,48,768]{2,1,0:T(8,128)(2,1)S(1)} %add.218.mine_ref), channel_id=1, source_target_pairs={{4,0},{5,1},{6,2},{7,3},{8,12},{9,13},{10,14},{11,15},{20,16},{21,... | collective-permute-start | bytes 2654216 | tf_op jit(solution)/shard_map/ppermute | solution.py:412
  261.7 29.2 %collective-permute-start.43 = (bf16[96,768]{1,0:T(8,128)(2,1)S(1)}, bf16[96,768]{1,0:T(8,128)(2,1)}, u32[]{:S(2)}, u32[]{:S(2)}) collective-permute-start(bf16[96,768]{1,0:T(8,128)(2,1)S(1)} %add_convert_fusion.3), channel_id=1, source_target_pairs={{0,16},{1,17},{2,18},{3,19},{4,20},{5,21},{6,22},{7,23},{8,24},{9,... | collective-permute-start | bytes 442376 | tf_op jit(solution)/shard_map/ppermute | solution.py:412
  262.1 28.9 %collective-permute-start.44 = (bf16[256,768]{1,0:T(8,128)(2,1)S(1)}, bf16[256,768]{1,0:T(8,128)(2,1)S(1)}, u32[]{:S(2)}, u32[]{:S(2)}) collective-permute-start(bf16[256,768]{1,0:T(8,128)(2,1)S(1)} %copy-done.24), channel_id=1, source_target_pairs={{0,0},{1,1},{2,2},{3,3},{4,8},{5,9},{6,10},{7,11},{8,4},{9,5},{10,... | collective-permute-start | bytes 1179656 | tf_op jit(solution)/shard_map/ppermute | solution.py:412
  315.5 34.2 %collective-permute-start.48 = (bf16[256,768]{1,0:T(8,128)(2,1)}, bf16[256,768]{1,0:T(8,128)(2,1)}, u32[]{:S(2)}, u32[]{:S(2)}) collective-permute-start(bf16[256,768]{1,0:T(8,128)(2,1)} %convolution_convert_fusion.1), channel_id=1, source_target_pairs={{0,3},{1,2},{2,1},{3,0},{4,7},{5,6},{6,5},{7,4},{8,11},{9,10},{10,... | collective-permute-start | bytes 1179656 | tf_op jit(solution)/shard_map/ppermute | solution.py:412
  315.5 34.2 %collective-permute-start.47 = (bf16[256,768]{1,0:T(8,128)(2,1)}, bf16[256,768]{1,0:T(8,128)(2,1)}, u32[]{:S(2)}, u32[]{:S(2)}) collective-permute-start(bf16[256,768]{1,0:T(8,128)(2,1)} %convolution_convert_fusion.2), channel_id=1, source_target_pairs={{0,2},{1,3},{2,0},{3,1},{4,6},{5,7},{6,4},{7,5},{8,10},{9,11},{10,... | collective-permute-start | bytes 1179656 | tf_op jit(solution)/shard_map/ppermute | solution.py:412
  318.4 31.3 %collective-permute-start.46 = (bf16[256,768]{1,0:T(8,128)(2,1)}, bf16[256,768]{1,0:T(8,128)(2,1)}, u32[]{:S(2)}, u32[]{:S(2)}) collective-permute-start(bf16[256,768]{1,0:T(8,128)(2,1)} %convolution_convert_fusion.3), channel_id=1, source_target_pairs={{0,1},{1,0},{2,3},{3,2},{4,5},{5,4},{6,7},{7,6},{8,9},{9,8},{10,11... | collective-permute-start | bytes 1179656 | tf_op jit(solution)/shard_map/ppermute | solution.py:412
  325.3 18.0 %collective-permute-start.51 = (bf16[2,48,768]{2,1,0:T(8,128)(2,1)}, bf16[2,48,768]{2,1,0:T(8,128)(2,1)S(1)}, u32[]{:S(2)}, u32[]{:S(2)}) collective-permute-start(bf16[2,48,768]{2,1,0:T(8,128)(2,1)} %get-tuple-element.187), channel_id=1, source_target_pairs={{0,2},{1,3},{2,0},{3,1},{12,14},{13,15},{14,12},{15,13},{16,18},{1... | collective-permute-start | bytes 442376 | tf_op jit(solution)/shard_map/ppermute | solution.py:412
  354.9 22.7 %collective-permute-start.57 = (bf16[12,48,768]{2,1,0:T(8,128)(2,1)}, bf16[12,48,768]{2,1,0:T(8,128)(2,1)S(1)}, u32[]{:S(2)}, u32[]{:S(2)}) collective-permute-start(bf16[12,48,768]{2,1,0:T(8,128)(2,1)} %join_feed.1.own_ref), channel_id=1, source_target_pairs={{0,16},{1,17},{2,18},{3,19},{12,28},{13,29},{14,30},{15,31},{16,0}... | collective-permute-start | bytes 2654216 | tf_op jit(solution)/shard_map/ppermute | solution.py:412
  358.8 19.5 %collective-permute-start.58 = (bf16[12,48,768]{2,1,0:T(8,128)(2,1)}, bf16[12,48,768]{2,1,0:T(8,128)(2,1)S(1)}, u32[]{:S(2)}, u32[]{:S(2)}) collective-permute-start(bf16[12,48,768]{2,1,0:T(8,128)(2,1)} %join_feed.1.own_ref), channel_id=1, source_target_pairs={{0,8},{1,9},{2,10},{3,11},{12,4},{13,5},{14,6},{15,7},{16,24},{17,... | collective-permute-start | bytes 2654216 | tf_op jit(solution)/shard_map/ppermute | solution.py:412
  (87 other events, 961.0 us)

commit v3 on v2

--- a/solution.py
+++ b/solution.py
@@ -371,6 +371,7 @@
 OWN_HEADS = 3
 NARROW = OWN_HEADS * HEAD_DIM
 WIDE = 256
+LANES = 128
 LOG2E = 1.4426950408889634
 SCORE_FACTOR = HEAD_DIM ** (-0.5) * LOG2E
 MASKED = -1e30
@@ -616,8 +617,15 @@
 
     queries = q_ref[...]
     upstream = up_ref[...]
-    q_heads = [head_only(queries, head) for head in range(OWN_HEADS)]
-    up_heads = [head_only(upstream, head) for head in range(OWN_HEADS)]
+    sides = (slice(0, LANES), slice(LANES, WIDE))
+    members = ((0, 1), (2,))
+    split = lambda values: [
+        [head_only(values[:, side], head % 2) for head in inside]
+        for side, inside in zip(sides, members)
+    ]
+    q_heads, up_heads = split(queries), split(upstream)
+    q_stacks = [jnp.concatenate(parts, axis=0) for parts in q_heads]
+    up_stacks = [jnp.concatenate(parts, axis=0) for parts in up_heads]
     products = upstream.astype(F32) * out_ref[...].astype(F32)
     lane_head = lax.broadcasted_iota(jnp.int32, (8, WIDE), 1) // HEAD_DIM
     selector = (lane_head == lax.broadcasted_iota(jnp.int32, (8, WIDE), 0)).astype(F32)
@@ -638,24 +646,31 @@
                 keys = ref[pl.ds(start, TILE), :WIDE]
                 values = ref[pl.ds(start, TILE), WIDE:]
                 same = col_ids_ref[place, :] == q_ids
-                for head in range(OWN_HEADS):
-                    scores = contract(keys, q_heads[head], 1, 1) * SCORE_FACTOR
-                    weights = jnp.where(
-                        same, jnp.exp2(scores - log_ref[head : head + 1, :]), 0.0
+                for side, inside, q_side, up_side, q_stack, up_stack in zip(
+                    sides, members, q_heads, up_heads, q_stacks, up_stacks
+                ):
+                    all_weights, all_grads = [], []
+                    for head, query, grad in zip(inside, q_side, up_side):
+                        scores = contract(keys[:, side], query, 1, 1) * SCORE_FACTOR
+                        weights = jnp.where(
+                            same, jnp.exp2(scores - log_ref[head : head + 1, :]), 0.0
+                        )
+                        grad_weights = contract(values[:, side], grad, 1, 1)
+                        grad_scores = (
+                            weights * (grad_weights - deltas[head : head + 1, :])
+                        ).astype(BF)
+                        all_weights.append(weights.astype(BF))
+                        all_grads.append(grad_scores)
+                        rows = slice(head * HEAD_DIM, (head + 1) * HEAD_DIM)
+                        acc_ref[rows, :] += jnp.dot(
+                            k_turned[base + tile, rows, :], grad_scores,
+                            preferred_element_type=F32,
+                        )
+                    value_acc[place, side] += jnp.dot(
+                        jnp.concatenate(all_weights, axis=1), up_stack, preferred_element_type=F32
                     )
-                    grad_weights = contract(values, up_heads[head], 1, 1)
-                    grad_scores = (
-                        weights * (grad_weights - deltas[head : head + 1, :])
-                    ).astype(BF)
-                    value_acc[place, :] += jnp.dot(
-                        weights.astype(BF), up_heads[head], preferred_element_type=F32
-                    )
-                    key_acc[place, :] += jnp.dot(
-                        grad_scores, q_heads[head], preferred_element_type=F32
-                    )
-                    rows = slice(head * HEAD_DIM, (head + 1) * HEAD_DIM)
-                    acc_ref[rows, :] += jnp.dot(
-                        k_turned[base + tile, rows, :], grad_scores, preferred_element_type=F32
+                    key_acc[place, side] += jnp.dot(
+                        jnp.concatenate(all_grads, axis=1), q_stack, preferred_element_type=F32
                     )
 
             return carry
@@ -852,23 +867,20 @@
 
 
 def unpack_kernel(place_ref, near_ref, far_ref, out_ref):
-    first = pl.program_id(0) < GROUP
-    out_ref[...] = jnp.where(first, near_ref[...], far_ref[...])
+    for index in range(2 * GROUP):
+        out_ref[place_ref[index]] = (near_ref, far_ref)[index // GROUP][index % GROUP]
 
 
 def unpack(places, near, far):
     count, rows, width = near.shape
     return pl.pallas_call(
         unpack_kernel,
-        grid_spec=pltpu.PrefetchScalarGridSpec(
-            num_scalar_prefetch=1,
-            grid=(2 * count,),
-            in_specs=[
-                pl.BlockSpec((1, rows, width), lambda i, p: (jnp.minimum(i, count - 1), 0, 0)),
-                pl.BlockSpec((1, rows, width), lambda i, p: (jnp.maximum(i - count, 0), 0, 0)),
-            ],
-            out_specs=pl.BlockSpec((1, rows, width), lambda i, p: (p[i], 0, 0)),
-        ),
+        in_specs=[
+            pl.BlockSpec(memory_space=pltpu.SMEM),
+            pl.BlockSpec(memory_space=pltpu.VMEM),
+            pl.BlockSpec(memory_space=pltpu.VMEM),
+        ],
+        out_specs=pl.BlockSpec(memory_space=pltpu.VMEM),
         out_shape=jax.ShapeDtypeStruct((2 * count, rows, width), BF),
         name="unpack",
     )(places, near, far)
@@ -1014,7 +1026,7 @@
     if parts is None:
         parts = square_parts(left, weight, weight_dim)
     got = [send(part, SQUARE[k + 1]) for k, part in enumerate(parts)]
-    total = contract(left[:TILE], weight, 1, weight_dim)
+    (total,) = join(contract(left[:TILE], weight, 1, weight_dim))
     for part in got:
         total = total + part.astype(F32)
     return total
@@ -1056,18 +1068,22 @@
     targets = by_x[:2]
     places = jnp.concatenate([GROUP * (h ^ c) + by_x, GROUP * (1 - (h ^ c)) + by_x])
 
+    out_got = send(w_out, OUT_FETCH)
     vectors = jnp.stack([ln1_gain, ln1_bias, ln2_gain, ln2_bias], axis=1)
     qkv_packed = pack_qkv(targets, w_qkv, vectors)
     qkv_mine = after(
         jnp.stack([send(part, ROUND[i]) for i, part in enumerate(qkv_packed)]), inputs_bf
     )
     x_tiles = gather_square(inputs_bf)
-    qkv_near = jnp.concatenate([qkv_mine, send(qkv_mine, OTHER_X)], axis=0)
+    qkv_second = send(qkv_mine, OTHER_X)
+    qkv_near = jnp.concatenate([qkv_mine, qkv_second], axis=0)
+    qkv_second, w_gate, w_up, down_whole, doc_ids, j = join(
+        qkv_second, w_gate, w_up, w_down, doc_ids, j
+    )
     qkv_far = send(qkv_near, OTHER_CORE)
     qkv_own, vectors_got = unpack_qkv(places, qkv_near, qkv_far)
     qkv_own = qkv_own.reshape(D, 3 * WIDE)
     x_rows = jnp.concatenate(x_tiles, axis=0)
-    x_rows, qkv_own, vectors_got, w_out = join(x_rows, qkv_own, vectors_got, w_out)
 
     tile_index = j ^ jnp.arange(GROUP, dtype=jnp.int32)
     first_row = (c * GROUP + tile_index) * token_count
@@ -1089,19 +1105,25 @@
 
     part_f = rows_f // 4
     gate_up_packed = pack_gate_up(targets, w_gate, w_up)
-    down_sent = lax.dynamic_slice_in_dim(w_down, (2 * c + x) * part_f, part_f, 0)
+    down_sent = lax.dynamic_slice_in_dim(down_whole, (2 * c + x) * part_f, part_f, 0)
+    (
+        x_rows, qkv_own, vectors_got, out_got, flat_ids, row_ids, col_ids, cosine, sine, down_sent,
+        *gate_up_packed,
+    ) = join(
+        x_rows, qkv_own, vectors_got, out_got, flat_ids, row_ids, col_ids, cosine, sine, down_sent,
+        *gate_up_packed,
+    )
 
     queries, kv_own = project(x_rows, qkv_own, cosine, sine)
     kv_other = send(kv_own, OTHER_CORE)
-    kv_other, w_out, down_sent, *gate_up_packed = join(kv_other, w_out, down_sent, *gate_up_packed)
+    out_other = send(out_got, OTHER_CORE)
+    kv_other, out_other, down_sent, *gate_up_packed = join(
+        kv_other, out_other, down_sent, *gate_up_packed
+    )
     attended, logs = attend(flat_ids, row_ids, col_ids, queries, kv_own, kv_other)
-    out_got = send(w_out, OUT_FETCH)
     gate_up_first = [send(part, ROUND[i]) for i, part in enumerate(gate_up_packed)]
     down_mine = send(down_sent, OTHER_HALF)
-    attended, logs, out_got, down_mine, *gate_up_first = join(
-        attended, logs, out_got, down_mine, *gate_up_first
-    )
-    out_other = send(out_got, OTHER_CORE)
+    attended, logs, down_mine, *gate_up_first = join(attended, logs, down_mine, *gate_up_first)
     out_own = jnp.concatenate(
         [
             pick(core_is_one, out_got, out_other),
@@ -1131,6 +1153,7 @@
     gate_up_near = jnp.concatenate([gate_up_mine, gate_up_second], axis=0)
     gate_up_far = send(gate_up_near, OTHER_CORE)
     gate_up_own = unpack(places, gate_up_near, gate_up_far).reshape(D, 2 * slice_f)
+    down_got = after(down_got, first_tiles[1])
     down_pair = jnp.concatenate(
         [pick(x_is_one, down_mine, down_got), pick(x_is_one, down_got, down_mine)], axis=0
     )
@@ -1183,20 +1206,21 @@
         contract(hidden_bf, after(grad_down_rows, *first_parts), 0, 0).reshape(2, rows_f, D)
     )
     bundle_shape = ((3 * GROUP, quarter, D), BF)
+    grad_first = grad_second + reduce_square(grad_acts, gate_up_own, 1, first_parts)
+    grad_gain_one = jnp.sum(grad_first * first_normed, axis=0, keepdims=True)
+    grad_bias_one = jnp.sum(grad_first, axis=0, keepdims=True)
+    grad_res = norm_backward(grad_first, first_normed, first_scale, gain_one)
+    grad_res_bf, down_got, gate_up_got = join(grad_res.astype(BF), down_got, gate_up_got)
+    grad_branch_tiles = gather_square(grad_res_bf)
     feed_keep, feed_away = whole_call(
         split_feed_kernel, "split_feed", [bundle_shape] * 2, x_flag,
         down_keep.reshape(by_x_rows + (D,)), down_got.reshape(by_x_rows + (D,)),
         gate_up_keep.reshape(by_x_rows + (2 * slice_f,)),
         gate_up_got.reshape(by_x_rows + (2 * slice_f,)),
     )
-    grad_first = grad_second + reduce_square(grad_acts, gate_up_own, 1, first_parts)
-    grad_first, feed_away = join(grad_first, feed_away)
     feed_got = send(feed_away, OTHER_X)
-    grad_gain_one = jnp.sum(grad_first * first_normed, axis=0, keepdims=True)
-    grad_bias_one = jnp.sum(grad_first, axis=0, keepdims=True)
-    grad_res = norm_backward(grad_first, first_normed, first_scale, gain_one)
-
-    grad_branch_rows = jnp.concatenate(gather_square(grad_res.astype(BF)), axis=0)
+
+    grad_branch_rows = jnp.concatenate(grad_branch_tiles, axis=0)
     grad_attended = contract(grad_branch_rows, out_own, 1, 1).astype(BF)
     out_keep, out_got = over_cores(
         contract(attended, grad_branch_rows, 0, 0)[:NARROW].reshape(2, rows_d, D)
@@ -1218,10 +1242,17 @@
         grad_queries, kv_grad_own, kv_grad_away, feed_home, out_far, result_home
     )
     kv_grad_got = send(kv_grad_away, OTHER_CORE)
+    feed_kept, *feed_sends = whole_call(
+        square_feed_kernel, "square_feed",
+        [((GROUP + 2, quarter, D), BF)] + [((2, quarter, D), BF)] * 3,
+        step_square, feed_mine, feed_home,
+    )
+    out_total = (out_total.astype(F32) + out_far.astype(F32)).astype(BF)
+    kv_grad_got, out_total, *feed_sends = join(kv_grad_got, out_total, *feed_sends)
+    feed_gots = [send(part, HOME_SQUARE[k + 1]) for k, part in enumerate(feed_sends)]
+    out_got = send(out_total, OTHER_HALF)
     grad_projected = join_grads(grad_queries, kv_grad_own, kv_grad_got, cosine, sine)
 
-    input_parts = square_parts(grad_projected, qkv_own, 1)
-    grad_projected, x_rows, *input_parts = join(grad_projected, x_rows, *input_parts)
     qkv_part = contract(x_rows, grad_projected, 0, 0).reshape(2, D // 2, 3 * WIDE)
     vector_part = jnp.concatenate(
         [grad_gain_one, grad_bias_one, grad_gain_two, grad_bias_two]
@@ -1232,48 +1263,45 @@
         split_cores_kernel, "split_cores", [((D // 2 + 16, 3 * WIDE), BF)], c.reshape(1),
         qkv_part, vector_part,
     )
-    qkv_away, feed_mine, feed_home = join(qkv_away, feed_mine, feed_home)
+    qkv_away, out_got, *feed_gots = join(qkv_away, out_got, *feed_gots)
     qkv_got = send(qkv_away, OTHER_CORE)
-    feed_kept, *feed_sends = whole_call(
-        square_feed_kernel, "square_feed",
-        [((GROUP + 2, quarter, D), BF)] + [((2, quarter, D), BF)] * 3,
-        step_square, feed_mine, feed_home,
-    )
-    qkv_got, *feed_sends = join(qkv_got, *feed_sends)
-    feed_gots = [send(part, HOME_SQUARE[k + 1]) for k, part in enumerate(feed_sends)]
+    (feed_bundle,) = whole_call(
+        join_feed_kernel, "join_feed", [bundle_shape], step_square, feed_kept, *feed_gots
+    )
+    qkv_got, feed_bundle, out_total = join(qkv_got, feed_bundle, out_total + out_got)
     qkv_keep, qkv_away = whole_call(
         split_x_kernel, "split_x", [((moved_rows, 3 * WIDE), BF)] * 2, jnp.stack([c, x]),
         qkv_part, vector_part, qkv_got,
     )
-    qkv_away, *feed_gots = join(qkv_away, *feed_gots)
+    grad_projected, qkv_away = join(grad_projected, qkv_away)
     qkv_got = send(qkv_away, OTHER_X)
-    (feed_bundle,) = whole_call(
-        join_feed_kernel, "join_feed", [bundle_shape], step_square, feed_kept, *feed_gots
-    )
-    grad_inputs = grad_res + reduce_square(grad_projected, qkv_own, 1, input_parts)
-    inputs_back, feed_bundle, qkv_got, out_total, out_far = join(
-        grad_inputs.astype(BF), feed_bundle, qkv_got, out_total, out_far
-    )
-    grad_inputs_home = send(inputs_back, SPREAD)
+    input_parts = square_parts(grad_projected, qkv_own, 1)
+    input_parts = join(*input_parts)
+
+    input_sum = reduce_square(grad_projected, qkv_own, 1, input_parts)
+    qkv_mine = qkv_keep + qkv_got
+    qkv_home = send(qkv_mine, HOME_HALF)
     feed_other = send(feed_bundle, HOME_X)
     feed_far = send(feed_bundle, HOME_CORE)
-    qkv_mine = qkv_keep + qkv_got
-    qkv_home = send(qkv_mine, HOME_HALF)
-    out_total = (out_total.astype(F32) + out_far.astype(F32)).astype(BF)
-    out_got = send(out_total, OTHER_HALF)
-    qkv_home, out_got, feed_other, feed_far = join(qkv_home, out_got, feed_other, feed_far)
+    grad_w_out = send(out_total, OUT_RETURN)
+    inputs_back, qkv_home, feed_other, feed_far, grad_w_out = join(
+        (grad_res + input_sum).astype(BF), qkv_home, feed_other, feed_far, grad_w_out
+    )
+    grad_inputs_home = send(inputs_back, SPREAD)
     feed_far_other = send(feed_other, HOME_CORE)
     qkv_sends = whole_call(
         square_qkv_kernel, "square_qkv", [((quarter + 16, 3 * WIDE), BF)] * GROUP,
         step_square, qkv_mine, qkv_home,
     )
-    qkv_sends, out_total, feed_far_other = join(qkv_sends, out_total + out_got, feed_far_other)
+    feed_far_other, *qkv_sends = join(feed_far_other, *qkv_sends)
     qkv_gots = [qkv_sends[0]] + [send(qkv_sends[k], HOME_SQUARE[k]) for k in range(1, GROUP)]
-    grad_w_out = send(out_total, OUT_RETURN)
     grad_w_down, grad_w_gate, grad_w_up = whole_call(
         finish_feed_kernel, "finish_feed",
         [(by_x_rows + (D,), F32)] + [((2, quarter, w_gate.shape[1]), F32)] * 2,
         home_flags, feed_bundle, feed_other, feed_far, feed_far_other,
+    )
+    grad_inputs_home, grad_w_down, grad_w_gate, grad_w_up, *qkv_gots = join(
+        grad_inputs_home, grad_w_down, grad_w_gate, grad_w_up, *qkv_gots
     )
     (qkv_bundle,) = whole_call(
         join_qkv_kernel, "join_qkv", [((moved_rows, 3 * WIDE), BF)], step_square, *qkv_gots

time: 429 us -> 386 us (0.90)
  waiting for transfers between devices: 136 us -> 110 us
  matrix products: 36 us -> 28.7 us
    ppermute x67, waiting for transfers between devices: 136 us -> 110 us  [send(): return lax.ppermute(value, AXES, pairs)]
    dot_general x23, matrix products: 36 us -> 28.7 us  [contract(): lax.dot_general(left, right, (((left_dim,), (right_dim,)), ((), ())), pre...]
    unnamed x114 -> x96, local copies, waits for them, and re-layouts: 9.64 us -> 7.04 us
  transfers between devices with their start and end apart: 67 -> 67, of which waited for: 29 -> 24; matrix products, arithmetic and copies ran while one was open for 11% -> 10% of each run, Pallas kernels for 15% -> 19%
where the time goes in v3:
time: 386 us; the launch traced here: 383 us
  starting transfers between devices  113 us (29%)
  waiting for transfers between devices  110 us (28%)
  Pallas kernels  89.4 us (23%)
  matrix products  28.7 us (7%)
  other arithmetic  26.5 us (7%)
  local copies, waits for them, and re-layouts  12.6 us (3%)
    ppermute x67, starting transfers between devices, send(): return lax.ppermute(value, AXES, pairs)  113 us
    ppermute x67, waiting for transfers between devices, send(): return lax.ppermute(value, AXES, pairs)  110 us
    pallas_call x1, Pallas kernels, attend_back(): pl.pallas_call(attend_back_kernel, grid_spec=pltpu.PrefetchScalarGridSpec...  29.4 us
    dot_general x23, matrix products, contract(): lax.dot_general(left, right, (((left_dim,), (right_dim,)), ((), ())), pre...  28.7 us
    pallas_call x9, Pallas kernels, whole_call(): pl.pallas_call(kernel, in_specs=[pl.BlockSpec(memory_space=pltpu.SMEM)] +...  24.1 us
    pallas_call x1, Pallas kernels, attend(): pl.pallas_call(attend_kernel, grid_spec=pltpu.PrefetchScalarGridSpec(num_...  16.2 us
  transfers between devices with their start and end apart: 67, of which 24 were waited for; matrix products, arithmetic and copies ran while one was open for 10% of the time, Pallas kernels for 19%

profile of v3, /device:TPU:0, one launch (start us, length us, event | category | flops | bytes accessed | tf_op | source)
XLA Modules:
  0.0 382.5 jit_solution(14217632875493649820)
XLA Ops:
  14.5 3.4 collective-permute-start.6
  19.7 6.7 %collective-permute-start.1 = (bf16[256,768]{1,0:T(8,128)(2,1)S(1)}, bf16[256,768]{1,0:T(8,128)(2,1)S(1)}, u32[]{:S(2)}, u32[]{:S(2)}) collective-permute-start(bf16[256,768]{1,0:T(8,128)(2,1)S(1)} %collective-permute-done), channel_id=1, source_target_pairs={{0,1},{1,0},{2,3},{3,2},{4,5},{5,4},{6,7},{7,6},{8,9},{9,8},{10,11... | collective-permute-start | bytes 1179656 | tf_op jit(solution)/shard_map/ppermute | solution.py:413
  28.0 6.7 %collective-permute-start.7 = (bf16[4,96,580]{2,1,0:T(8,128)(2,1)S(1)}, bf16[4,96,580]{2,1,0:T(8,128)(2,1)S(1)}, u32[]{:S(2)}, u32[]{:S(2)}) collective-permute-start(bf16[4,96,580]{2,1,0:T(8,128)(2,1)S(1)} %constant_dynamic-update-slice_fusion.near_ref), channel_id=1, source_target_pairs={{0,8},{1,9},{2,10},{3,11},{4,12},{5,13},{6,14},{7,15},{8,0},{9,1},... | collective-permute-start | bytes 1336328 | tf_op jit(solution)/shard_map/ppermute | solution.py:413
  46.5 5.4 %project.1 = (bf16[1024,256]{1,0:T(8,128)(2,1)}, bf16[1024,512]{1,0:T(8,128)(2,1)}) custom-call(bf16[1024,768]{1,0:T(8,128)(2,1)} %pad_maximum_fusion.1.x_ref, bf16[768,768]{1,0:T(8,128)(2,1)} %bitcast.88, f32[1024,128]{1,0:T(8,128)} %get-tuple-element.151.cos_ref, f32[1024,128]{1,0:T(8,128)} %get-tuple-element.152.sin_ref), custom_call_target="tpu_custom_call" | custom-call | flops 1207959552 | bytes 5373952 | tf_op jit(solution)/shard_map/project/pallas_call | solution.py:454
  51.9 4.2 %collective-permute-start.10 = (bf16[1024,512]{1,0:T(8,128)(2,1)}, bf16[1024,512]{1,0:T(8,128)(2,1)S(1)}, u32[]{:S(2)}, u32[]{:S(2)}) collective-permute-start(bf16[1024,512]{1,0:T(8,128)(2,1)} %get-tuple-element.154.own_ref), channel_id=1, source_target_pairs={{0,8},{1,9},{2,10},{3,11},{4,12},{5,13},{6,14},{7,15},{8,0},{9,1},... | collective-permute-start | bytes 3145736 | tf_op jit(solution)/shard_map/ppermute | solution.py:413
  63.5 16.2 %attend.1 = (bf16[1024,256]{1,0:T(8,128)(2,1)}, f32[8,1024]{1,0:T(8,128)}) custom-call(s32[2048]{0:T(1024)} %bitcast.103, s32[8,1,256]{2,1,0:T(1,128)} %reshape.184.row_ids_ref, s32[2048,1]{1,0:T(8,128)} %copy.43.col_ids_ref, bf16[1024,256]{1,0:T(8,128)(2,1)} %get-tuple-element.153.q_ref, bf16[1024,512]{1,0:T(8,128)(2,1)} %get-tuple-element.154.own_ref, ...), custom_call_target="tpu_custom_call" | custom-call | flops 6442450944 | bytes 3145728 | tf_op jit(solution)/shard_map/attend/pallas_call | solution.py:566
  90.5 3.1 collective-permute-done.15
  95.4 8.4 %collective-permute-done.17 = bf16[256,768]{1,0:T(8,128)(2,1)} collective-permute-done((bf16[256,768]{1,0:T(8,128)(2,1)}, bf16[256,768]{1,0:T(8,128)(2,1)}, u32[]{:S(2)}, u32[]{:S(2)}) %collective-permute-start.17) | collective-permute-done | bytes 393248 | tf_op jit(solution)/shard_map/ppermute | solution.py:413
  111.2 4.9 %collective-permute-done.20 = bf16[256,768]{1,0:T(8,128)(2,1)S(1)} collective-permute-done((bf16[256,768]{1,0:T(8,128)(2,1)S(1)}, bf16[256,768]{1,0:T(8,128)(2,1)S(1)}, u32[]{:S(2)}, u32[]{:S(2)}) %collective-permute-start.20) | collective-permute-done | bytes 393248 | tf_op jit(solution)/shard_map/ppermute | solution.py:413
  119.0 8.7 %collective-permute-done.22 = bf16[256,768]{1,0:T(8,128)(2,1)S(1)} collective-permute-done((bf16[256,768]{1,0:T(8,128)(2,1)S(1)}, bf16[256,768]{1,0:T(8,128)(2,1)S(1)}, u32[]{:S(2)}, u32[]{:S(2)}) %collective-permute-start.22) | collective-permute-done | bytes 393248 | tf_op jit(solution)/shard_map/ppermute | solution.py:413
  129.1 3.2 unpack.1
  132.2 4.3 %fusion.49 = f32[1024,1536]{1,0:T(8,128)S(1)} fusion(bf16[1024,768]{1,0:T(8,128)(2,1)S(1)} %constant_dynamic-update-slice_fusion.2, bf16[768,1536]{1,0:T(8,128)(2,1)} %bitcast.79), kind=kOutput, calls=%fused_computation.168 | convolution fusion | flops 2415919104 | bytes 10223616 | tf_op jit(solution)/shard_map/dot_general | solution.py:490
  144.2 6.6 %collective-permute-done.25 = bf16[256,768]{1,0:T(8,128)(2,1)S(1)} collective-permute-done((bf16[256,768]{1,0:T(8,128)(2,1)S(1)}, bf16[256,768]{1,0:T(8,128)(2,1)S(1)}, u32[]{:S(2)}, u32[]{:S(2)}) %collective-permute-start.25) | collective-permute-done | bytes 393248 | tf_op jit(solution)/shard_map/ppermute | solution.py:413
  150.8 4.9 %collective-permute-done.26 = bf16[256,768]{1,0:T(8,128)(2,1)S(1)} collective-permute-done((bf16[256,768]{1,0:T(8,128)(2,1)S(1)}, bf16[256,768]{1,0:T(8,128)(2,1)S(1)}, u32[]{:S(2)}, u32[]{:S(2)}) %collective-permute-start.26) | collective-permute-done | bytes 393248 | tf_op jit(solution)/shard_map/ppermute | solution.py:413
  155.7 8.9 %collective-permute-done.27 = bf16[256,768]{1,0:T(8,128)(2,1)S(1)} collective-permute-done((bf16[256,768]{1,0:T(8,128)(2,1)S(1)}, bf16[256,768]{1,0:T(8,128)(2,1)S(1)}, u32[]{:S(2)}, u32[]{:S(2)}) %collective-permute-start.27) | collective-permute-done | bytes 393248 | tf_op jit(solution)/shard_map/ppermute | solution.py:413
  170.4 7.6 %collective-permute-done.29 = bf16[256,768]{1,0:T(8,128)(2,1)S(1)} collective-permute-done((bf16[256,768]{1,0:T(8,128)(2,1)S(1)}, bf16[256,768]{1,0:T(8,128)(2,1)S(1)}, u32[]{:S(2)}, u32[]{:S(2)}) %collective-permute-start.29) | collective-permute-done | bytes 393248 | tf_op jit(solution)/shard_map/ppermute | solution.py:413
  179.8 7.1 %collective-permute-done.31 = bf16[256,768]{1,0:T(8,128)(2,1)S(1)} collective-permute-done((bf16[256,768]{1,0:T(8,128)(2,1)S(1)}, bf16[256,768]{1,0:T(8,128)(2,1)S(1)}, u32[]{:S(2)}, u32[]{:S(2)}) %collective-permute-start.31) | collective-permute-done | bytes 393248 | tf_op jit(solution)/shard_map/ppermute | solution.py:413
  206.3 5.9 %collective-permute-done.34 = bf16[256,768]{1,0:T(8,128)(2,1)S(1)} collective-permute-done((bf16[256,768]{1,0:T(8,128)(2,1)S(1)}, bf16[256,768]{1,0:T(8,128)(2,1)S(1)}, u32[]{:S(2)}, u32[]{:S(2)}) %collective-permute-start.34) | collective-permute-done | bytes 393248 | tf_op jit(solution)/shard_map/ppermute | solution.py:413
  218.4 4.1 %split_feed.1 = (bf16[12,48,768]{2,1,0:T(8,128)(2,1)}, bf16[12,48,768]{2,1,0:T(8,128)(2,1)}) custom-call(s32[1]{0:T(128)} %bitcast.20.x_ref, f32[4,2,48,768]{3,2,1,0:T(8,128)} %bitcast.87, bf16[4,2,48,768]{3,2,1,0:T(8,128)(2,1)} %bitcast.94, f32[4,2,48,1536]{3,2,1,0:T(8,128)} %bitcast.84, bf16[4,2,48,1536]{3,2,1,0:T(8,128)(2,1)} %bitcast.93), custom_call_target="tpu_custom_call" | custom-call | flops 1769472 | bytes 10616832 | tf_op jit(solution)/shard_map/split_feed/pallas_call | solution.py:903
  227.2 4.7 %collective-permute-done.39 = bf16[256,768]{1,0:T(8,128)(2,1)S(1)} collective-permute-done((bf16[256,768]{1,0:T(8,128)(2,1)S(1)}, bf16[256,768]{1,0:T(8,128)(2,1)S(1)}, u32[]{:S(2)}, u32[]{:S(2)}) %collective-permute-start.39) | collective-permute-done | bytes 393248 | tf_op jit(solution)/shard_map/ppermute | solution.py:413
  234.4 6.8 %collective-permute-done.40 = bf16[12,48,768]{2,1,0:T(8,128)(2,1)S(1)} collective-permute-done((bf16[12,48,768]{2,1,0:T(8,128)(2,1)}, bf16[12,48,768]{2,1,0:T(8,128)(2,1)S(1)}, u32[]{:S(2)}, u32[]{:S(2)}) %collective-permute-start.40) | collective-permute-done | bytes 884768 | tf_op jit(solution)/shard_map/ppermute | solution.py:413
  244.7 29.4 %attend_back.1 = (bf16[1024,256]{1,0:T(8,128)(2,1)}, f32[1024,512]{1,0:T(8,128)}, bf16[1024,512]{1,0:T(8,128)(2,1)}) custom-call(s32[2048]{0:T(1024)} %bitcast.104, s32[8,1,256]{2,1,0:T(1,128)} %reshape.184.row_ids_ref, s32[2048,1]{1,0:T(8,128)} %copy.43.col_ids_ref, bf16[1024,256]{1,0:T(8,128)(2,1)} %get-tuple-element.153.q_ref, ...), custom_call_target="tpu_custom_call" | custom-call | flops 16106127360 | bytes 3145728 | tf_op jit(solution)/shard_map/attend_back/pallas_call | solution.py:704
  280.2 3.6 collective-permute-start.47
  283.8 3.3 collective-permute-start.48
  289.4 4.5 %join_grads.1 = bf16[1024,768]{1,0:T(8,128)(2,1)} custom-call(bf16[1024,256]{1,0:T(8,128)(2,1)} %get-tuple-element.201.dq_ref, f32[1024,512]{1,0:T(8,128)} %get-tuple-element.202.own_ref, bf16[1024,512]{1,0:T(8,128)(2,1)} %copy-done.11, f32[1024,128]{1,0:T(8,128)} %get-tuple-element.151.cos_ref, f32[1024,128]{1,0:T(8,128)} %get-tuple-element.152.sin_ref), custom_call_target="tpu_custom_call" | custom-call | flops 4194304 | bytes 5767168 | tf_op jit(solution)/shard_map/join_grads/pallas_call | solution.py:758
  294.0 4.2 %fusion.53 = f32[768,768]{1,0:T(8,128)} fusion(bf16[1024,768]{1,0:T(8,128)(2,1)S(1)} %copy-done.5, bf16[1024,768]{1,0:T(8,128)(2,1)} %join_grads.1), kind=kOutput, calls=%fused_computation.172 | convolution fusion | flops 1207959552 | bytes 5505024 | tf_op jit(solution)/shard_map/dot_general | solution.py:490
  324.4 4.5 %collective-permute-done.52 = bf16[256,768]{1,0:T(8,128)(2,1)S(1)} collective-permute-done((bf16[256,768]{1,0:T(8,128)(2,1)S(1)}, bf16[256,768]{1,0:T(8,128)(2,1)S(1)}, u32[]{:S(2)}, u32[]{:S(2)}) %collective-permute-start.52) | collective-permute-done | bytes 393248 | tf_op jit(solution)/shard_map/ppermute | solution.py:413
  329.6 9.0 %collective-permute-done.53 = bf16[256,768]{1,0:T(8,128)(2,1)S(1)} collective-permute-done((bf16[256,768]{1,0:T(8,128)(2,1)S(1)}, bf16[256,768]{1,0:T(8,128)(2,1)S(1)}, u32[]{:S(2)}, u32[]{:S(2)}) %collective-permute-start.53) | collective-permute-done | bytes 393248 | tf_op jit(solution)/shard_map/ppermute | solution.py:413
  343.8 6.8 %collective-permute-start.61 = (bf16[64,768]{1,0:T(8,128)(2,1)}, bf16[64,768]{1,0:T(8,128)(2,1)S(1)}, u32[]{:S(2)}, u32[]{:S(2)}) collective-permute-start(bf16[64,768]{1,0:T(8,128)(2,1)} %get-tuple-element.243), channel_id=1, source_target_pairs={{0,1},{1,0},{2,3},{3,2},{12,13},{13,12},{14,15},{15,14},{16,17},{1... | collective-permute-start | bytes 294920 | tf_op jit(solution)/shard_map/ppermute | solution.py:413
  353.5 3.4 collective-permute-start.63
  357.5 4.0 %finish_feed.1 = (f32[4,2,48,768]{3,2,1,0:T(8,128)}, f32[2,48,3072]{2,1,0:T(8,128)}, f32[2,48,3072]{2,1,0:T(8,128)}) custom-call(s32[2]{0:T(128)} %pad_add_fusion.4.flag_ref, bf16[12,48,768]{2,1,0:T(8,128)(2,1)} %join_feed.1.own_ref, bf16[12,48,768]{2,1,0:T(8,128)(2,1)} %collective-permute-done.56.other_ref, bf16[12,48,768]{2,1,0:T(8,128)(2,1)} %copy-done.14, ...), custom_call_target="tpu_custom_call" | custom-call | flops 1769472 | bytes 7077888 | tf_op jit(solution)/shard_map/finish_feed/pallas_call | solution.py:903
  367.5 5.7 %collective-permute-done.64.other_ref = bf16[208,768]{1,0:T(8,128)(2,1)S(1)} collective-permute-done((bf16[208,768]{1,0:T(8,128)(2,1)}, bf16[208,768]{1,0:T(8,128)(2,1)S(1)}, u32[]{:S(2)}, u32[]{:S(2)}) %collective-permute-start.64) | collective-permute-done | bytes 319520 | tf_op jit(solution)/shard_map/ppermute | solution.py:413
  (317 shorter events, 170.0 us)
Async XLA Ops:
  12.2 34.2 %collective-permute-start.8 = (bf16[96,768]{1,0:T(8,128)(2,1)}, bf16[96,768]{1,0:T(8,128)(2,1)S(1)}, u32[]{:S(2)}, u32[]{:S(2)}) collective-permute-start(bf16[96,768]{1,0:T(8,128)(2,1)} %param.15), channel_id=1, source_target_pairs={{0,0},{1,8},{2,1},{3,9},{4,2},{5,10},{6,3},{7,11},{8,4},{9,12},{10... | collective-permute-start | bytes 442376 | tf_op jit(solution)/shard_map/ppermute | solution.py:413
  19.7 22.2 %collective-permute-start.1 = (bf16[256,768]{1,0:T(8,128)(2,1)S(1)}, bf16[256,768]{1,0:T(8,128)(2,1)S(1)}, u32[]{:S(2)}, u32[]{:S(2)}) collective-permute-start(bf16[256,768]{1,0:T(8,128)(2,1)S(1)} %collective-permute-done), channel_id=1, source_target_pairs={{0,1},{1,0},{2,3},{3,2},{4,5},{5,4},{6,7},{7,6},{8,9},{9,8},{10,11... | collective-permute-start | bytes 1179656 | tf_op jit(solution)/shard_map/ppermute | solution.py:413
  26.4 15.5 %collective-permute-start.2 = (bf16[256,768]{1,0:T(8,128)(2,1)S(1)}, bf16[256,768]{1,0:T(8,128)(2,1)S(1)}, u32[]{:S(2)}, u32[]{:S(2)}) collective-permute-start(bf16[256,768]{1,0:T(8,128)(2,1)S(1)} %collective-permute-done), channel_id=1, source_target_pairs={{0,2},{1,3},{2,0},{3,1},{4,6},{5,7},{6,4},{7,5},{8,10},{9,11},{10,... | collective-permute-start | bytes 1179656 | tf_op jit(solution)/shard_map/ppermute | solution.py:413
  26.9 15.0 %collective-permute-start.3 = (bf16[256,768]{1,0:T(8,128)(2,1)S(1)}, bf16[256,768]{1,0:T(8,128)(2,1)S(1)}, u32[]{:S(2)}, u32[]{:S(2)}) collective-permute-start(bf16[256,768]{1,0:T(8,128)(2,1)S(1)} %collective-permute-done), channel_id=1, source_target_pairs={{0,3},{1,2},{2,1},{3,0},{4,7},{5,6},{6,5},{7,4},{8,11},{9,10},{10,... | collective-permute-start | bytes 1179656 | tf_op jit(solution)/shard_map/ppermute | solution.py:413
  28.0 15.1 %collective-permute-start.7 = (bf16[4,96,580]{2,1,0:T(8,128)(2,1)S(1)}, bf16[4,96,580]{2,1,0:T(8,128)(2,1)S(1)}, u32[]{:S(2)}, u32[]{:S(2)}) collective-permute-start(bf16[4,96,580]{2,1,0:T(8,128)(2,1)S(1)} %constant_dynamic-update-slice_fusion.near_ref), channel_id=1, source_target_pairs={{0,8},{1,9},{2,10},{3,11},{4,12},{5,13},{6,14},{7,15},{8,0},{9,1},... | collective-permute-start | bytes 1336328 | tf_op jit(solution)/shard_map/ppermute | solution.py:413
  58.8 21.0 %collective-permute-start.13 = (bf16[96,1536]{1,0:T(8,128)(2,1)}, bf16[96,1536]{1,0:T(8,128)(2,1)S(1)}, u32[]{:S(2)}, u32[]{:S(2)}) collective-permute-start(bf16[96,1536]{1,0:T(8,128)(2,1)} %get-tuple-element.163), channel_id=1, source_target_pairs={{0,0},{1,1},{2,2},{3,3},{4,4},{5,5},{6,6},{7,7},{8,12},{9,13},{10,... | collective-permute-start | bytes 884744 | tf_op jit(solution)/shard_map/ppermute | solution.py:413
  60.6 19.3 %collective-permute-start.14 = (bf16[96,1536]{1,0:T(8,128)(2,1)}, bf16[96,1536]{1,0:T(8,128)(2,1)S(1)}, u32[]{:S(2)}, u32[]{:S(2)}) collective-permute-start(bf16[96,1536]{1,0:T(8,128)(2,1)} %get-tuple-element.164), channel_id=1, source_target_pairs={{0,1},{1,0},{2,3},{3,2},{4,5},{5,4},{6,7},{7,6},{8,13},{9,12},{10,... | collective-permute-start | bytes 884744 | tf_op jit(solution)/shard_map/ppermute | solution.py:413
  62.6 17.2 %collective-permute-start.12 = (bf16[96,768]{1,0:T(8,128)(2,1)S(1)}, bf16[96,768]{1,0:T(8,128)(2,1)}, u32[]{:S(2)}, u32[]{:S(2)}) collective-permute-start(bf16[96,768]{1,0:T(8,128)(2,1)S(1)} %constant_dynamic-slice_fusion.1), channel_id=1, source_target_pairs={{0,4},{1,5},{2,6},{3,7},{4,0},{5,1},{6,2},{7,3},{8,12},{9,13},{10,... | collective-permute-start | bytes 442376 | tf_op jit(solution)/shard_map/ppermute | solution.py:413
  86.5 17.3 %collective-permute-start.17 = (bf16[256,768]{1,0:T(8,128)(2,1)}, bf16[256,768]{1,0:T(8,128)(2,1)}, u32[]{:S(2)}, u32[]{:S(2)}) collective-permute-start(bf16[256,768]{1,0:T(8,128)(2,1)} %convolution_convert_fusion.10), channel_id=1, source_target_pairs={{0,3},{1,2},{2,1},{3,0},{4,7},{5,6},{6,5},{7,4},{8,11},{9,10},{10,... | collective-permute-start | bytes 1179656 | tf_op jit(solution)/shard_map/ppermute | solution.py:413
  88.4 17.3 %collective-permute-start.18 = (bf16[2,96,1536]{2,1,0:T(8,128)(2,1)S(1)}, bf16[2,96,1536]{2,1,0:T(8,128)(2,1)S(1)}, u32[]{:S(2)}, u32[]{:S(2)}) collective-permute-start(bf16[2,96,1536]{2,1,0:T(8,128)(2,1)S(1)} %pad_maximum_fusion.4), channel_id=1, source_target_pairs={{0,16},{1,17},{2,18},{3,19},{4,20},{5,21},{6,22},{7,23},{8,24},{9,... | collective-permute-start | bytes 1769480 | tf_op jit(solution)/shard_map/ppermute | solution.py:413
  89.8 15.9 %collective-permute-start.19 = (bf16[96,768]{1,0:T(8,128)(2,1)}, bf16[96,768]{1,0:T(8,128)(2,1)S(1)}, u32[]{:S(2)}, u32[]{:S(2)}) collective-permute-start(bf16[96,768]{1,0:T(8,128)(2,1)} %collective-permute-done.12), channel_id=1, source_target_pairs={{0,16},{1,17},{2,18},{3,19},{4,20},{5,21},{6,22},{7,23},{8,24},{9,... | collective-permute-start | bytes 442376 | tf_op jit(solution)/shard_map/ppermute | solution.py:413
  108.5 19.2 %collective-permute-start.22 = (bf16[256,768]{1,0:T(8,128)(2,1)S(1)}, bf16[256,768]{1,0:T(8,128)(2,1)S(1)}, u32[]{:S(2)}, u32[]{:S(2)}) collective-permute-start(bf16[256,768]{1,0:T(8,128)(2,1)S(1)} %fusion.17), channel_id=1, source_target_pairs={{0,3},{1,2},{2,1},{3,0},{4,7},{5,6},{6,5},{7,4},{8,11},{9,10},{10,... | collective-permute-start | bytes 1179656 | tf_op jit(solution)/shard_map/ppermute | solution.py:413
  110.1 19.0 %collective-permute-start.23 = (bf16[4,96,1536]{2,1,0:T(8,128)(2,1)S(1)}, bf16[4,96,1536]{2,1,0:T(8,128)(2,1)}, u32[]{:S(2)}, u32[]{:S(2)}) collective-permute-start(bf16[4,96,1536]{2,1,0:T(8,128)(2,1)S(1)} %constant_dynamic-update-slice_fusion.6.near_ref), channel_id=1, source_target_pairs={{0,8},{1,9},{2,10},{3,11},{4,12},{5,13},{6,14},{7,15},{8,0},{9,1},... | collective-permute-start | bytes 3538952 | tf_op jit(solution)/shard_map/ppermute | solution.py:413
  139.5 16.2 %collective-permute-start.26 = (bf16[256,768]{1,0:T(8,128)(2,1)S(1)}, bf16[256,768]{1,0:T(8,128)(2,1)S(1)}, u32[]{:S(2)}, u32[]{:S(2)}) collective-permute-start(bf16[256,768]{1,0:T(8,128)(2,1)S(1)} %convolution_convert_fusion.8), channel_id=1, source_target_pairs={{0,2},{1,3},{2,0},{3,1},{4,6},{5,7},{6,4},{7,5},{8,10},{9,11},{10,... | collective-permute-start | bytes 1179656 | tf_op jit(solution)/shard_map/ppermute | solution.py:413
  141.4 23.3 %collective-permute-start.27 = (bf16[256,768]{1,0:T(8,128)(2,1)S(1)}, bf16[256,768]{1,0:T(8,128)(2,1)S(1)}, u32[]{:S(2)}, u32[]{:S(2)}) collective-permute-start(bf16[256,768]{1,0:T(8,128)(2,1)S(1)} %convolution_convert_fusion.7), channel_id=1, source_target_pairs={{0,3},{1,2},{2,1},{3,0},{4,7},{5,6},{6,5},{7,4},{8,11},{9,10},{10,... | collective-permute-start | bytes 1179656 | tf_op jit(solution)/shard_map/ppermute | solution.py:413
  143.3 22.1 %collective-permute-start.28 = (bf16[256,768]{1,0:T(8,128)(2,1)S(1)}, bf16[256,768]{1,0:T(8,128)(2,1)S(1)}, u32[]{:S(2)}, u32[]{:S(2)}) collective-permute-start(bf16[256,768]{1,0:T(8,128)(2,1)S(1)} %bitcast.116), channel_id=1, source_target_pairs={{0,0},{1,1},{2,2},{3,3},{4,8},{5,9},{6,10},{7,11},{8,4},{9,5},{10,... | collective-permute-start | bytes 1179656 | tf_op jit(solution)/shard_map/ppermute | solution.py:413
  167.9 19.1 %collective-permute-start.31 = (bf16[256,768]{1,0:T(8,128)(2,1)S(1)}, bf16[256,768]{1,0:T(8,128)(2,1)S(1)}, u32[]{:S(2)}, u32[]{:S(2)}) collective-permute-start(bf16[256,768]{1,0:T(8,128)(2,1)S(1)} %fusion.44), channel_id=1, source_target_pairs={{0,3},{1,2},{2,1},{3,0},{4,7},{5,6},{6,5},{7,4},{8,11},{9,10},{10,... | collective-permute-start | bytes 1179656 | tf_op jit(solution)/shard_map/ppermute | solution.py:413
  194.6 17.6 %collective-permute-start.34 = (bf16[256,768]{1,0:T(8,128)(2,1)S(1)}, bf16[256,768]{1,0:T(8,128)(2,1)S(1)}, u32[]{:S(2)}, u32[]{:S(2)}) collective-permute-start(bf16[256,768]{1,0:T(8,128)(2,1)S(1)} %convolution_convert_fusion.4), channel_id=1, source_target_pairs={{0,3},{1,2},{2,1},{3,0},{4,7},{5,6},{6,5},{7,4},{8,11},{9,10},{10,... | collective-permute-start | bytes 1179656 | tf_op jit(solution)/shard_map/ppermute | solution.py:413
  215.8 16.2 %collective-permute-start.39 = (bf16[256,768]{1,0:T(8,128)(2,1)S(1)}, bf16[256,768]{1,0:T(8,128)(2,1)S(1)}, u32[]{:S(2)}, u32[]{:S(2)}) collective-permute-start(bf16[256,768]{1,0:T(8,128)(2,1)S(1)} %get-tuple-element.184), channel_id=1, source_target_pairs={{0,3},{1,2},{2,1},{3,0},{4,7},{5,6},{6,5},{7,4},{8,11},{9,10},{10,... | collective-permute-start | bytes 1179656 | tf_op jit(solution)/shard_map/ppermute | solution.py:413
  222.5 18.7 %collective-permute-start.40 = (bf16[12,48,768]{2,1,0:T(8,128)(2,1)}, bf16[12,48,768]{2,1,0:T(8,128)(2,1)S(1)}, u32[]{:S(2)}, u32[]{:S(2)}) collective-permute-start(bf16[12,48,768]{2,1,0:T(8,128)(2,1)} %get-tuple-element.187), channel_id=1, source_target_pairs={{0,16},{1,17},{2,18},{3,19},{4,20},{5,21},{6,22},{7,23},{8,24},{9,... | collective-permute-start | bytes 2654216 | tf_op jit(solution)/shard_map/ppermute | solution.py:413
  241.5 32.6 %collective-permute-start.42 = (bf16[12,48,768]{2,1,0:T(8,128)(2,1)S(1)}, bf16[12,48,768]{2,1,0:T(8,128)(2,1)S(1)}, u32[]{:S(2)}, u32[]{:S(2)}) collective-permute-start(bf16[12,48,768]{2,1,0:T(8,128)(2,1)S(1)} %add.218.mine_ref), channel_id=1, source_target_pairs={{4,0},{5,1},{6,2},{7,3},{8,12},{9,13},{10,14},{11,15},{20,16},{21,... | collective-permute-start | bytes 2654216 | tf_op jit(solution)/shard_map/ppermute | solution.py:413
  242.8 31.3 %collective-permute-start.44 = (bf16[256,768]{1,0:T(8,128)(2,1)}, bf16[256,768]{1,0:T(8,128)(2,1)S(1)}, u32[]{:S(2)}, u32[]{:S(2)}) collective-permute-start(bf16[256,768]{1,0:T(8,128)(2,1)} %get-tuple-element.199), channel_id=1, source_target_pairs={{0,0},{1,1},{2,2},{3,3},{4,8},{5,9},{6,10},{7,11},{8,4},{9,5},{10,... | collective-permute-start | bytes 1179656 | tf_op jit(solution)/shard_map/ppermute | solution.py:413
  244.4 29.7 %collective-permute-start.43 = (bf16[96,768]{1,0:T(8,128)(2,1)S(1)}, bf16[96,768]{1,0:T(8,128)(2,1)S(1)}, u32[]{:S(2)}, u32[]{:S(2)}) collective-permute-start(bf16[96,768]{1,0:T(8,128)(2,1)S(1)} %add_convert_fusion.3), channel_id=1, source_target_pairs={{0,16},{1,17},{2,18},{3,19},{4,20},{5,21},{6,22},{7,23},{8,24},{9,... | collective-permute-start | bytes 442376 | tf_op jit(solution)/shard_map/ppermute | solution.py:413
  278.9 21.8 %collective-permute-start.46 = (bf16[96,768]{1,0:T(8,128)(2,1)}, bf16[96,768]{1,0:T(8,128)(2,1)}, u32[]{:S(2)}, u32[]{:S(2)}) collective-permute-start(bf16[96,768]{1,0:T(8,128)(2,1)} %add_convert_fusion.2), channel_id=1, source_target_pairs={{0,4},{1,5},{2,6},{3,7},{4,0},{5,1},{6,2},{7,3},{8,12},{9,13},{10,... | collective-permute-start | bytes 442376 | tf_op jit(solution)/shard_map/ppermute | solution.py:413
  280.2 20.6 %collective-permute-start.47 = (bf16[2,48,768]{2,1,0:T(8,128)(2,1)}, bf16[2,48,768]{2,1,0:T(8,128)(2,1)}, u32[]{:S(2)}, u32[]{:S(2)}) collective-permute-start(bf16[2,48,768]{2,1,0:T(8,128)(2,1)} %get-tuple-element.211), channel_id=1, source_target_pairs={{0,1},{1,0},{2,3},{3,2},{12,13},{13,12},{14,15},{15,14},{16,17},{1... | collective-permute-start | bytes 442376 | tf_op jit(solution)/shard_map/ppermute | solution.py:413
  283.8 17.0 %collective-permute-start.48 = (bf16[2,48,768]{2,1,0:T(8,128)(2,1)}, bf16[2,48,768]{2,1,0:T(8,128)(2,1)}, u32[]{:S(2)}, u32[]{:S(2)}) collective-permute-start(bf16[2,48,768]{2,1,0:T(8,128)(2,1)} %get-tuple-element.212), channel_id=1, source_target_pairs={{0,2},{1,3},{2,0},{3,1},{12,14},{13,15},{14,12},{15,13},{16,18},{1... | collective-permute-start | bytes 442376 | tf_op jit(solution)/shard_map/ppermute | solution.py:413
  313.1 25.8 %collective-permute-start.56 = (bf16[12,48,768]{2,1,0:T(8,128)(2,1)S(1)}, bf16[12,48,768]{2,1,0:T(8,128)(2,1)}, u32[]{:S(2)}, u32[]{:S(2)}) collective-permute-start(bf16[12,48,768]{2,1,0:T(8,128)(2,1)S(1)} %copy-done.1), channel_id=1, source_target_pairs={{0,16},{1,17},{2,18},{3,19},{12,28},{13,29},{14,30},{15,31},{16,0}... | collective-permute-start | bytes 2654216 | tf_op jit(solution)/shard_map/ppermute | solution.py:413
  315.5 23.4 %collective-permute-start.57 = (bf16[12,48,768]{2,1,0:T(8,128)(2,1)S(1)}, bf16[12,48,768]{2,1,0:T(8,128)(2,1)S(1)}, u32[]{:S(2)}, u32[]{:S(2)}) collective-permute-start(bf16[12,48,768]{2,1,0:T(8,128)(2,1)S(1)} %copy-done.1), channel_id=1, source_target_pairs={{0,8},{1,9},{2,10},{3,11},{12,4},{13,5},{14,6},{15,7},{16,24},{17,... | collective-permute-start | bytes 2654216 | tf_op jit(solution)/shard_map/ppermute | solution.py:413
  319.3 19.3 %collective-permute-start.53 = (bf16[256,768]{1,0:T(8,128)(2,1)S(1)}, bf16[256,768]{1,0:T(8,128)(2,1)S(1)}, u32[]{:S(2)}, u32[]{:S(2)}) collective-permute-start(bf16[256,768]{1,0:T(8,128)(2,1)S(1)} %convolution_convert_fusion.1), channel_id=1, source_target_pairs={{0,3},{1,2},{2,1},{3,0},{4,7},{5,6},{6,5},{7,4},{8,11},{9,10},{10,... | collective-permute-start | bytes 1179656 | tf_op jit(solution)/shard_map/ppermute | solution.py:413
  322.6 16.3 %collective-permute-start.55 = (bf16[208,768]{1,0:T(8,128)(2,1)S(1)}, bf16[208,768]{1,0:T(8,128)(2,1)S(1)}, u32[]{:S(2)}, u32[]{:S(2)}) collective-permute-start(bf16[208,768]{1,0:T(8,128)(2,1)S(1)} %add.229.mine_ref), channel_id=1, source_target_pairs={{4,0},{5,1},{6,2},{7,3},{8,12},{9,13},{10,14},{11,15},{20,16},{21,... | collective-permute-start | bytes 958472 | tf_op jit(solution)/shard_map/ppermute | solution.py:413
  341.3 20.2 %collective-permute-start.59 = (bf16[256,768]{1,0:T(8,128)(2,1)S(1)}, bf16[256,768]{1,0:T(8,128)(2,1)S(1)}, u32[]{:S(2)}, u32[]{:S(2)}) collective-permute-start(bf16[256,768]{1,0:T(8,128)(2,1)S(1)} %add_convert_fusion), channel_id=1, source_target_pairs={{0,0},{1,1},{2,2},{3,3},{4,8},{5,9},{6,10},{7,11},{8,4},{9,5},{10,... | collective-permute-start | bytes 1179656 | tf_op jit(solution)/shard_map/ppermute | solution.py:413
  343.8 17.7 %collective-permute-start.61 = (bf16[64,768]{1,0:T(8,128)(2,1)}, bf16[64,768]{1,0:T(8,128)(2,1)S(1)}, u32[]{:S(2)}, u32[]{:S(2)}) collective-permute-start(bf16[64,768]{1,0:T(8,128)(2,1)} %get-tuple-element.243), channel_id=1, source_target_pairs={{0,1},{1,0},{2,3},{3,2},{12,13},{13,12},{14,15},{15,14},{16,17},{1... | collective-permute-start | bytes 294920 | tf_op jit(solution)/shard_map/ppermute | solution.py:413
  (77 other events, 653.7 us)

commit v4 on v3

--- a/solution.py
+++ b/solution.py
@@ -406,7 +406,6 @@
     moves(lambda x, c, h, j, k=k: (x, c, h, j ^ k) if c == h else None) for k in range(GROUP)
 ]
 HOME_X = moves(lambda x, c, h, j: (1 - x, c, h, j) if c == h else None)
-HOME_CORE = moves(lambda x, c, h, j: (x, 1 - c, h, j) if c == h else None)
 
 
 def send(value, pairs):
@@ -742,28 +741,62 @@
     )(ids, row_ids, col_ids, queries, upstream, attended, logs, kv_own, kv_other, cosine, sine)
 
 
-def join_grads_kernel(dq_ref, own_ref, got_ref, cos_ref, sin_ref, out_ref):
-    out_ref[:, :WIDE] = dq_ref[...]
+def grad_qkv_kernel(
+    c_ref, x_ref, dq_ref, own_ref, got_ref, cos_ref, sin_ref, vectors_ref,
+    out_ref, keep_ref, away_ref, acc_ref,
+):
+    tile = pl.program_id(0)
     total = own_ref[...] + got_ref[...].astype(F32)
     keys = total[:, :WIDE]
-    out_ref[:, WIDE : 2 * WIDE] = (
-        keys * doubled(cos_ref[...]) - turned(keys) * doubled(sin_ref[...])
-    ).astype(BF)
-    out_ref[:, 2 * WIDE :] = total[:, WIDE:].astype(BF)
-
-
-def join_grads(grad_queries, own, got, cosine, sine):
+    keys = keys * doubled(cos_ref[...]) - turned(keys) * doubled(sin_ref[...])
+    grads = jnp.concatenate(
+        [dq_ref[...], keys.astype(BF), total[:, WIDE:].astype(BF)], axis=1
+    )
+    out_ref[...] = grads
+    part = contract(x_ref[...], grads, 0, 0)
+
+    @pl.when(tile == 0)
+    def _():
+        acc_ref[...] = part
+
+    @pl.when(tile > 0)
+    def _():
+        acc_ref[...] += part
+
+    @pl.when(tile == pl.num_programs(0) - 1)
+    def _():
+        rows = keep_ref.shape[0]
+        core = c_ref[0]
+        keep_ref[...] = acc_ref[pl.ds(pl.multiple_of(core * rows, 8), rows), :]
+        away_ref[:rows] = acc_ref[pl.ds(pl.multiple_of((1 - core) * rows, 8), rows), :].astype(BF)
+        away_ref[rows:] = jnp.zeros((16, away_ref.shape[1]), BF)
+        away_ref[rows : rows + 8] = vectors_ref[...].astype(BF)
+
+
+def grad_qkv(core, x_rows, grad_queries, own, got, cosine, sine, vectors):
     rows = grad_queries.shape[0]
-    tiled = lambda width: pl.BlockSpec((TILE, width), lambda i: (i, 0))
+    tiled = lambda width: pl.BlockSpec((TILE, width), lambda i, c: (i, 0))
+    whole = lambda *shape: pl.BlockSpec(shape, lambda i, c: (0, 0))
     return pl.pallas_call(
-        join_grads_kernel,
-        grid=(rows // TILE,),
-        in_specs=[tiled(WIDE), tiled(2 * WIDE), tiled(2 * WIDE), tiled(128), tiled(128)],
-        out_specs=tiled(3 * WIDE),
-        out_shape=jax.ShapeDtypeStruct((rows, 3 * WIDE), BF),
-        cost_estimate=cost(8 * own.size, own, own, got, grad_queries),
-        name="join_grads",
-    )(grad_queries, own, got, cosine, sine)
+        grad_qkv_kernel,
+        grid_spec=pltpu.PrefetchScalarGridSpec(
+            num_scalar_prefetch=1,
+            grid=(rows // TILE,),
+            in_specs=[
+                tiled(D), tiled(WIDE), tiled(2 * WIDE), tiled(2 * WIDE), tiled(LANES),
+                tiled(LANES), whole(*vectors.shape),
+            ],
+            out_specs=[tiled(3 * WIDE), whole(D // 2, 3 * WIDE), whole(D // 2 + 16, 3 * WIDE)],
+            scratch_shapes=[pltpu.VMEM((D, 3 * WIDE), F32)],
+        ),
+        out_shape=[
+            jax.ShapeDtypeStruct((rows, 3 * WIDE), BF),
+            jax.ShapeDtypeStruct((D // 2, 3 * WIDE), F32),
+            jax.ShapeDtypeStruct((D // 2 + 16, 3 * WIDE), BF),
+        ],
+        cost_estimate=cost(2 * rows * D * 3 * WIDE, own, own, got, grad_queries),
+        name="grad_qkv",
+    )(core, x_rows, grad_queries, own, got, cosine, sine, vectors)
 
 
 def after(value, *others):
@@ -950,22 +983,15 @@
                 ref[side, :, width + start : width + start + half] = block[:, half:]
 
 
-def split_cores_kernel(c_ref, part_ref, vectors_ref, away_ref):
-    rows = part_ref.shape[1]
-    away_ref[:rows] = part_ref[1 - c_ref[0]].astype(BF)
-    away_ref[rows:] = jnp.zeros((16, part_ref.shape[2]), BF)
-    away_ref[rows : rows + 8] = vectors_ref[...].astype(BF)
-
-
 def split_x_kernel(flag_ref, part_ref, vectors_ref, got_ref, keep_ref, away_ref):
-    core, mine = flag_ref[0], flag_ref[1]
-    rows = part_ref.shape[1]
+    mine = flag_ref[0]
+    rows = part_ref.shape[0]
     step = rows // (2 * GROUP)
     for block in range(GROUP):
         for side, ref in ((mine, keep_ref), (1 - mine, away_ref)):
             place = pl.ds(pl.multiple_of((2 * block + side) * step, step), step)
             ref[block * step : (block + 1) * step] = (
-                part_ref[core, place] + got_ref[place].astype(F32)
+                part_ref[place] + got_ref[place].astype(F32)
             ).astype(BF)
     for ref in (keep_ref, away_ref):
         ref[GROUP * step :] = got_ref[rows:]
@@ -1083,6 +1109,7 @@
     qkv_far = send(qkv_near, OTHER_CORE)
     qkv_own, vectors_got = unpack_qkv(places, qkv_near, qkv_far)
     qkv_own = qkv_own.reshape(D, 3 * WIDE)
+    qkv_own, *x_tiles = join(qkv_own, *x_tiles)
     x_rows = jnp.concatenate(x_tiles, axis=0)
 
     tile_index = j ^ jnp.arange(GROUP, dtype=jnp.int32)
@@ -1106,24 +1133,22 @@
     part_f = rows_f // 4
     gate_up_packed = pack_gate_up(targets, w_gate, w_up)
     down_sent = lax.dynamic_slice_in_dim(down_whole, (2 * c + x) * part_f, part_f, 0)
+    down_mine = send(down_sent, OTHER_HALF)
     (
-        x_rows, qkv_own, vectors_got, out_got, flat_ids, row_ids, col_ids, cosine, sine, down_sent,
+        x_rows, qkv_own, vectors_got, out_got, flat_ids, row_ids, col_ids, cosine, sine, down_mine,
         *gate_up_packed,
     ) = join(
-        x_rows, qkv_own, vectors_got, out_got, flat_ids, row_ids, col_ids, cosine, sine, down_sent,
+        x_rows, qkv_own, vectors_got, out_got, flat_ids, row_ids, col_ids, cosine, sine, down_mine,
         *gate_up_packed,
     )
 
     queries, kv_own = project(x_rows, qkv_own, cosine, sine)
     kv_other = send(kv_own, OTHER_CORE)
     out_other = send(out_got, OTHER_CORE)
-    kv_other, out_other, down_sent, *gate_up_packed = join(
-        kv_other, out_other, down_sent, *gate_up_packed
-    )
+    kv_other, out_other, *gate_up_packed = join(kv_other, out_other, *gate_up_packed)
     attended, logs = attend(flat_ids, row_ids, col_ids, queries, kv_own, kv_other)
     gate_up_first = [send(part, ROUND[i]) for i, part in enumerate(gate_up_packed)]
-    down_mine = send(down_sent, OTHER_HALF)
-    attended, logs, down_mine, *gate_up_first = join(attended, logs, down_mine, *gate_up_first)
+    attended, logs, *gate_up_first = join(attended, logs, *gate_up_first)
     out_own = jnp.concatenate(
         [
             pick(core_is_one, out_got, out_other),
@@ -1225,91 +1250,84 @@
     out_keep, out_got = over_cores(
         contract(attended, grad_branch_rows, 0, 0)[:NARROW].reshape(2, rows_d, D)
     )
-    grad_attended, feed_got, out_got = join(grad_attended, feed_got, out_got)
-    feed_mine = feed_keep + feed_got
+    grad_attended, out_got = join(grad_attended, out_got)
     out_total = (out_keep + out_got.astype(F32)).astype(BF)
-    grad_attended, feed_mine, out_total, result_bf = join(
-        grad_attended, feed_mine, out_total, result.astype(BF)
-    )
+    grad_attended, out_total, result_bf = join(grad_attended, out_total, result.astype(BF))
     grad_queries, kv_grad_own, kv_grad_away = attend_back(
         flat_ids, row_ids, col_ids, queries, grad_attended, attended, logs, kv_own, kv_other,
         cosine, sine,
     )
-    feed_home = send(feed_mine, HOME_HALF)
     out_far = send(out_total, OTHER_X)
     result_home = send(result_bf, SPREAD)
-    grad_queries, kv_grad_own, kv_grad_away, feed_home, out_far, result_home = join(
-        grad_queries, kv_grad_own, kv_grad_away, feed_home, out_far, result_home
+    vector_part = jnp.concatenate(
+        [grad_gain_one, grad_bias_one, grad_gain_two, grad_bias_two]
+        + [jnp.zeros((4, D), F32)], axis=0
+    )
+    grad_queries, kv_grad_own, kv_grad_away, feed_got, out_far, result_home = join(
+        grad_queries, kv_grad_own, kv_grad_away, feed_got, out_far, result_home
     )
     kv_grad_got = send(kv_grad_away, OTHER_CORE)
+    feed_mine = feed_keep + feed_got
+    out_total = (out_total.astype(F32) + out_far.astype(F32)).astype(BF)
+    kv_grad_got, feed_mine, out_total = join(kv_grad_got, feed_mine, out_total)
+    feed_home = send(feed_mine, HOME_HALF)
+    out_got = send(out_total, OTHER_HALF)
+
+    grad_projected, qkv_keep, qkv_away = grad_qkv(
+        c.reshape(1), x_rows, grad_queries, kv_grad_own, kv_grad_got, cosine, sine, vector_part
+    )
+    moved_rows = D // 4 + 16
+    qkv_got = send(qkv_away, OTHER_CORE)
+    input_parts = square_parts(grad_projected, qkv_own, 1)
+    qkv_got, *input_parts = join(qkv_got, *input_parts)
+
+    input_sum = reduce_square(grad_projected, qkv_own, 1, input_parts)
+    qkv_keep, qkv_away = whole_call(
+        split_x_kernel, "split_x", [((moved_rows, 3 * WIDE), BF)] * 2, x_flag,
+        qkv_keep, vector_part, qkv_got,
+    )
+    qkv_mine, feed_home = join(qkv_keep + send(qkv_away, OTHER_X), feed_home)
+    qkv_home = send(qkv_mine, HOME_HALF)
     feed_kept, *feed_sends = whole_call(
         square_feed_kernel, "square_feed",
         [((GROUP + 2, quarter, D), BF)] + [((2, quarter, D), BF)] * 3,
         step_square, feed_mine, feed_home,
     )
-    out_total = (out_total.astype(F32) + out_far.astype(F32)).astype(BF)
-    kv_grad_got, out_total, *feed_sends = join(kv_grad_got, out_total, *feed_sends)
     feed_gots = [send(part, HOME_SQUARE[k + 1]) for k, part in enumerate(feed_sends)]
-    out_got = send(out_total, OTHER_HALF)
-    grad_projected = join_grads(grad_queries, kv_grad_own, kv_grad_got, cosine, sine)
-
-    qkv_part = contract(x_rows, grad_projected, 0, 0).reshape(2, D // 2, 3 * WIDE)
-    vector_part = jnp.concatenate(
-        [grad_gain_one, grad_bias_one, grad_gain_two, grad_bias_two]
-        + [jnp.zeros((4, D), F32)], axis=0
-    )
-    moved_rows = D // 4 + 16
-    (qkv_away,) = whole_call(
-        split_cores_kernel, "split_cores", [((D // 2 + 16, 3 * WIDE), BF)], c.reshape(1),
-        qkv_part, vector_part,
-    )
-    qkv_away, out_got, *feed_gots = join(qkv_away, out_got, *feed_gots)
-    qkv_got = send(qkv_away, OTHER_CORE)
-    (feed_bundle,) = whole_call(
-        join_feed_kernel, "join_feed", [bundle_shape], step_square, feed_kept, *feed_gots
-    )
-    qkv_got, feed_bundle, out_total = join(qkv_got, feed_bundle, out_total + out_got)
-    qkv_keep, qkv_away = whole_call(
-        split_x_kernel, "split_x", [((moved_rows, 3 * WIDE), BF)] * 2, jnp.stack([c, x]),
-        qkv_part, vector_part, qkv_got,
-    )
-    grad_projected, qkv_away = join(grad_projected, qkv_away)
-    qkv_got = send(qkv_away, OTHER_X)
-    input_parts = square_parts(grad_projected, qkv_own, 1)
-    input_parts = join(*input_parts)
-
-    input_sum = reduce_square(grad_projected, qkv_own, 1, input_parts)
-    qkv_mine = qkv_keep + qkv_got
-    qkv_home = send(qkv_mine, HOME_HALF)
-    feed_other = send(feed_bundle, HOME_X)
-    feed_far = send(feed_bundle, HOME_CORE)
-    grad_w_out = send(out_total, OUT_RETURN)
-    inputs_back, qkv_home, feed_other, feed_far, grad_w_out = join(
-        (grad_res + input_sum).astype(BF), qkv_home, feed_other, feed_far, grad_w_out
+    inputs_back, qkv_home, out_got, *feed_gots = join(
+        (grad_res + input_sum).astype(BF), qkv_home, out_got, *feed_gots
     )
     grad_inputs_home = send(inputs_back, SPREAD)
-    feed_far_other = send(feed_other, HOME_CORE)
+    grad_w_out = send(out_total + out_got, OUT_RETURN)
     qkv_sends = whole_call(
         square_qkv_kernel, "square_qkv", [((quarter + 16, 3 * WIDE), BF)] * GROUP,
         step_square, qkv_mine, qkv_home,
     )
-    feed_far_other, *qkv_sends = join(feed_far_other, *qkv_sends)
+    feed_kept, *qkv_sends = join(feed_kept, *qkv_sends)
     qkv_gots = [qkv_sends[0]] + [send(qkv_sends[k], HOME_SQUARE[k]) for k in range(1, GROUP)]
+    (feed_bundle,) = whole_call(
+        join_feed_kernel, "join_feed", [bundle_shape], step_square, feed_kept, *feed_gots
+    )
+    feed_other = send(feed_bundle, HOME_X)
+    feed_far = send(feed_bundle, OTHER_CORE)
+    grad_inputs_home, grad_w_out, feed_other, feed_far, *qkv_gots = join(
+        grad_inputs_home, grad_w_out, feed_other, feed_far, *qkv_gots
+    )
+    feed_far_other = send(feed_other, OTHER_CORE)
     grad_w_down, grad_w_gate, grad_w_up = whole_call(
         finish_feed_kernel, "finish_feed",
         [(by_x_rows + (D,), F32)] + [((2, quarter, w_gate.shape[1]), F32)] * 2,
         home_flags, feed_bundle, feed_other, feed_far, feed_far_other,
     )
-    grad_inputs_home, grad_w_down, grad_w_gate, grad_w_up, *qkv_gots = join(
-        grad_inputs_home, grad_w_down, grad_w_gate, grad_w_up, *qkv_gots
-    )
     (qkv_bundle,) = whole_call(
         join_qkv_kernel, "join_qkv", [((moved_rows, 3 * WIDE), BF)], step_square, *qkv_gots
     )
-    qkv_other = send(qkv_bundle, HOME_X)
+    qkv_other, grad_w_down, grad_w_gate, grad_w_up = join(
+        send(qkv_bundle, HOME_X), grad_w_down, grad_w_gate, grad_w_up
+    )
     grad_w_qkv, vector_grads = whole_call(
         finish_qkv_kernel, "finish_qkv", [((2, quarter, 3 * D), F32), ((8, D), F32)],
-        home_flags, qkv_bundle, qkv_other, send(qkv_bundle, HOME_CORE), send(qkv_other, HOME_CORE),
+        home_flags, qkv_bundle, qkv_other, send(qkv_bundle, OTHER_CORE), send(qkv_other, OTHER_CORE),
     )
     vector_grads = lax.dynamic_slice_in_dim(vector_grads, shard * rows_d, rows_d, 1)
 

time: 386 us -> 386 us (level)
  waiting for transfers between devices: 110 us -> 133 us
  starting transfers between devices: 113 us -> 95.2 us
  Pallas kernels: 89.4 us -> 82.8 us
    ppermute x67, waiting for transfers between devices: 110 us -> 133 us  [send(): return lax.ppermute(value, AXES, pairs)]
    ppermute x67, starting transfers between devices: 113 us -> 95.2 us  [send(): return lax.ppermute(value, AXES, pairs)]
    pallas_call x1, Pallas kernels: 29.4 us -> 25.3 us  [attend_back(): pl.pallas_call(attend_back_kernel, grid_spec=pltpu.PrefetchScalarGridSpec...]
    pallas_call x9 -> x8, Pallas kernels: 24.1 us -> 21 us  [whole_call(): pl.pallas_call(kernel, in_specs=[pl.BlockSpec(memory_space=pltpu.SMEM)] +...]
    unnamed x96 -> x90, local copies, waits for them, and re-layouts: 7.04 us -> 8.05 us
    dot_general x23 -> x22, matrix products: 28.7 us -> 28.7 us  [contract(): lax.dot_general(left, right, (((left_dim,), (right_dim,)), ((), ())), pre...]
  transfers between devices with their start and end apart: 67 -> 67, of which waited for: 24 -> 29; matrix products, arithmetic and copies ran while one was open for 10% -> 11% of each run, Pallas kernels for 19% -> 15%
where the time goes in v4:
time: 386 us; the launch traced here: 383 us
  waiting for transfers between devices  133 us (34%)
  starting transfers between devices  95.2 us (25%)
  Pallas kernels  82.8 us (21%)
  matrix products  28.7 us (7%)
  other arithmetic  27.2 us (7%)
  local copies, waits for them, and re-layouts  13.6 us (4%)
    ppermute x67, waiting for transfers between devices, send(): return lax.ppermute(value, AXES, pairs)  133 us
    ppermute x67, starting transfers between devices, send(): return lax.ppermute(value, AXES, pairs)  95.2 us
    dot_general x22, matrix products, contract(): lax.dot_general(left, right, (((left_dim,), (right_dim,)), ((), ())), pre...  28.7 us
    pallas_call x1, Pallas kernels, attend_back(): pl.pallas_call(attend_back_kernel, grid_spec=pltpu.PrefetchScalarGridSpec...  25.3 us
    pallas_call x8, Pallas kernels, whole_call(): pl.pallas_call(kernel, in_specs=[pl.BlockSpec(memory_space=pltpu.SMEM)] +...  21 us
    pallas_call x1, Pallas kernels, attend(): pl.pallas_call(attend_kernel, grid_spec=pltpu.PrefetchScalarGridSpec(num_...  14 us
    unnamed x90, local copies, waits for them, and re-layouts  8.05 us
  transfers between devices with their start and end apart: 67, of which 29 were waited for; matrix products, arithmetic and copies ran while one was open for 11% of the time, Pallas kernels for 15%

profile of v4, /device:TPU:0, one launch (start us, length us, event | category | flops | bytes accessed | tf_op | source)
XLA Modules:
  0.0 382.8 jit_solution(2682685617190243577)
XLA Ops:
  14.6 3.8 collective-permute-start.3
  20.2 6.3 %collective-permute-start.5 = (bf16[256,768]{1,0:T(8,128)(2,1)S(1)}, bf16[256,768]{1,0:T(8,128)(2,1)S(1)}, u32[]{:S(2)}, u32[]{:S(2)}) collective-permute-start(bf16[256,768]{1,0:T(8,128)(2,1)S(1)} %collective-permute-done.2), channel_id=1, source_target_pairs={{0,1},{1,0},{2,3},{3,2},{4,5},{5,4},{6,7},{7,6},{8,9},{9,8},{10,11... | collective-permute-start | bytes 1179656 | tf_op jit(solution)/shard_map/ppermute | solution.py:412
  28.2 6.7 %collective-permute-start.4 = (bf16[4,96,580]{2,1,0:T(8,128)(2,1)S(1)}, bf16[4,96,580]{2,1,0:T(8,128)(2,1)S(1)}, u32[]{:S(2)}, u32[]{:S(2)}) collective-permute-start(bf16[4,96,580]{2,1,0:T(8,128)(2,1)S(1)} %constant_dynamic-update-slice_fusion.near_ref), channel_id=1, source_target_pairs={{0,8},{1,9},{2,10},{3,11},{4,12},{5,13},{6,14},{7,15},{8,0},{9,1},... | collective-permute-start | bytes 1336328 | tf_op jit(solution)/shard_map/ppermute | solution.py:412
  39.0 3.1 multiply_sine_fusion
  47.4 4.7 %collective-permute-done.10 = bf16[96,768]{1,0:T(8,128)(2,1)} collective-permute-done((bf16[96,768]{1,0:T(8,128)(2,1)S(1)}, bf16[96,768]{1,0:T(8,128)(2,1)}, u32[]{:S(2)}, u32[]{:S(2)}) %collective-permute-start.10) | collective-permute-done | bytes 147488 | tf_op jit(solution)/shard_map/ppermute | solution.py:412
  52.1 5.4 %project.1 = (bf16[1024,256]{1,0:T(8,128)(2,1)}, bf16[1024,512]{1,0:T(8,128)(2,1)}) custom-call(bf16[1024,768]{1,0:T(8,128)(2,1)} %pad_maximum_fusion.1.x_ref, bf16[768,768]{1,0:T(8,128)(2,1)} %bitcast.83, f32[1024,128]{1,0:T(8,128)} %get-tuple-element.156.cos_ref, f32[1024,128]{1,0:T(8,128)} %get-tuple-element.157.sin_ref), custom_call_target="tpu_custom_call" | custom-call | flops 1207959552 | bytes 5373952 | tf_op jit(solution)/shard_map/project/pallas_call | solution.py:453
  63.1 14.0 %attend.1 = (bf16[1024,256]{1,0:T(8,128)(2,1)}, f32[8,1024]{1,0:T(8,128)}) custom-call(s32[2048]{0:T(1024)} %bitcast.98, s32[8,1,256]{2,1,0:T(1,128)} %reshape.183.row_ids_ref, s32[2048,1]{1,0:T(8,128)} %copy.43.col_ids_ref, bf16[1024,256]{1,0:T(8,128)(2,1)} %get-tuple-element.158.q_ref, bf16[1024,512]{1,0:T(8,128)(2,1)} %get-tuple-element.159.own_ref, ...), custom_call_target="tpu_custom_call" | custom-call | flops 6442450944 | bytes 3145728 | tf_op jit(solution)/shard_map/attend/pallas_call | solution.py:565
  85.7 4.5 %collective-permute-start.18 = (bf16[2,96,1536]{2,1,0:T(8,128)(2,1)S(1)}, bf16[2,96,1536]{2,1,0:T(8,128)(2,1)S(1)}, u32[]{:S(2)}, u32[]{:S(2)}) collective-permute-start(bf16[2,96,1536]{2,1,0:T(8,128)(2,1)S(1)} %pad_maximum_fusion.4), channel_id=1, source_target_pairs={{0,16},{1,17},{2,18},{3,19},{4,20},{5,21},{6,22},{7,23},{8,24},{9,... | collective-permute-start | bytes 1769480 | tf_op jit(solution)/shard_map/ppermute | solution.py:412
  94.9 8.5 %collective-permute-done.17 = bf16[256,768]{1,0:T(8,128)(2,1)} collective-permute-done((bf16[256,768]{1,0:T(8,128)(2,1)}, bf16[256,768]{1,0:T(8,128)(2,1)}, u32[]{:S(2)}, u32[]{:S(2)}) %collective-permute-start.17) | collective-permute-done | bytes 393248 | tf_op jit(solution)/shard_map/ppermute | solution.py:412
  109.2 7.4 %collective-permute-done.20 = bf16[256,768]{1,0:T(8,128)(2,1)S(1)} collective-permute-done((bf16[256,768]{1,0:T(8,128)(2,1)S(1)}, bf16[256,768]{1,0:T(8,128)(2,1)S(1)}, u32[]{:S(2)}, u32[]{:S(2)}) %collective-permute-start.20) | collective-permute-done | bytes 393248 | tf_op jit(solution)/shard_map/ppermute | solution.py:412
  118.9 7.4 %collective-permute-done.22 = bf16[256,768]{1,0:T(8,128)(2,1)S(1)} collective-permute-done((bf16[256,768]{1,0:T(8,128)(2,1)S(1)}, bf16[256,768]{1,0:T(8,128)(2,1)S(1)}, u32[]{:S(2)}, u32[]{:S(2)}) %collective-permute-start.22) | collective-permute-done | bytes 393248 | tf_op jit(solution)/shard_map/ppermute | solution.py:412
  127.7 3.2 unpack.1
  130.9 4.3 %fusion.49 = f32[1024,1536]{1,0:T(8,128)S(1)} fusion(bf16[1024,768]{1,0:T(8,128)(2,1)S(1)} %constant_dynamic-update-slice_fusion.2, bf16[768,1536]{1,0:T(8,128)(2,1)} %bitcast.76), kind=kOutput, calls=%fused_computation.167 | convolution fusion | flops 2415919104 | bytes 10223616 | tf_op jit(solution)/shard_map/dot_general | solution.py:489
  142.8 6.2 %collective-permute-done.25 = bf16[256,768]{1,0:T(8,128)(2,1)S(1)} collective-permute-done((bf16[256,768]{1,0:T(8,128)(2,1)S(1)}, bf16[256,768]{1,0:T(8,128)(2,1)S(1)}, u32[]{:S(2)}, u32[]{:S(2)}) %collective-permute-start.25) | collective-permute-done | bytes 393248 | tf_op jit(solution)/shard_map/ppermute | solution.py:412
  149.0 6.5 %collective-permute-done.26 = bf16[256,768]{1,0:T(8,128)(2,1)S(1)} collective-permute-done((bf16[256,768]{1,0:T(8,128)(2,1)S(1)}, bf16[256,768]{1,0:T(8,128)(2,1)S(1)}, u32[]{:S(2)}, u32[]{:S(2)}) %collective-permute-start.26) | collective-permute-done | bytes 393248 | tf_op jit(solution)/shard_map/ppermute | solution.py:412
  155.5 6.3 %collective-permute-done.27 = bf16[256,768]{1,0:T(8,128)(2,1)S(1)} collective-permute-done((bf16[256,768]{1,0:T(8,128)(2,1)S(1)}, bf16[256,768]{1,0:T(8,128)(2,1)S(1)}, u32[]{:S(2)}, u32[]{:S(2)}) %collective-permute-start.27) | collective-permute-done | bytes 393248 | tf_op jit(solution)/shard_map/ppermute | solution.py:412
  167.6 5.4 %collective-permute-done.29 = bf16[256,768]{1,0:T(8,128)(2,1)S(1)} collective-permute-done((bf16[256,768]{1,0:T(8,128)(2,1)S(1)}, bf16[256,768]{1,0:T(8,128)(2,1)S(1)}, u32[]{:S(2)}, u32[]{:S(2)}) %collective-permute-start.29) | collective-permute-done | bytes 393248 | tf_op jit(solution)/shard_map/ppermute | solution.py:412
  173.0 4.5 %collective-permute-done.30 = bf16[256,768]{1,0:T(8,128)(2,1)S(1)} collective-permute-done((bf16[256,768]{1,0:T(8,128)(2,1)S(1)}, bf16[256,768]{1,0:T(8,128)(2,1)S(1)}, u32[]{:S(2)}, u32[]{:S(2)}) %collective-permute-start.30) | collective-permute-done | bytes 393248 | tf_op jit(solution)/shard_map/ppermute | solution.py:412
  177.5 8.5 %collective-permute-done.31 = bf16[256,768]{1,0:T(8,128)(2,1)S(1)} collective-permute-done((bf16[256,768]{1,0:T(8,128)(2,1)S(1)}, bf16[256,768]{1,0:T(8,128)(2,1)S(1)}, u32[]{:S(2)}, u32[]{:S(2)}) %collective-permute-start.31) | collective-permute-done | bytes 393248 | tf_op jit(solution)/shard_map/ppermute | solution.py:412
  204.8 7.7 %collective-permute-done.34 = bf16[256,768]{1,0:T(8,128)(2,1)S(1)} collective-permute-done((bf16[256,768]{1,0:T(8,128)(2,1)S(1)}, bf16[256,768]{1,0:T(8,128)(2,1)S(1)}, u32[]{:S(2)}, u32[]{:S(2)}) %collective-permute-start.34) | collective-permute-done | bytes 393248 | tf_op jit(solution)/shard_map/ppermute | solution.py:412
  218.6 4.0 %split_feed.1 = (bf16[12,48,768]{2,1,0:T(8,128)(2,1)}, bf16[12,48,768]{2,1,0:T(8,128)(2,1)}) custom-call(s32[1]{0:T(128)} %bitcast.20.x_ref.flag_ref, f32[4,2,48,768]{3,2,1,0:T(8,128)} %bitcast.82, bf16[4,2,48,768]{3,2,1,0:T(8,128)(2,1)} %bitcast.89, f32[4,2,48,1536]{3,2,1,0:T(8,128)} %bitcast.81, bf16[4,2,48,1536]{3,2,1,0:T(8,128)(2,1)} %bitcast.88), custom_call_target="tpu_custom_call" | custom-call | flops 1769472 | bytes 10616832 | tf_op jit(solution)/shard_map/split_feed/pallas_call | solution.py:936
  227.6 5.7 %collective-permute-done.39 = bf16[256,768]{1,0:T(8,128)(2,1)S(1)} collective-permute-done((bf16[256,768]{1,0:T(8,128)(2,1)S(1)}, bf16[256,768]{1,0:T(8,128)(2,1)S(1)}, u32[]{:S(2)}, u32[]{:S(2)}) %collective-permute-start.39) | collective-permute-done | bytes 393248 | tf_op jit(solution)/shard_map/ppermute | solution.py:412
  236.6 25.3 %attend_back.1 = (bf16[1024,256]{1,0:T(8,128)(2,1)}, f32[1024,512]{1,0:T(8,128)}, bf16[1024,512]{1,0:T(8,128)(2,1)}) custom-call(s32[2048]{0:T(1024)} %bitcast.99, s32[8,1,256]{2,1,0:T(1,128)} %reshape.183.row_ids_ref, s32[2048,1]{1,0:T(8,128)} %copy.43.col_ids_ref, bf16[1024,256]{1,0:T(8,128)(2,1)} %get-tuple-element.158.q_ref, ...), custom_call_target="tpu_custom_call" | custom-call | flops 16106127360 | bytes 3145728 | tf_op jit(solution)/shard_map/attend_back/pallas_call | solution.py:703
  266.6 7.3 %grad_qkv.1 = (bf16[1024,768]{1,0:T(8,128)(2,1)}, f32[384,768]{1,0:T(8,128)}, bf16[400,768]{1,0:T(8,128)(2,1)}) custom-call(s32[1]{0:T(128)} %bitcast.26.c_ref, bf16[1024,768]{1,0:T(8,128)(2,1)} %pad_maximum_fusion.1.x_ref, bf16[1024,256]{1,0:T(8,128)(2,1)} %get-tuple-element.201.dq_ref, f32[1024,512]{1,0:T(8,128)} %get-tuple-element.202.own_ref, ...), custom_call_target="tpu_custom_call" | custom-call | flops 1207959552 | bytes 5767168 | tf_op jit(solution)/shard_map/grad_qkv/pallas_call | solution.py:780
  282.8 6.1 %collective-permute-start.49 = (bf16[208,768]{1,0:T(8,128)(2,1)}, bf16[208,768]{1,0:T(8,128)(2,1)S(1)}, u32[]{:S(2)}, u32[]{:S(2)}) collective-permute-start(bf16[208,768]{1,0:T(8,128)(2,1)} %get-tuple-element.216), channel_id=1, source_target_pairs={{0,16},{1,17},{2,18},{3,19},{4,20},{5,21},{6,22},{7,23},{8,24},{9,... | collective-permute-start | bytes 958472 | tf_op jit(solution)/shard_map/ppermute | solution.py:412
  295.3 9.2 %collective-permute-done.50.got_ref = bf16[12,48,768]{2,1,0:T(8,128)(2,1)} collective-permute-done((bf16[12,48,768]{2,1,0:T(8,128)(2,1)S(1)}, bf16[12,48,768]{2,1,0:T(8,128)(2,1)}, u32[]{:S(2)}, u32[]{:S(2)}) %collective-permute-start.50) | collective-permute-done | bytes 884768 | tf_op jit(solution)/shard_map/ppermute | solution.py:412
  307.3 4.3 %collective-permute-start.52 = (bf16[96,768]{1,0:T(8,128)(2,1)S(1)}, bf16[96,768]{1,0:T(8,128)(2,1)S(1)}, u32[]{:S(2)}, u32[]{:S(2)}) collective-permute-start(bf16[96,768]{1,0:T(8,128)(2,1)S(1)} %add_convert_fusion.2), channel_id=1, source_target_pairs={{0,4},{1,5},{2,6},{3,7},{4,0},{5,1},{6,2},{7,3},{8,12},{9,13},{10,... | collective-permute-start | bytes 442376 | tf_op jit(solution)/shard_map/ppermute | solution.py:412
  318.2 7.5 %collective-permute-done.48 = bf16[256,768]{1,0:T(8,128)(2,1)} collective-permute-done((bf16[256,768]{1,0:T(8,128)(2,1)}, bf16[256,768]{1,0:T(8,128)(2,1)}, u32[]{:S(2)}, u32[]{:S(2)}) %collective-permute-start.48) | collective-permute-done | bytes 393248 | tf_op jit(solution)/shard_map/ppermute | solution.py:412
  329.1 4.7 %collective-permute-done.55.refs_2_ = bf16[2,48,768]{2,1,0:T(8,128)(2,1)S(1)} collective-permute-done((bf16[2,48,768]{2,1,0:T(8,128)(2,1)}, bf16[2,48,768]{2,1,0:T(8,128)(2,1)S(1)}, u32[]{:S(2)}, u32[]{:S(2)}) %collective-permute-start.55) | collective-permute-done | bytes 147488 | tf_op jit(solution)/shard_map/ppermute | solution.py:412
  347.9 8.5 %collective-permute-done.61.refs_2_ = bf16[64,768]{1,0:T(8,128)(2,1)S(1)} collective-permute-done((bf16[64,768]{1,0:T(8,128)(2,1)}, bf16[64,768]{1,0:T(8,128)(2,1)S(1)}, u32[]{:S(2)}, u32[]{:S(2)}) %collective-permute-start.61) | collective-permute-done | bytes 98336 | tf_op jit(solution)/shard_map/ppermute | solution.py:412
  358.3 5.7 %collective-permute-done.62.refs_3_ = bf16[64,768]{1,0:T(8,128)(2,1)S(1)} collective-permute-done((bf16[64,768]{1,0:T(8,128)(2,1)}, bf16[64,768]{1,0:T(8,128)(2,1)S(1)}, u32[]{:S(2)}, u32[]{:S(2)}) %collective-permute-start.62) | collective-permute-done | bytes 98336 | tf_op jit(solution)/shard_map/ppermute | solution.py:412
  369.9 4.0 %finish_feed.1 = (f32[4,2,48,768]{3,2,1,0:T(8,128)}, f32[2,48,3072]{2,1,0:T(8,128)}, f32[2,48,3072]{2,1,0:T(8,128)}) custom-call(s32[2]{0:T(128)} %pad_add_fusion.3.flag_ref, bf16[12,48,768]{2,1,0:T(8,128)(2,1)} %join_feed.1.own_ref, bf16[12,48,768]{2,1,0:T(8,128)(2,1)} %copy-done.10, bf16[12,48,768]{2,1,0:T(8,128)(2,1)} %copy-done.11, ...), custom_call_target="tpu_custom_call" | custom-call | flops 1769472 | bytes 7077888 | tf_op jit(solution)/shard_map/finish_feed/pallas_call | solution.py:936
  (308 shorter events, 163.8 us)
Async XLA Ops:
  12.3 35.1 %collective-permute-start.8 = (bf16[96,768]{1,0:T(8,128)(2,1)}, bf16[96,768]{1,0:T(8,128)(2,1)S(1)}, u32[]{:S(2)}, u32[]{:S(2)}) collective-permute-start(bf16[96,768]{1,0:T(8,128)(2,1)} %param.15), channel_id=1, source_target_pairs={{0,0},{1,8},{2,1},{3,9},{4,2},{5,10},{6,3},{7,11},{8,4},{9,12},{10... | collective-permute-start | bytes 442376 | tf_op jit(solution)/shard_map/ppermute | solution.py:412
  20.2 25.9 %collective-permute-start.5 = (bf16[256,768]{1,0:T(8,128)(2,1)S(1)}, bf16[256,768]{1,0:T(8,128)(2,1)S(1)}, u32[]{:S(2)}, u32[]{:S(2)}) collective-permute-start(bf16[256,768]{1,0:T(8,128)(2,1)S(1)} %collective-permute-done.2), channel_id=1, source_target_pairs={{0,1},{1,0},{2,3},{3,2},{4,5},{5,4},{6,7},{7,6},{8,9},{9,8},{10,11... | collective-permute-start | bytes 1179656 | tf_op jit(solution)/shard_map/ppermute | solution.py:412
  26.5 19.6 %collective-permute-start.6 = (bf16[256,768]{1,0:T(8,128)(2,1)S(1)}, bf16[256,768]{1,0:T(8,128)(2,1)S(1)}, u32[]{:S(2)}, u32[]{:S(2)}) collective-permute-start(bf16[256,768]{1,0:T(8,128)(2,1)S(1)} %collective-permute-done.2), channel_id=1, source_target_pairs={{0,2},{1,3},{2,0},{3,1},{4,6},{5,7},{6,4},{7,5},{8,10},{9,11},{10,... | collective-permute-start | bytes 1179656 | tf_op jit(solution)/shard_map/ppermute | solution.py:412
  27.1 19.1 %collective-permute-start.7 = (bf16[256,768]{1,0:T(8,128)(2,1)S(1)}, bf16[256,768]{1,0:T(8,128)(2,1)S(1)}, u32[]{:S(2)}, u32[]{:S(2)}) collective-permute-start(bf16[256,768]{1,0:T(8,128)(2,1)S(1)} %collective-permute-done.2), channel_id=1, source_target_pairs={{0,3},{1,2},{2,1},{3,0},{4,7},{5,6},{6,5},{7,4},{8,11},{9,10},{10,... | collective-permute-start | bytes 1179656 | tf_op jit(solution)/shard_map/ppermute | solution.py:412
  28.2 13.9 %collective-permute-start.4 = (bf16[4,96,580]{2,1,0:T(8,128)(2,1)S(1)}, bf16[4,96,580]{2,1,0:T(8,128)(2,1)S(1)}, u32[]{:S(2)}, u32[]{:S(2)}) collective-permute-start(bf16[4,96,580]{2,1,0:T(8,128)(2,1)S(1)} %constant_dynamic-update-slice_fusion.near_ref), channel_id=1, source_target_pairs={{0,8},{1,9},{2,10},{3,11},{4,12},{5,13},{6,14},{7,15},{8,0},{9,1},... | collective-permute-start | bytes 1336328 | tf_op jit(solution)/shard_map/ppermute | solution.py:412
  60.6 16.6 %collective-permute-start.13 = (bf16[96,1536]{1,0:T(8,128)(2,1)}, bf16[96,1536]{1,0:T(8,128)(2,1)S(1)}, u32[]{:S(2)}, u32[]{:S(2)}) collective-permute-start(bf16[96,1536]{1,0:T(8,128)(2,1)} %get-tuple-element.166), channel_id=1, source_target_pairs={{0,0},{1,1},{2,2},{3,3},{4,4},{5,5},{6,6},{7,7},{8,12},{9,13},{10,... | collective-permute-start | bytes 884744 | tf_op jit(solution)/shard_map/ppermute | solution.py:412
  62.4 14.8 %collective-permute-start.14 = (bf16[96,1536]{1,0:T(8,128)(2,1)}, bf16[96,1536]{1,0:T(8,128)(2,1)S(1)}, u32[]{:S(2)}, u32[]{:S(2)}) collective-permute-start(bf16[96,1536]{1,0:T(8,128)(2,1)} %get-tuple-element.167), channel_id=1, source_target_pairs={{0,1},{1,0},{2,3},{3,2},{4,5},{5,4},{6,7},{7,6},{8,13},{9,12},{10,... | collective-permute-start | bytes 884744 | tf_op jit(solution)/shard_map/ppermute | solution.py:412
  83.3 20.1 %collective-permute-start.17 = (bf16[256,768]{1,0:T(8,128)(2,1)}, bf16[256,768]{1,0:T(8,128)(2,1)}, u32[]{:S(2)}, u32[]{:S(2)}) collective-permute-start(bf16[256,768]{1,0:T(8,128)(2,1)} %convolution_convert_fusion.10), channel_id=1, source_target_pairs={{0,3},{1,2},{2,1},{3,0},{4,7},{5,6},{6,5},{7,4},{8,11},{9,10},{10,... | collective-permute-start | bytes 1179656 | tf_op jit(solution)/shard_map/ppermute | solution.py:412
  85.7 19.7 %collective-permute-start.18 = (bf16[2,96,1536]{2,1,0:T(8,128)(2,1)S(1)}, bf16[2,96,1536]{2,1,0:T(8,128)(2,1)S(1)}, u32[]{:S(2)}, u32[]{:S(2)}) collective-permute-start(bf16[2,96,1536]{2,1,0:T(8,128)(2,1)S(1)} %pad_maximum_fusion.4), channel_id=1, source_target_pairs={{0,16},{1,17},{2,18},{3,19},{4,20},{5,21},{6,22},{7,23},{8,24},{9,... | collective-permute-start | bytes 1769480 | tf_op jit(solution)/shard_map/ppermute | solution.py:412
  90.2 15.2 %collective-permute-start.19 = (bf16[96,768]{1,0:T(8,128)(2,1)}, bf16[96,768]{1,0:T(8,128)(2,1)S(1)}, u32[]{:S(2)}, u32[]{:S(2)}) collective-permute-start(bf16[96,768]{1,0:T(8,128)(2,1)} %collective-permute-done.10), channel_id=1, source_target_pairs={{0,16},{1,17},{2,18},{3,19},{4,20},{5,21},{6,22},{7,23},{8,24},{9,... | collective-permute-start | bytes 442376 | tf_op jit(solution)/shard_map/ppermute | solution.py:412
  107.4 18.9 %collective-permute-start.22 = (bf16[256,768]{1,0:T(8,128)(2,1)S(1)}, bf16[256,768]{1,0:T(8,128)(2,1)S(1)}, u32[]{:S(2)}, u32[]{:S(2)}) collective-permute-start(bf16[256,768]{1,0:T(8,128)(2,1)S(1)} %fusion.17), channel_id=1, source_target_pairs={{0,3},{1,2},{2,1},{3,0},{4,7},{5,6},{6,5},{7,4},{8,11},{9,10},{10,... | collective-permute-start | bytes 1179656 | tf_op jit(solution)/shard_map/ppermute | solution.py:412
  109.1 18.6 %collective-permute-start.23 = (bf16[4,96,1536]{2,1,0:T(8,128)(2,1)S(1)}, bf16[4,96,1536]{2,1,0:T(8,128)(2,1)}, u32[]{:S(2)}, u32[]{:S(2)}) collective-permute-start(bf16[4,96,1536]{2,1,0:T(8,128)(2,1)S(1)} %constant_dynamic-update-slice_fusion.6.near_ref), channel_id=1, source_target_pairs={{0,8},{1,9},{2,10},{3,11},{4,12},{5,13},{6,14},{7,15},{8,0},{9,1},... | collective-permute-start | bytes 3538952 | tf_op jit(solution)/shard_map/ppermute | solution.py:412
  139.3 16.2 %collective-permute-start.26 = (bf16[256,768]{1,0:T(8,128)(2,1)S(1)}, bf16[256,768]{1,0:T(8,128)(2,1)S(1)}, u32[]{:S(2)}, u32[]{:S(2)}) collective-permute-start(bf16[256,768]{1,0:T(8,128)(2,1)S(1)} %convolution_convert_fusion.8), channel_id=1, source_target_pairs={{0,2},{1,3},{2,0},{3,1},{4,6},{5,7},{6,4},{7,5},{8,10},{9,11},{10,... | collective-permute-start | bytes 1179656 | tf_op jit(solution)/shard_map/ppermute | solution.py:412
  139.7 22.0 %collective-permute-start.27 = (bf16[256,768]{1,0:T(8,128)(2,1)S(1)}, bf16[256,768]{1,0:T(8,128)(2,1)S(1)}, u32[]{:S(2)}, u32[]{:S(2)}) collective-permute-start(bf16[256,768]{1,0:T(8,128)(2,1)S(1)} %convolution_convert_fusion.7), channel_id=1, source_target_pairs={{0,3},{1,2},{2,1},{3,0},{4,7},{5,6},{6,5},{7,4},{8,11},{9,10},{10,... | collective-permute-start | bytes 1179656 | tf_op jit(solution)/shard_map/ppermute | solution.py:412
  141.9 20.6 %collective-permute-start.28 = (bf16[256,768]{1,0:T(8,128)(2,1)S(1)}, bf16[256,768]{1,0:T(8,128)(2,1)S(1)}, u32[]{:S(2)}, u32[]{:S(2)}) collective-permute-start(bf16[256,768]{1,0:T(8,128)(2,1)S(1)} %bitcast.111), channel_id=1, source_target_pairs={{0,0},{1,1},{2,2},{3,3},{4,8},{5,9},{6,10},{7,11},{8,4},{9,5},{10,... | collective-permute-start | bytes 1179656 | tf_op jit(solution)/shard_map/ppermute | solution.py:412
  165.5 20.5 %collective-permute-start.31 = (bf16[256,768]{1,0:T(8,128)(2,1)S(1)}, bf16[256,768]{1,0:T(8,128)(2,1)S(1)}, u32[]{:S(2)}, u32[]{:S(2)}) collective-permute-start(bf16[256,768]{1,0:T(8,128)(2,1)S(1)} %fusion.44), channel_id=1, source_target_pairs={{0,3},{1,2},{2,1},{3,0},{4,7},{5,6},{6,5},{7,4},{8,11},{9,10},{10,... | collective-permute-start | bytes 1179656 | tf_op jit(solution)/shard_map/ppermute | solution.py:412
  192.8 19.7 %collective-permute-start.34 = (bf16[256,768]{1,0:T(8,128)(2,1)S(1)}, bf16[256,768]{1,0:T(8,128)(2,1)S(1)}, u32[]{:S(2)}, u32[]{:S(2)}) collective-permute-start(bf16[256,768]{1,0:T(8,128)(2,1)S(1)} %convolution_convert_fusion.4), channel_id=1, source_target_pairs={{0,3},{1,2},{2,1},{3,0},{4,7},{5,6},{6,5},{7,4},{8,11},{9,10},{10,... | collective-permute-start | bytes 1179656 | tf_op jit(solution)/shard_map/ppermute | solution.py:412
  214.9 18.4 %collective-permute-start.39 = (bf16[256,768]{1,0:T(8,128)(2,1)S(1)}, bf16[256,768]{1,0:T(8,128)(2,1)S(1)}, u32[]{:S(2)}, u32[]{:S(2)}) collective-permute-start(bf16[256,768]{1,0:T(8,128)(2,1)S(1)} %get-tuple-element.187), channel_id=1, source_target_pairs={{0,3},{1,2},{2,1},{3,0},{4,7},{5,6},{6,5},{7,4},{8,11},{9,10},{10,... | collective-permute-start | bytes 1179656 | tf_op jit(solution)/shard_map/ppermute | solution.py:412
  222.7 39.2 %collective-permute-start.41 = (bf16[12,48,768]{2,1,0:T(8,128)(2,1)}, bf16[12,48,768]{2,1,0:T(8,128)(2,1)S(1)}, u32[]{:S(2)}, u32[]{:S(2)}) collective-permute-start(bf16[12,48,768]{2,1,0:T(8,128)(2,1)} %get-tuple-element.197), channel_id=1, source_target_pairs={{0,16},{1,17},{2,18},{3,19},{4,20},{5,21},{6,22},{7,23},{8,24},{9,... | collective-permute-start | bytes 2654216 | tf_op jit(solution)/shard_map/ppermute | solution.py:412
  235.8 26.1 %collective-permute-start.43 = (bf16[256,768]{1,0:T(8,128)(2,1)S(1)}, bf16[256,768]{1,0:T(8,128)(2,1)S(1)}, u32[]{:S(2)}, u32[]{:S(2)}) collective-permute-start(bf16[256,768]{1,0:T(8,128)(2,1)S(1)} %copy-done.23), channel_id=1, source_target_pairs={{0,0},{1,1},{2,2},{3,3},{4,8},{5,9},{6,10},{7,11},{8,4},{9,5},{10,... | collective-permute-start | bytes 1179656 | tf_op jit(solution)/shard_map/ppermute | solution.py:412
  236.5 25.4 %collective-permute-start.42 = (bf16[96,768]{1,0:T(8,128)(2,1)S(1)}, bf16[96,768]{1,0:T(8,128)(2,1)S(1)}, u32[]{:S(2)}, u32[]{:S(2)}) collective-permute-start(bf16[96,768]{1,0:T(8,128)(2,1)S(1)} %add_convert_fusion.3), channel_id=1, source_target_pairs={{0,16},{1,17},{2,18},{3,19},{4,20},{5,21},{6,22},{7,23},{8,24},{9,... | collective-permute-start | bytes 442376 | tf_op jit(solution)/shard_map/ppermute | solution.py:412
  274.2 30.3 %collective-permute-start.50 = (bf16[12,48,768]{2,1,0:T(8,128)(2,1)S(1)}, bf16[12,48,768]{2,1,0:T(8,128)(2,1)}, u32[]{:S(2)}, u32[]{:S(2)}) collective-permute-start(bf16[12,48,768]{2,1,0:T(8,128)(2,1)S(1)} %add.222.mine_ref), channel_id=1, source_target_pairs={{4,0},{5,1},{6,2},{7,3},{8,12},{9,13},{10,14},{11,15},{20,16},{21,... | collective-permute-start | bytes 2654216 | tf_op jit(solution)/shard_map/ppermute | solution.py:412
  288.9 25.1 %collective-permute-start.46 = (bf16[256,768]{1,0:T(8,128)(2,1)}, bf16[256,768]{1,0:T(8,128)(2,1)}, u32[]{:S(2)}, u32[]{:S(2)}) collective-permute-start(bf16[256,768]{1,0:T(8,128)(2,1)} %convolution_convert_fusion.3), channel_id=1, source_target_pairs={{0,1},{1,0},{2,3},{3,2},{4,5},{5,4},{6,7},{7,6},{8,9},{9,8},{10,11... | collective-permute-start | bytes 1179656 | tf_op jit(solution)/shard_map/ppermute | solution.py:412
  289.3 27.0 %collective-permute-start.47 = (bf16[256,768]{1,0:T(8,128)(2,1)}, bf16[256,768]{1,0:T(8,128)(2,1)}, u32[]{:S(2)}, u32[]{:S(2)}) collective-permute-start(bf16[256,768]{1,0:T(8,128)(2,1)} %convolution_convert_fusion.2), channel_id=1, source_target_pairs={{0,2},{1,3},{2,0},{3,1},{4,6},{5,7},{6,4},{7,5},{8,10},{9,11},{10,... | collective-permute-start | bytes 1179656 | tf_op jit(solution)/shard_map/ppermute | solution.py:412
  290.1 35.6 %collective-permute-start.48 = (bf16[256,768]{1,0:T(8,128)(2,1)}, bf16[256,768]{1,0:T(8,128)(2,1)}, u32[]{:S(2)}, u32[]{:S(2)}) collective-permute-start(bf16[256,768]{1,0:T(8,128)(2,1)} %convolution_convert_fusion.1), channel_id=1, source_target_pairs={{0,3},{1,2},{2,1},{3,0},{4,7},{5,6},{6,5},{7,4},{8,11},{9,10},{10,... | collective-permute-start | bytes 1179656 | tf_op jit(solution)/shard_map/ppermute | solution.py:412
  304.5 29.4 %collective-permute-start.51 = (bf16[208,768]{1,0:T(8,128)(2,1)S(1)}, bf16[208,768]{1,0:T(8,128)(2,1)}, u32[]{:S(2)}, u32[]{:S(2)}) collective-permute-start(bf16[208,768]{1,0:T(8,128)(2,1)S(1)} %add.228.mine_ref), channel_id=1, source_target_pairs={{4,0},{5,1},{6,2},{7,3},{8,12},{9,13},{10,14},{11,15},{20,16},{21,... | collective-permute-start | bytes 958472 | tf_op jit(solution)/shard_map/ppermute | solution.py:412
  307.3 21.8 %collective-permute-start.52 = (bf16[96,768]{1,0:T(8,128)(2,1)S(1)}, bf16[96,768]{1,0:T(8,128)(2,1)S(1)}, u32[]{:S(2)}, u32[]{:S(2)}) collective-permute-start(bf16[96,768]{1,0:T(8,128)(2,1)S(1)} %add_convert_fusion.2), channel_id=1, source_target_pairs={{0,4},{1,5},{2,6},{3,7},{4,0},{5,1},{6,2},{7,3},{8,12},{9,13},{10,... | collective-permute-start | bytes 442376 | tf_op jit(solution)/shard_map/ppermute | solution.py:412
  314.0 15.1 %collective-permute-start.53 = (bf16[2,48,768]{2,1,0:T(8,128)(2,1)}, bf16[2,48,768]{2,1,0:T(8,128)(2,1)S(1)}, u32[]{:S(2)}, u32[]{:S(2)}) collective-permute-start(bf16[2,48,768]{2,1,0:T(8,128)(2,1)} %get-tuple-element.221), channel_id=1, source_target_pairs={{0,1},{1,0},{2,3},{3,2},{12,13},{13,12},{14,15},{15,14},{16,17},{1... | collective-permute-start | bytes 442376 | tf_op jit(solution)/shard_map/ppermute | solution.py:412
  338.0 26.0 %collective-permute-start.58 = (bf16[12,48,768]{2,1,0:T(8,128)(2,1)}, bf16[12,48,768]{2,1,0:T(8,128)(2,1)S(1)}, u32[]{:S(2)}, u32[]{:S(2)}) collective-permute-start(bf16[12,48,768]{2,1,0:T(8,128)(2,1)} %join_feed.1.own_ref), channel_id=1, source_target_pairs={{0,16},{1,17},{2,18},{3,19},{12,28},{13,29},{14,30},{15,31},{16,0}... | collective-permute-start | bytes 2654216 | tf_op jit(solution)/shard_map/ppermute | solution.py:412
  339.9 24.1 %collective-permute-start.59 = (bf16[12,48,768]{2,1,0:T(8,128)(2,1)}, bf16[12,48,768]{2,1,0:T(8,128)(2,1)S(1)}, u32[]{:S(2)}, u32[]{:S(2)}) collective-permute-start(bf16[12,48,768]{2,1,0:T(8,128)(2,1)} %join_feed.1.own_ref), channel_id=1, source_target_pairs={{0,8},{1,9},{2,10},{3,11},{4,12},{5,13},{6,14},{7,15},{8,0},{9,1},... | collective-permute-start | bytes 2654216 | tf_op jit(solution)/shard_map/ppermute | solution.py:412
  340.0 24.0 %collective-permute-start.56 = (bf16[256,768]{1,0:T(8,128)(2,1)S(1)}, bf16[256,768]{1,0:T(8,128)(2,1)S(1)}, u32[]{:S(2)}, u32[]{:S(2)}) collective-permute-start(bf16[256,768]{1,0:T(8,128)(2,1)S(1)} %add_convert_fusion), channel_id=1, source_target_pairs={{0,0},{1,1},{2,2},{3,3},{4,8},{5,9},{6,10},{7,11},{8,4},{9,5},{10,... | collective-permute-start | bytes 1179656 | tf_op jit(solution)/shard_map/ppermute | solution.py:412
  347.2 16.8 %collective-permute-start.57 = (bf16[96,768]{1,0:T(8,128)(2,1)S(1)}, bf16[96,768]{1,0:T(8,128)(2,1)S(1)}, u32[]{:S(2)}, u32[]{:S(2)}) collective-permute-start(bf16[96,768]{1,0:T(8,128)(2,1)S(1)} %add.229), channel_id=1, source_target_pairs={{0,0},{1,2},{2,4},{3,6},{4,8},{5,10},{6,12},{7,14},{8,1},{9,3},{10... | collective-permute-start | bytes 442376 | tf_op jit(solution)/shard_map/ppermute | solution.py:412
  (74 other events, 584.8 us)

commit v5 on v4

--- a/solution.py
+++ b/solution.py
@@ -493,7 +493,7 @@
 
 def attend_kernel(
     ids_ref, row_ids_ref, col_ids_ref, q_ref, own_ref, other_ref, out_ref, log_ref,
-    v_turned, max_ref, total_ref, acc_ref,
+    k_all, v_turned, max_ref, total_ref, acc_ref,
 ):
     q_tile = pl.program_id(0)
     own_tiles = own_ref.shape[0] // TILE
@@ -501,10 +501,14 @@
     @pl.when(q_tile == 0)
     def _():
         for base, ref in ((0, own_ref), (own_tiles, other_ref)):
-            for tile in range(own_tiles):
-                v_turned[base + tile] = jnp.transpose(
-                    ref[pl.ds(tile * TILE, TILE), WIDE:]
-                )[:NARROW]
+
+            def gather(tile, carry, base=base, ref=ref):
+                place = pl.ds(pl.multiple_of(tile * TILE, TILE), TILE)
+                k_all[base + tile] = ref[place, :WIDE]
+                v_turned[base + tile] = jnp.transpose(ref[place, WIDE:])[:NARROW]
+                return carry
+
+            lax.fori_loop(0, own_tiles, gather, 0)
 
     queries = q_ref[...]
     per_head = [head_only(queries, head) for head in range(OWN_HEADS)]
@@ -513,37 +517,34 @@
     total_ref[...] = jnp.zeros(total_ref.shape, F32)
     acc_ref[...] = jnp.zeros(acc_ref.shape, F32)
 
-    for base, ref in ((0, own_ref), (own_tiles, other_ref)):
-
-        def one_tile(tile, carry, base=base, ref=ref):
-            @pl.when(share_document(ids_ref, q_tile, base + tile))
-            def _():
-                start = pl.multiple_of(tile * TILE, TILE)
-                keys = ref[pl.ds(start, TILE), :WIDE]
-                same = (
-                    col_ids_ref[pl.ds(pl.multiple_of((base + tile) * TILE, TILE), TILE), :] == q_ids
+    def one_tile(tile, carry):
+        @pl.when(share_document(ids_ref, q_tile, tile))
+        def _():
+            keys = k_all[tile]
+            same = (
+                col_ids_ref[pl.ds(pl.multiple_of(tile * TILE, TILE), TILE), :] == q_ids
+            )
+            for head in range(OWN_HEADS):
+                scores = contract(keys, per_head[head], 1, 1) * SCORE_FACTOR
+                scores = jnp.where(same, scores, MASKED)
+                old_max = max_ref[head : head + 1, :]
+                new_max = jnp.maximum(old_max, jnp.max(scores, axis=0, keepdims=True))
+                shrink = jnp.exp2(old_max - new_max)
+                expons = jnp.exp2(scores - new_max)
+                max_ref[head : head + 1, :] = new_max
+                total_ref[head : head + 1, :] = total_ref[
+                    head : head + 1, :
+                ] * shrink + jnp.sum(expons, axis=0, keepdims=True)
+                rows = slice(head * HEAD_DIM, (head + 1) * HEAD_DIM)
+                acc_ref[rows, :] = acc_ref[rows, :] * shrink + jnp.dot(
+                    v_turned[tile, rows, :],
+                    expons.astype(BF),
+                    preferred_element_type=F32,
                 )
-                for head in range(OWN_HEADS):
-                    scores = contract(keys, per_head[head], 1, 1) * SCORE_FACTOR
-                    scores = jnp.where(same, scores, MASKED)
-                    old_max = max_ref[head : head + 1, :]
-                    new_max = jnp.maximum(old_max, jnp.max(scores, axis=0, keepdims=True))
-                    shrink = jnp.exp2(old_max - new_max)
-                    expons = jnp.exp2(scores - new_max)
-                    max_ref[head : head + 1, :] = new_max
-                    total_ref[head : head + 1, :] = total_ref[
-                        head : head + 1, :
-                    ] * shrink + jnp.sum(expons, axis=0, keepdims=True)
-                    rows = slice(head * HEAD_DIM, (head + 1) * HEAD_DIM)
-                    acc_ref[rows, :] = acc_ref[rows, :] * shrink + jnp.dot(
-                        v_turned[base + tile, rows, :],
-                        expons.astype(BF),
-                        preferred_element_type=F32,
-                    )
-
-            return carry
-
-        lax.fori_loop(0, own_tiles, one_tile, 0)
+
+        return carry
+
+    lax.fori_loop(0, 2 * own_tiles, one_tile, 0)
 
     parts = []
     for head in range(OWN_HEADS):
@@ -579,6 +580,7 @@
                 pl.BlockSpec((8, TILE), lambda i, ids: (0, i)),
             ],
             scratch_shapes=[
+                pltpu.VMEM((2 * rows // TILE, TILE, WIDE), BF),
                 pltpu.VMEM((2 * rows // TILE, NARROW, TILE), BF),
                 pltpu.VMEM((8, TILE), F32),
                 pltpu.VMEM((8, TILE), F32),
@@ -599,7 +601,7 @@
 def attend_back_kernel(
     ids_ref, row_ids_ref, col_ids_ref, q_ref, up_ref, out_ref, log_ref, own_ref, other_ref,
     cos_ref, sin_ref, dq_ref, own_grad_ref, other_grad_ref,
-    k_turned, acc_ref, key_acc, value_acc,
+    kv_all, k_turned, acc_ref, key_acc, value_acc,
 ):
     q_tile = pl.program_id(0)
     own_tiles = own_ref.shape[0] // TILE
@@ -607,12 +609,17 @@
     @pl.when(q_tile == 0)
     def _():
         for base, ref in ((0, own_ref), (own_tiles, other_ref)):
-            for tile in range(own_tiles):
-                k_turned[base + tile] = jnp.transpose(
-                    ref[pl.ds(tile * TILE, TILE), :WIDE]
-                )[:NARROW]
-        key_acc[...] = jnp.zeros(key_acc.shape, F32)
-        value_acc[...] = jnp.zeros(value_acc.shape, F32)
+
+            def gather(tile, carry, base=base, ref=ref):
+                place = pl.ds(pl.multiple_of(tile * TILE, TILE), TILE)
+                kv_all[base + tile] = ref[place, :]
+                k_turned[base + tile] = jnp.transpose(ref[place, :WIDE])[:NARROW]
+                rows = pl.ds(pl.multiple_of((base + tile) * TILE, TILE), TILE)
+                key_acc[rows, :] = jnp.zeros((TILE, WIDE), F32)
+                value_acc[rows, :] = jnp.zeros((TILE, WIDE), F32)
+                return carry
+
+            lax.fori_loop(0, own_tiles, gather, 0)
 
     queries = q_ref[...]
     upstream = up_ref[...]
@@ -635,46 +642,43 @@
     q_ids = row_ids_ref[0]
     acc_ref[...] = jnp.zeros(acc_ref.shape, F32)
 
-    for base, ref in ((0, own_ref), (own_tiles, other_ref)):
-
-        def one_tile(tile, carry, base=base, ref=ref):
-            @pl.when(share_document(ids_ref, q_tile, base + tile))
-            def _():
-                start = pl.multiple_of(tile * TILE, TILE)
-                place = pl.ds(pl.multiple_of((base + tile) * TILE, TILE), TILE)
-                keys = ref[pl.ds(start, TILE), :WIDE]
-                values = ref[pl.ds(start, TILE), WIDE:]
-                same = col_ids_ref[place, :] == q_ids
-                for side, inside, q_side, up_side, q_stack, up_stack in zip(
-                    sides, members, q_heads, up_heads, q_stacks, up_stacks
-                ):
-                    all_weights, all_grads = [], []
-                    for head, query, grad in zip(inside, q_side, up_side):
-                        scores = contract(keys[:, side], query, 1, 1) * SCORE_FACTOR
-                        weights = jnp.where(
-                            same, jnp.exp2(scores - log_ref[head : head + 1, :]), 0.0
-                        )
-                        grad_weights = contract(values[:, side], grad, 1, 1)
-                        grad_scores = (
-                            weights * (grad_weights - deltas[head : head + 1, :])
-                        ).astype(BF)
-                        all_weights.append(weights.astype(BF))
-                        all_grads.append(grad_scores)
-                        rows = slice(head * HEAD_DIM, (head + 1) * HEAD_DIM)
-                        acc_ref[rows, :] += jnp.dot(
-                            k_turned[base + tile, rows, :], grad_scores,
-                            preferred_element_type=F32,
-                        )
-                    value_acc[place, side] += jnp.dot(
-                        jnp.concatenate(all_weights, axis=1), up_stack, preferred_element_type=F32
+    def one_tile(tile, carry):
+        @pl.when(share_document(ids_ref, q_tile, tile))
+        def _():
+            place = pl.ds(pl.multiple_of(tile * TILE, TILE), TILE)
+            keys = kv_all[tile, :, :WIDE]
+            values = kv_all[tile, :, WIDE:]
+            same = col_ids_ref[place, :] == q_ids
+            for side, inside, q_side, up_side, q_stack, up_stack in zip(
+                sides, members, q_heads, up_heads, q_stacks, up_stacks
+            ):
+                all_weights, all_grads = [], []
+                for head, query, grad in zip(inside, q_side, up_side):
+                    scores = contract(keys[:, side], query, 1, 1) * SCORE_FACTOR
+                    weights = jnp.where(
+                        same, jnp.exp2(scores - log_ref[head : head + 1, :]), 0.0
                     )
-                    key_acc[place, side] += jnp.dot(
-                        jnp.concatenate(all_grads, axis=1), q_stack, preferred_element_type=F32
+                    grad_weights = contract(values[:, side], grad, 1, 1)
+                    grad_scores = (
+                        weights * (grad_weights - deltas[head : head + 1, :])
+                    ).astype(BF)
+                    all_weights.append(weights.astype(BF))
+                    all_grads.append(grad_scores)
+                    rows = slice(head * HEAD_DIM, (head + 1) * HEAD_DIM)
+                    acc_ref[rows, :] += jnp.dot(
+                        k_turned[tile, rows, :], grad_scores,
+                        preferred_element_type=F32,
                     )
-
-            return carry
-
-        lax.fori_loop(0, own_tiles, one_tile, 0)
+                value_acc[place, side] += jnp.dot(
+                    jnp.concatenate(all_weights, axis=1), up_stack, preferred_element_type=F32
+                )
+                key_acc[place, side] += jnp.dot(
+                    jnp.concatenate(all_grads, axis=1), q_stack, preferred_element_type=F32
+                )
+
+        return carry
+
+    lax.fori_loop(0, 2 * own_tiles, one_tile, 0)
 
     factor = HEAD_DIM ** (-0.5)
     grad_query = jnp.transpose(
@@ -687,11 +691,17 @@
 
     @pl.when(q_tile == pl.num_programs(0) - 1)
     def _():
-        rows = own_grad_ref.shape[0]
-        own_grad_ref[:, :WIDE] = key_acc[:rows, :] * factor
-        own_grad_ref[:, WIDE:] = value_acc[:rows, :]
-        other_grad_ref[:, :WIDE] = (key_acc[rows:, :] * factor).astype(BF)
-        other_grad_ref[:, WIDE:] = value_acc[rows:, :].astype(BF)
+
+        def write(tile, carry):
+            own = pl.ds(pl.multiple_of(tile * TILE, TILE), TILE)
+            other = pl.ds(pl.multiple_of((own_tiles + tile) * TILE, TILE), TILE)
+            own_grad_ref[own, :WIDE] = key_acc[own, :] * factor
+            own_grad_ref[own, WIDE:] = value_acc[own, :]
+            other_grad_ref[own, :WIDE] = (key_acc[other, :] * factor).astype(BF)
+            other_grad_ref[own, WIDE:] = value_acc[other, :].astype(BF)
+            return carry
+
+        lax.fori_loop(0, own_tiles, write, 0)
 
 
 def attend_back(
@@ -723,6 +733,7 @@
                 pl.BlockSpec((rows, 2 * WIDE), lambda i, ids: (0, 0)),
             ],
             scratch_shapes=[
+                pltpu.VMEM((2 * rows // TILE, TILE, 2 * WIDE), BF),
                 pltpu.VMEM((2 * rows // TILE, NARROW, TILE), BF),
                 pltpu.VMEM((NARROW, TILE), F32),
                 pltpu.VMEM((2 * rows, WIDE), F32),
@@ -767,8 +778,17 @@
     def _():
         rows = keep_ref.shape[0]
         core = c_ref[0]
-        keep_ref[...] = acc_ref[pl.ds(pl.multiple_of(core * rows, 8), rows), :]
-        away_ref[:rows] = acc_ref[pl.ds(pl.multiple_of((1 - core) * rows, 8), rows), :].astype(BF)
+        step = rows // 8
+
+        def write(index, carry):
+            place = pl.ds(pl.multiple_of(index * step, 16), step)
+            keep_ref[place, :] = acc_ref[pl.ds(pl.multiple_of(core * rows + index * step, 8), step), :]
+            away_ref[place, :] = acc_ref[
+                pl.ds(pl.multiple_of((1 - core) * rows + index * step, 8), step), :
+            ].astype(BF)
+            return carry
+
+        lax.fori_loop(0, 8, write, 0)
         away_ref[rows:] = jnp.zeros((16, away_ref.shape[1]), BF)
         away_ref[rows : rows + 8] = vectors_ref[...].astype(BF)
 
@@ -870,15 +890,19 @@
 
 def unpack_qkv_kernel(place_ref, near_ref, far_ref, out_ref, vectors_ref):
     zeros = jnp.zeros((near_ref.shape[1], WIDE - NARROW), BF)
-    for index in range(2 * GROUP):
-        source = (near_ref, far_ref)[index // GROUP]
-        place = place_ref[index]
-        for part in range(3):
-            out_ref[place, :, part * WIDE : part * WIDE + NARROW] = source[
-                index % GROUP, :, part * NARROW : (part + 1) * NARROW
-            ]
-            out_ref[place, :, part * WIDE + NARROW : (part + 1) * WIDE] = zeros
-        vectors_ref[place] = source[index % GROUP, :, 3 * NARROW :]
+    for base, source in ((0, near_ref), (GROUP, far_ref)):
+
+        def one_block(index, carry, base=base, source=source):
+            place = place_ref[base + index]
+            for part in range(3):
+                out_ref[place, :, part * WIDE : part * WIDE + NARROW] = source[
+                    index, :, part * NARROW : (part + 1) * NARROW
+                ]
+                out_ref[place, :, part * WIDE + NARROW : (part + 1) * WIDE] = zeros
+            vectors_ref[place] = source[index, :, 3 * NARROW :]
+            return carry
+
+        lax.fori_loop(0, GROUP, one_block, 0)
 
 
 def unpack_qkv(places, near, far):
@@ -900,8 +924,13 @@
 
 
 def unpack_kernel(place_ref, near_ref, far_ref, out_ref):
-    for index in range(2 * GROUP):
-        out_ref[place_ref[index]] = (near_ref, far_ref)[index // GROUP][index % GROUP]
+    for base, ref in ((0, near_ref), (GROUP, far_ref)):
+
+        def one_block(index, carry, base=base, ref=ref):
+            out_ref[place_ref[base + index]] = ref[index]
+            return carry
+
+        lax.fori_loop(0, GROUP, one_block, 0)
 
 
 def unpack(places, near, far):
@@ -922,7 +951,8 @@
 def split_feed_kernel(x_ref, down_ref, down_got_ref, gate_up_ref, gate_up_got_ref, keep_ref, away_ref):
     mine = x_ref[0]
     width = down_ref.shape[-1]
-    for block in range(GROUP):
+
+    def one_block(block, carry):
         for side, ref in ((mine, keep_ref), (1 - mine, away_ref)):
             ref[block] = (
                 down_ref[block, side] + down_got_ref[block, side].astype(F32)
@@ -930,6 +960,9 @@
             total = gate_up_ref[block, side] + gate_up_got_ref[block, side].astype(F32)
             ref[GROUP + block] = total[:, :width].astype(BF)
             ref[2 * GROUP + block] = total[:, width:].astype(BF)
+        return carry
+
+    lax.fori_loop(0, GROUP, one_block, 0)
 
 
 def whole_call(kernel, name, shapes, scalars, *arrays):
@@ -970,13 +1003,19 @@
     mine, at_home = flag_ref[0], flag_ref[1] == 1
     rows = own_ref.shape[1]
     half = own_ref.shape[2] // 2
-    for slot in range(3 * GROUP):
-        for near, far, side in ((own_ref, far_own_ref, mine), (other_ref, far_other_ref, 1 - mine)):
-            block = jnp.where(at_home, near[slot], far[slot]).astype(F32)
-            if slot < GROUP:
-                down_ref[slot, side] = block
-            else:
-                ref = gate_ref if slot < 2 * GROUP else up_ref
+    pairs = ((own_ref, far_own_ref, mine), (other_ref, far_other_ref, 1 - mine))
+
+    def down_slot(slot, carry):
+        for near, far, side in pairs:
+            down_ref[slot, side] = jnp.where(at_home, near[slot], far[slot]).astype(F32)
+        return carry
+
+    lax.fori_loop(0, GROUP, down_slot, 0)
+    for slot in range(GROUP):
+        for near, far, side in pairs:
+            for part, ref in ((1, gate_ref), (2, up_ref)):
+                place = part * GROUP + slot
+                block = jnp.where(at_home, near[place], far[place]).astype(F32)
                 start = slot % GROUP * half
                 width = GROUP * half
                 ref[side, :, start : start + half] = block[:, :half]
@@ -987,12 +1026,16 @@
     mine = flag_ref[0]
     rows = part_ref.shape[0]
     step = rows // (2 * GROUP)
-    for block in range(GROUP):
+
+    def one_block(block, carry):
         for side, ref in ((mine, keep_ref), (1 - mine, away_ref)):
             place = pl.ds(pl.multiple_of((2 * block + side) * step, step), step)
-            ref[block * step : (block + 1) * step] = (
+            ref[pl.ds(pl.multiple_of(block * step, step), step)] = (
                 part_ref[place] + got_ref[place].astype(F32)
             ).astype(BF)
+        return carry
+
+    lax.fori_loop(0, GROUP, one_block, 0)
     for ref in (keep_ref, away_ref):
         ref[GROUP * step :] = got_ref[rows:]
         ref[GROUP * step : GROUP * step + 8] = (

time: 386 us -> 377 us (0.977)
  waiting for transfers between devices: 133 us -> 122 us
  starting transfers between devices: 95.2 us -> 99.2 us
    ppermute x67, waiting for transfers between devices: 133 us -> 122 us  [send(): return lax.ppermute(value, AXES, pairs)]
    ppermute x67, starting transfers between devices: 95.2 us -> 99.2 us  [send(): return lax.ppermute(value, AXES, pairs)]
  transfers between devices with their start and end apart: 67 -> 67, of which waited for: 29 -> 28; matrix products, arithmetic and copies ran while one was open for 11% -> 11% of each run, Pallas kernels for 15% -> 16%
where the time goes in v5:
time: 377 us
  waiting for transfers between devices  122 us (32%)
  starting transfers between devices  99.2 us (26%)
  Pallas kernels  84.2 us (22%)
  matrix products  28.7 us (8%)
  other arithmetic  27.2 us (7%)
  local copies, waits for them, and re-layouts  13.7 us (4%)
    ppermute x67, waiting for transfers between devices, send(): return lax.ppermute(value, AXES, pairs)  122 us
    ppermute x67, starting transfers between devices, send(): return lax.ppermute(value, AXES, pairs)  99.2 us
    dot_general x22, matrix products, contract(): lax.dot_general(left, right, (((left_dim,), (right_dim,)), ((), ())), pre...  28.7 us
    pallas_call x1, Pallas kernels, attend_back(): pl.pallas_call(attend_back_kernel, grid_spec=pltpu.PrefetchScalarGridSpec...  25.6 us
    pallas_call x8, Pallas kernels, whole_call(): pl.pallas_call(kernel, in_specs=[pl.BlockSpec(memory_space=pltpu.SMEM)] +...  21 us
    pallas_call x1, Pallas kernels, attend(): pl.pallas_call(attend_kernel, grid_spec=pltpu.PrefetchScalarGridSpec(num_...  14.5 us
    unnamed x90, local copies, waits for them, and re-layouts  8.16 us
  transfers between devices with their start and end apart: 67, of which 28 were waited for; matrix products, arithmetic and copies ran while one was open for 11% of the time, Pallas kernels for 16%

profile of v5, /device:TPU:0, one launch (start us, length us, event | category | flops | bytes accessed | tf_op | source)
XLA Modules:
  0.0 377.3 jit_solution(8021683799467833294)
XLA Ops:
  14.6 3.8 %collective-permute-start.3 = (bf16[2,96,580]{2,1,0:T(8,128)(2,1)S(1)}, bf16[2,96,580]{2,1,0:T(8,128)(2,1)S(1)}, u32[]{:S(2)}, u32[]{:S(2)}) collective-permute-start(bf16[2,96,580]{2,1,0:T(8,128)(2,1)S(1)} %pad_maximum_fusion.7), channel_id=1, source_target_pairs={{0,16},{1,17},{2,18},{3,19},{4,20},{5,21},{6,22},{7,23},{8,24},{9,... | collective-permute-start | bytes 668168 | tf_op jit(solution)/shard_map/ppermute | solution.py:412
  20.2 6.3 %collective-permute-start.5 = (bf16[256,768]{1,0:T(8,128)(2,1)S(1)}, bf16[256,768]{1,0:T(8,128)(2,1)S(1)}, u32[]{:S(2)}, u32[]{:S(2)}) collective-permute-start(bf16[256,768]{1,0:T(8,128)(2,1)S(1)} %collective-permute-done.2), channel_id=1, source_target_pairs={{0,1},{1,0},{2,3},{3,2},{4,5},{5,4},{6,7},{7,6},{8,9},{9,8},{10,11... | collective-permute-start | bytes 1179656 | tf_op jit(solution)/shard_map/ppermute | solution.py:412
  28.2 6.7 %collective-permute-start.4 = (bf16[4,96,580]{2,1,0:T(8,128)(2,1)S(1)}, bf16[4,96,580]{2,1,0:T(8,128)(2,1)S(1)}, u32[]{:S(2)}, u32[]{:S(2)}) collective-permute-start(bf16[4,96,580]{2,1,0:T(8,128)(2,1)S(1)} %constant_dynamic-update-slice_fusion.near_ref), channel_id=1, source_target_pairs={{0,8},{1,9},{2,10},{3,11},{4,12},{5,13},{6,14},{7,15},{8,0},{9,1},... | collective-permute-start | bytes 1336328 | tf_op jit(solution)/shard_map/ppermute | solution.py:412
  39.0 3.1 multiply_sine_fusion
  47.9 4.2 %collective-permute-done.10 = bf16[96,768]{1,0:T(8,128)(2,1)} collective-permute-done((bf16[96,768]{1,0:T(8,128)(2,1)S(1)}, bf16[96,768]{1,0:T(8,128)(2,1)}, u32[]{:S(2)}, u32[]{:S(2)}) %collective-permute-start.10) | collective-permute-done | bytes 147488 | tf_op jit(solution)/shard_map/ppermute | solution.py:412
  52.1 5.4 %project.1 = (bf16[1024,256]{1,0:T(8,128)(2,1)}, bf16[1024,512]{1,0:T(8,128)(2,1)}) custom-call(bf16[1024,768]{1,0:T(8,128)(2,1)} %pad_maximum_fusion.1.x_ref, bf16[768,768]{1,0:T(8,128)(2,1)} %bitcast.83, f32[1024,128]{1,0:T(8,128)} %get-tuple-element.156.cos_ref, f32[1024,128]{1,0:T(8,128)} %get-tuple-element.157.sin_ref), custom_call_target="tpu_custom_call" | custom-call | flops 1207959552 | bytes 5373952 | tf_op jit(solution)/shard_map/project/pallas_call | solution.py:453
  62.8 14.5 %attend.1 = (bf16[1024,256]{1,0:T(8,128)(2,1)}, f32[8,1024]{1,0:T(8,128)}) custom-call(s32[2048]{0:T(1024)} %bitcast.98, s32[8,1,256]{2,1,0:T(1,128)} %reshape.183.row_ids_ref, s32[2048,1]{1,0:T(8,128)} %copy.43.col_ids_ref, bf16[1024,256]{1,0:T(8,128)(2,1)} %get-tuple-element.158.q_ref, bf16[1024,512]{1,0:T(8,128)(2,1)} %get-tuple-element.159.own_ref, ...), custom_call_target="tpu_custom_call" | custom-call | flops 6442450944 | bytes 3145728 | tf_op jit(solution)/shard_map/attend/pallas_call | solution.py:566
  92.3 8.5 %collective-permute-done.17 = bf16[256,768]{1,0:T(8,128)(2,1)} collective-permute-done((bf16[256,768]{1,0:T(8,128)(2,1)}, bf16[256,768]{1,0:T(8,128)(2,1)}, u32[]{:S(2)}, u32[]{:S(2)}) %collective-permute-start.17) | collective-permute-done | bytes 393248 | tf_op jit(solution)/shard_map/ppermute | solution.py:412
  108.8 7.4 %collective-permute-done.20 = bf16[256,768]{1,0:T(8,128)(2,1)S(1)} collective-permute-done((bf16[256,768]{1,0:T(8,128)(2,1)S(1)}, bf16[256,768]{1,0:T(8,128)(2,1)S(1)}, u32[]{:S(2)}, u32[]{:S(2)}) %collective-permute-start.20) | collective-permute-done | bytes 393248 | tf_op jit(solution)/shard_map/ppermute | solution.py:412
  118.7 7.7 %collective-permute-done.22 = bf16[256,768]{1,0:T(8,128)(2,1)S(1)} collective-permute-done((bf16[256,768]{1,0:T(8,128)(2,1)S(1)}, bf16[256,768]{1,0:T(8,128)(2,1)S(1)}, u32[]{:S(2)}, u32[]{:S(2)}) %collective-permute-start.22) | collective-permute-done | bytes 393248 | tf_op jit(solution)/shard_map/ppermute | solution.py:412
  127.8 3.2 unpack.1
  131.0 4.3 %fusion.49 = f32[1024,1536]{1,0:T(8,128)S(1)} fusion(bf16[1024,768]{1,0:T(8,128)(2,1)S(1)} %constant_dynamic-update-slice_fusion.2, bf16[768,1536]{1,0:T(8,128)(2,1)} %bitcast.76), kind=kOutput, calls=%fused_computation.167 | convolution fusion | flops 2415919104 | bytes 10223616 | tf_op jit(solution)/shard_map/dot_general | solution.py:489
  142.9 6.3 %collective-permute-done.25 = bf16[256,768]{1,0:T(8,128)(2,1)S(1)} collective-permute-done((bf16[256,768]{1,0:T(8,128)(2,1)S(1)}, bf16[256,768]{1,0:T(8,128)(2,1)S(1)}, u32[]{:S(2)}, u32[]{:S(2)}) %collective-permute-start.25) | collective-permute-done | bytes 393248 | tf_op jit(solution)/shard_map/ppermute | solution.py:412
  149.2 6.8 %collective-permute-done.26 = bf16[256,768]{1,0:T(8,128)(2,1)S(1)} collective-permute-done((bf16[256,768]{1,0:T(8,128)(2,1)S(1)}, bf16[256,768]{1,0:T(8,128)(2,1)S(1)}, u32[]{:S(2)}, u32[]{:S(2)}) %collective-permute-start.26) | collective-permute-done | bytes 393248 | tf_op jit(solution)/shard_map/ppermute | solution.py:412
  156.0 7.0 %collective-permute-done.27 = bf16[256,768]{1,0:T(8,128)(2,1)S(1)} collective-permute-done((bf16[256,768]{1,0:T(8,128)(2,1)S(1)}, bf16[256,768]{1,0:T(8,128)(2,1)S(1)}, u32[]{:S(2)}, u32[]{:S(2)}) %collective-permute-start.27) | collective-permute-done | bytes 393248 | tf_op jit(solution)/shard_map/ppermute | solution.py:412
  168.8 6.5 %collective-permute-done.29 = bf16[256,768]{1,0:T(8,128)(2,1)S(1)} collective-permute-done((bf16[256,768]{1,0:T(8,128)(2,1)S(1)}, bf16[256,768]{1,0:T(8,128)(2,1)S(1)}, u32[]{:S(2)}, u32[]{:S(2)}) %collective-permute-start.29) | collective-permute-done | bytes 393248 | tf_op jit(solution)/shard_map/ppermute | solution.py:412
  175.3 3.4 collective-permute-done.30
  178.7 7.1 %collective-permute-done.31 = bf16[256,768]{1,0:T(8,128)(2,1)S(1)} collective-permute-done((bf16[256,768]{1,0:T(8,128)(2,1)S(1)}, bf16[256,768]{1,0:T(8,128)(2,1)S(1)}, u32[]{:S(2)}, u32[]{:S(2)}) %collective-permute-start.31) | collective-permute-done | bytes 393248 | tf_op jit(solution)/shard_map/ppermute | solution.py:412
  204.5 7.2 %collective-permute-done.34 = bf16[256,768]{1,0:T(8,128)(2,1)S(1)} collective-permute-done((bf16[256,768]{1,0:T(8,128)(2,1)S(1)}, bf16[256,768]{1,0:T(8,128)(2,1)S(1)}, u32[]{:S(2)}, u32[]{:S(2)}) %collective-permute-start.34) | collective-permute-done | bytes 393248 | tf_op jit(solution)/shard_map/ppermute | solution.py:412
  217.9 4.1 %split_feed.1 = (bf16[12,48,768]{2,1,0:T(8,128)(2,1)}, bf16[12,48,768]{2,1,0:T(8,128)(2,1)}) custom-call(s32[1]{0:T(128)} %bitcast.20.x_ref.flag_ref, f32[4,2,48,768]{3,2,1,0:T(8,128)} %bitcast.82, bf16[4,2,48,768]{3,2,1,0:T(8,128)(2,1)} %bitcast.89, f32[4,2,48,1536]{3,2,1,0:T(8,128)} %bitcast.81, bf16[4,2,48,1536]{3,2,1,0:T(8,128)(2,1)} %bitcast.88), custom_call_target="tpu_custom_call" | custom-call | flops 1769472 | bytes 10616832 | tf_op jit(solution)/shard_map/split_feed/pallas_call | solution.py:969
  227.5 5.2 %collective-permute-done.39 = bf16[256,768]{1,0:T(8,128)(2,1)S(1)} collective-permute-done((bf16[256,768]{1,0:T(8,128)(2,1)S(1)}, bf16[256,768]{1,0:T(8,128)(2,1)S(1)}, u32[]{:S(2)}, u32[]{:S(2)}) %collective-permute-start.39) | collective-permute-done | bytes 393248 | tf_op jit(solution)/shard_map/ppermute | solution.py:412
  237.1 25.6 %attend_back.1 = (bf16[1024,256]{1,0:T(8,128)(2,1)}, f32[1024,512]{1,0:T(8,128)}, bf16[1024,512]{1,0:T(8,128)(2,1)}) custom-call(s32[2048]{0:T(1024)} %bitcast.99, s32[8,1,256]{2,1,0:T(1,128)} %reshape.183.row_ids_ref, s32[2048,1]{1,0:T(8,128)} %copy.43.col_ids_ref, bf16[1024,256]{1,0:T(8,128)(2,1)} %get-tuple-element.158.q_ref, ...), custom_call_target="tpu_custom_call" | custom-call | flops 16106127360 | bytes 3145728 | tf_op jit(solution)/shard_map/attend_back/pallas_call | solution.py:713
  263.6 5.4 %collective-permute-start.44 = (bf16[1024,512]{1,0:T(8,128)(2,1)}, bf16[1024,512]{1,0:T(8,128)(2,1)S(1)}, u32[]{:S(2)}, u32[]{:S(2)}) collective-permute-start(bf16[1024,512]{1,0:T(8,128)(2,1)} %get-tuple-element.203), channel_id=1, source_target_pairs={{0,8},{1,9},{2,10},{3,11},{4,12},{5,13},{6,14},{7,15},{8,0},{9,1},... | collective-permute-start | bytes 3145736 | tf_op jit(solution)/shard_map/ppermute | solution.py:412
  272.6 7.3 %grad_qkv.1 = (bf16[1024,768]{1,0:T(8,128)(2,1)}, f32[384,768]{1,0:T(8,128)}, bf16[400,768]{1,0:T(8,128)(2,1)}) custom-call(s32[1]{0:T(128)} %bitcast.26.c_ref, bf16[1024,768]{1,0:T(8,128)(2,1)} %pad_maximum_fusion.1.x_ref, bf16[1024,256]{1,0:T(8,128)(2,1)} %get-tuple-element.201.dq_ref, f32[1024,512]{1,0:T(8,128)} %get-tuple-element.202.own_ref, ...), custom_call_target="tpu_custom_call" | custom-call | flops 1207959552 | bytes 5767168 | tf_op jit(solution)/shard_map/grad_qkv/pallas_call | solution.py:800
  292.4 5.6 %collective-permute-done.49 = bf16[208,768]{1,0:T(8,128)(2,1)S(1)} collective-permute-done((bf16[208,768]{1,0:T(8,128)(2,1)}, bf16[208,768]{1,0:T(8,128)(2,1)S(1)}, u32[]{:S(2)}, u32[]{:S(2)}) %collective-permute-start.49) | collective-permute-done | bytes 319520 | tf_op jit(solution)/shard_map/ppermute | solution.py:412
  299.1 6.8 %collective-permute-done.50.got_ref = bf16[12,48,768]{2,1,0:T(8,128)(2,1)} collective-permute-done((bf16[12,48,768]{2,1,0:T(8,128)(2,1)S(1)}, bf16[12,48,768]{2,1,0:T(8,128)(2,1)}, u32[]{:S(2)}, u32[]{:S(2)}) %collective-permute-start.50) | collective-permute-done | bytes 884768 | tf_op jit(solution)/shard_map/ppermute | solution.py:412
  308.8 4.3 %collective-permute-start.52 = (bf16[96,768]{1,0:T(8,128)(2,1)S(1)}, bf16[96,768]{1,0:T(8,128)(2,1)S(1)}, u32[]{:S(2)}, u32[]{:S(2)}) collective-permute-start(bf16[96,768]{1,0:T(8,128)(2,1)S(1)} %add_convert_fusion.2), channel_id=1, source_target_pairs={{0,4},{1,5},{2,6},{3,7},{4,0},{5,1},{6,2},{7,3},{8,12},{9,13},{10,... | collective-permute-start | bytes 442376 | tf_op jit(solution)/shard_map/ppermute | solution.py:412
  319.6 5.4 %collective-permute-done.48 = bf16[256,768]{1,0:T(8,128)(2,1)} collective-permute-done((bf16[256,768]{1,0:T(8,128)(2,1)}, bf16[256,768]{1,0:T(8,128)(2,1)}, u32[]{:S(2)}, u32[]{:S(2)}) %collective-permute-start.48) | collective-permute-done | bytes 393248 | tf_op jit(solution)/shard_map/ppermute | solution.py:412
  328.4 4.7 %collective-permute-done.55.refs_2_ = bf16[2,48,768]{2,1,0:T(8,128)(2,1)S(1)} collective-permute-done((bf16[2,48,768]{2,1,0:T(8,128)(2,1)}, bf16[2,48,768]{2,1,0:T(8,128)(2,1)S(1)}, u32[]{:S(2)}, u32[]{:S(2)}) %collective-permute-start.55) | collective-permute-done | bytes 147488 | tf_op jit(solution)/shard_map/ppermute | solution.py:412
  337.3 4.0 %collective-permute-start.58 = (bf16[12,48,768]{2,1,0:T(8,128)(2,1)}, bf16[12,48,768]{2,1,0:T(8,128)(2,1)S(1)}, u32[]{:S(2)}, u32[]{:S(2)}) collective-permute-start(bf16[12,48,768]{2,1,0:T(8,128)(2,1)} %join_feed.1.own_ref), channel_id=1, source_target_pairs={{0,16},{1,17},{2,18},{3,19},{12,28},{13,29},{14,30},{15,31},{16,0}... | collective-permute-start | bytes 2654216 | tf_op jit(solution)/shard_map/ppermute | solution.py:412
  354.0 4.9 %collective-permute-done.62.refs_3_ = bf16[64,768]{1,0:T(8,128)(2,1)S(1)} collective-permute-done((bf16[64,768]{1,0:T(8,128)(2,1)}, bf16[64,768]{1,0:T(8,128)(2,1)S(1)}, u32[]{:S(2)}, u32[]{:S(2)}) %collective-permute-start.62) | collective-permute-done | bytes 98336 | tf_op jit(solution)/shard_map/ppermute | solution.py:412
  365.0 4.0 %finish_feed.1 = (f32[4,2,48,768]{3,2,1,0:T(8,128)}, f32[2,48,3072]{2,1,0:T(8,128)}, f32[2,48,3072]{2,1,0:T(8,128)}) custom-call(s32[2]{0:T(128)} %pad_add_fusion.3.flag_ref, bf16[12,48,768]{2,1,0:T(8,128)(2,1)} %join_feed.1.own_ref, bf16[12,48,768]{2,1,0:T(8,128)(2,1)} %copy-done.10, bf16[12,48,768]{2,1,0:T(8,128)(2,1)} %copy-done.11, ...), custom_call_target="tpu_custom_call" | custom-call | flops 1769472 | bytes 7077888 | tf_op jit(solution)/shard_map/finish_feed/pallas_call | solution.py:969
  (308 shorter events, 168.7 us)
Async XLA Ops:
  12.3 35.6 %collective-permute-start.8 = (bf16[96,768]{1,0:T(8,128)(2,1)}, bf16[96,768]{1,0:T(8,128)(2,1)S(1)}, u32[]{:S(2)}, u32[]{:S(2)}) collective-permute-start(bf16[96,768]{1,0:T(8,128)(2,1)} %param.15), channel_id=1, source_target_pairs={{0,0},{1,8},{2,1},{3,9},{4,2},{5,10},{6,3},{7,11},{8,4},{9,12},{10... | collective-permute-start | bytes 442376 | tf_op jit(solution)/shard_map/ppermute | solution.py:412
  14.6 13.5 %collective-permute-start.3 = (bf16[2,96,580]{2,1,0:T(8,128)(2,1)S(1)}, bf16[2,96,580]{2,1,0:T(8,128)(2,1)S(1)}, u32[]{:S(2)}, u32[]{:S(2)}) collective-permute-start(bf16[2,96,580]{2,1,0:T(8,128)(2,1)S(1)} %pad_maximum_fusion.7), channel_id=1, source_target_pairs={{0,16},{1,17},{2,18},{3,19},{4,20},{5,21},{6,22},{7,23},{8,24},{9,... | collective-permute-start | bytes 668168 | tf_op jit(solution)/shard_map/ppermute | solution.py:412
  20.2 26.4 %collective-permute-start.5 = (bf16[256,768]{1,0:T(8,128)(2,1)S(1)}, bf16[256,768]{1,0:T(8,128)(2,1)S(1)}, u32[]{:S(2)}, u32[]{:S(2)}) collective-permute-start(bf16[256,768]{1,0:T(8,128)(2,1)S(1)} %collective-permute-done.2), channel_id=1, source_target_pairs={{0,1},{1,0},{2,3},{3,2},{4,5},{5,4},{6,7},{7,6},{8,9},{9,8},{10,11... | collective-permute-start | bytes 1179656 | tf_op jit(solution)/shard_map/ppermute | solution.py:412
  26.5 20.1 %collective-permute-start.6 = (bf16[256,768]{1,0:T(8,128)(2,1)S(1)}, bf16[256,768]{1,0:T(8,128)(2,1)S(1)}, u32[]{:S(2)}, u32[]{:S(2)}) collective-permute-start(bf16[256,768]{1,0:T(8,128)(2,1)S(1)} %collective-permute-done.2), channel_id=1, source_target_pairs={{0,2},{1,3},{2,0},{3,1},{4,6},{5,7},{6,4},{7,5},{8,10},{9,11},{10,... | collective-permute-start | bytes 1179656 | tf_op jit(solution)/shard_map/ppermute | solution.py:412
  27.1 19.5 %collective-permute-start.7 = (bf16[256,768]{1,0:T(8,128)(2,1)S(1)}, bf16[256,768]{1,0:T(8,128)(2,1)S(1)}, u32[]{:S(2)}, u32[]{:S(2)}) collective-permute-start(bf16[256,768]{1,0:T(8,128)(2,1)S(1)} %collective-permute-done.2), channel_id=1, source_target_pairs={{0,3},{1,2},{2,1},{3,0},{4,7},{5,6},{6,5},{7,4},{8,11},{9,10},{10,... | collective-permute-start | bytes 1179656 | tf_op jit(solution)/shard_map/ppermute | solution.py:412
  28.2 13.9 %collective-permute-start.4 = (bf16[4,96,580]{2,1,0:T(8,128)(2,1)S(1)}, bf16[4,96,580]{2,1,0:T(8,128)(2,1)S(1)}, u32[]{:S(2)}, u32[]{:S(2)}) collective-permute-start(bf16[4,96,580]{2,1,0:T(8,128)(2,1)S(1)} %constant_dynamic-update-slice_fusion.near_ref), channel_id=1, source_target_pairs={{0,8},{1,9},{2,10},{3,11},{4,12},{5,13},{6,14},{7,15},{8,0},{9,1},... | collective-permute-start | bytes 1336328 | tf_op jit(solution)/shard_map/ppermute | solution.py:412
  60.6 16.8 %collective-permute-start.13 = (bf16[96,1536]{1,0:T(8,128)(2,1)}, bf16[96,1536]{1,0:T(8,128)(2,1)S(1)}, u32[]{:S(2)}, u32[]{:S(2)}) collective-permute-start(bf16[96,1536]{1,0:T(8,128)(2,1)} %get-tuple-element.166), channel_id=1, source_target_pairs={{0,0},{1,1},{2,2},{3,3},{4,4},{5,5},{6,6},{7,7},{8,12},{9,13},{10,... | collective-permute-start | bytes 884744 | tf_op jit(solution)/shard_map/ppermute | solution.py:412
  62.2 15.2 %collective-permute-start.14 = (bf16[96,1536]{1,0:T(8,128)(2,1)}, bf16[96,1536]{1,0:T(8,128)(2,1)S(1)}, u32[]{:S(2)}, u32[]{:S(2)}) collective-permute-start(bf16[96,1536]{1,0:T(8,128)(2,1)} %get-tuple-element.167), channel_id=1, source_target_pairs={{0,1},{1,0},{2,3},{3,2},{4,5},{5,4},{6,7},{7,6},{8,13},{9,12},{10,... | collective-permute-start | bytes 884744 | tf_op jit(solution)/shard_map/ppermute | solution.py:412
  83.6 17.1 %collective-permute-start.17 = (bf16[256,768]{1,0:T(8,128)(2,1)}, bf16[256,768]{1,0:T(8,128)(2,1)}, u32[]{:S(2)}, u32[]{:S(2)}) collective-permute-start(bf16[256,768]{1,0:T(8,128)(2,1)} %convolution_convert_fusion.10), channel_id=1, source_target_pairs={{0,3},{1,2},{2,1},{3,0},{4,7},{5,6},{6,5},{7,4},{8,11},{9,10},{10,... | collective-permute-start | bytes 1179656 | tf_op jit(solution)/shard_map/ppermute | solution.py:412
  86.0 18.4 %collective-permute-start.18 = (bf16[2,96,1536]{2,1,0:T(8,128)(2,1)S(1)}, bf16[2,96,1536]{2,1,0:T(8,128)(2,1)S(1)}, u32[]{:S(2)}, u32[]{:S(2)}) collective-permute-start(bf16[2,96,1536]{2,1,0:T(8,128)(2,1)S(1)} %pad_maximum_fusion.4), channel_id=1, source_target_pairs={{0,16},{1,17},{2,18},{3,19},{4,20},{5,21},{6,22},{7,23},{8,24},{9,... | collective-permute-start | bytes 1769480 | tf_op jit(solution)/shard_map/ppermute | solution.py:412
  88.3 16.0 %collective-permute-start.19 = (bf16[96,768]{1,0:T(8,128)(2,1)}, bf16[96,768]{1,0:T(8,128)(2,1)S(1)}, u32[]{:S(2)}, u32[]{:S(2)}) collective-permute-start(bf16[96,768]{1,0:T(8,128)(2,1)} %collective-permute-done.10), channel_id=1, source_target_pairs={{0,16},{1,17},{2,18},{3,19},{4,20},{5,21},{6,22},{7,23},{8,24},{9,... | collective-permute-start | bytes 442376 | tf_op jit(solution)/shard_map/ppermute | solution.py:412
  106.7 19.8 %collective-permute-start.22 = (bf16[256,768]{1,0:T(8,128)(2,1)S(1)}, bf16[256,768]{1,0:T(8,128)(2,1)S(1)}, u32[]{:S(2)}, u32[]{:S(2)}) collective-permute-start(bf16[256,768]{1,0:T(8,128)(2,1)S(1)} %fusion.17), channel_id=1, source_target_pairs={{0,3},{1,2},{2,1},{3,0},{4,7},{5,6},{6,5},{7,4},{8,11},{9,10},{10,... | collective-permute-start | bytes 1179656 | tf_op jit(solution)/shard_map/ppermute | solution.py:412
  108.2 19.6 %collective-permute-start.23 = (bf16[4,96,1536]{2,1,0:T(8,128)(2,1)S(1)}, bf16[4,96,1536]{2,1,0:T(8,128)(2,1)}, u32[]{:S(2)}, u32[]{:S(2)}) collective-permute-start(bf16[4,96,1536]{2,1,0:T(8,128)(2,1)S(1)} %constant_dynamic-update-slice_fusion.6.near_ref), channel_id=1, source_target_pairs={{0,8},{1,9},{2,10},{3,11},{4,12},{5,13},{6,14},{7,15},{8,0},{9,1},... | collective-permute-start | bytes 3538952 | tf_op jit(solution)/shard_map/ppermute | solution.py:412
  139.8 16.2 %collective-permute-start.26 = (bf16[256,768]{1,0:T(8,128)(2,1)S(1)}, bf16[256,768]{1,0:T(8,128)(2,1)S(1)}, u32[]{:S(2)}, u32[]{:S(2)}) collective-permute-start(bf16[256,768]{1,0:T(8,128)(2,1)S(1)} %convolution_convert_fusion.8), channel_id=1, source_target_pairs={{0,2},{1,3},{2,0},{3,1},{4,6},{5,7},{6,4},{7,5},{8,10},{9,11},{10,... | collective-permute-start | bytes 1179656 | tf_op jit(solution)/shard_map/ppermute | solution.py:412
  140.1 22.9 %collective-permute-start.27 = (bf16[256,768]{1,0:T(8,128)(2,1)S(1)}, bf16[256,768]{1,0:T(8,128)(2,1)S(1)}, u32[]{:S(2)}, u32[]{:S(2)}) collective-permute-start(bf16[256,768]{1,0:T(8,128)(2,1)S(1)} %convolution_convert_fusion.7), channel_id=1, source_target_pairs={{0,3},{1,2},{2,1},{3,0},{4,7},{5,6},{6,5},{7,4},{8,11},{9,10},{10,... | collective-permute-start | bytes 1179656 | tf_op jit(solution)/shard_map/ppermute | solution.py:412
  142.1 21.7 %collective-permute-start.28 = (bf16[256,768]{1,0:T(8,128)(2,1)S(1)}, bf16[256,768]{1,0:T(8,128)(2,1)S(1)}, u32[]{:S(2)}, u32[]{:S(2)}) collective-permute-start(bf16[256,768]{1,0:T(8,128)(2,1)S(1)} %bitcast.111), channel_id=1, source_target_pairs={{0,0},{1,1},{2,2},{3,3},{4,8},{5,9},{6,10},{7,11},{8,4},{9,5},{10,... | collective-permute-start | bytes 1179656 | tf_op jit(solution)/shard_map/ppermute | solution.py:412
  166.7 19.1 %collective-permute-start.31 = (bf16[256,768]{1,0:T(8,128)(2,1)S(1)}, bf16[256,768]{1,0:T(8,128)(2,1)S(1)}, u32[]{:S(2)}, u32[]{:S(2)}) collective-permute-start(bf16[256,768]{1,0:T(8,128)(2,1)S(1)} %fusion.44), channel_id=1, source_target_pairs={{0,3},{1,2},{2,1},{3,0},{4,7},{5,6},{6,5},{7,4},{8,11},{9,10},{10,... | collective-permute-start | bytes 1179656 | tf_op jit(solution)/shard_map/ppermute | solution.py:412
  194.2 17.5 %collective-permute-start.34 = (bf16[256,768]{1,0:T(8,128)(2,1)S(1)}, bf16[256,768]{1,0:T(8,128)(2,1)S(1)}, u32[]{:S(2)}, u32[]{:S(2)}) collective-permute-start(bf16[256,768]{1,0:T(8,128)(2,1)S(1)} %convolution_convert_fusion.4), channel_id=1, source_target_pairs={{0,3},{1,2},{2,1},{3,0},{4,7},{5,6},{6,5},{7,4},{8,11},{9,10},{10,... | collective-permute-start | bytes 1179656 | tf_op jit(solution)/shard_map/ppermute | solution.py:412
  199.7 13.2 %collective-permute-start.36 = (bf16[384,1536]{1,0:T(8,128)(2,1)S(1)}, bf16[384,1536]{1,0:T(8,128)(2,1)S(1)}, u32[]{:S(2)}, u32[]{:S(2)}) collective-permute-start(bf16[384,1536]{1,0:T(8,128)(2,1)S(1)} %select_convert_fusion), channel_id=1, source_target_pairs={{0,8},{1,9},{2,10},{3,11},{4,12},{5,13},{6,14},{7,15},{8,0},{9,1},... | collective-permute-start | bytes 3538952 | tf_op jit(solution)/shard_map/ppermute | solution.py:412
  216.1 16.5 %collective-permute-start.39 = (bf16[256,768]{1,0:T(8,128)(2,1)S(1)}, bf16[256,768]{1,0:T(8,128)(2,1)S(1)}, u32[]{:S(2)}, u32[]{:S(2)}) collective-permute-start(bf16[256,768]{1,0:T(8,128)(2,1)S(1)} %get-tuple-element.187), channel_id=1, source_target_pairs={{0,3},{1,2},{2,1},{3,0},{4,7},{5,6},{6,5},{7,4},{8,11},{9,10},{10,... | collective-permute-start | bytes 1179656 | tf_op jit(solution)/shard_map/ppermute | solution.py:412
  221.9 40.8 %collective-permute-start.41 = (bf16[12,48,768]{2,1,0:T(8,128)(2,1)}, bf16[12,48,768]{2,1,0:T(8,128)(2,1)S(1)}, u32[]{:S(2)}, u32[]{:S(2)}) collective-permute-start(bf16[12,48,768]{2,1,0:T(8,128)(2,1)} %get-tuple-element.197), channel_id=1, source_target_pairs={{0,16},{1,17},{2,18},{3,19},{4,20},{5,21},{6,22},{7,23},{8,24},{9,... | collective-permute-start | bytes 2654216 | tf_op jit(solution)/shard_map/ppermute | solution.py:412
  235.2 27.6 %collective-permute-start.43 = (bf16[256,768]{1,0:T(8,128)(2,1)S(1)}, bf16[256,768]{1,0:T(8,128)(2,1)S(1)}, u32[]{:S(2)}, u32[]{:S(2)}) collective-permute-start(bf16[256,768]{1,0:T(8,128)(2,1)S(1)} %copy-done.23), channel_id=1, source_target_pairs={{0,0},{1,1},{2,2},{3,3},{4,8},{5,9},{6,10},{7,11},{8,4},{9,5},{10,... | collective-permute-start | bytes 1179656 | tf_op jit(solution)/shard_map/ppermute | solution.py:412
  235.9 26.9 %collective-permute-start.42 = (bf16[96,768]{1,0:T(8,128)(2,1)S(1)}, bf16[96,768]{1,0:T(8,128)(2,1)S(1)}, u32[]{:S(2)}, u32[]{:S(2)}) collective-permute-start(bf16[96,768]{1,0:T(8,128)(2,1)S(1)} %add_convert_fusion.3), channel_id=1, source_target_pairs={{0,16},{1,17},{2,18},{3,19},{4,20},{5,21},{6,22},{7,23},{8,24},{9,... | collective-permute-start | bytes 442376 | tf_op jit(solution)/shard_map/ppermute | solution.py:412
  280.3 25.6 %collective-permute-start.50 = (bf16[12,48,768]{2,1,0:T(8,128)(2,1)S(1)}, bf16[12,48,768]{2,1,0:T(8,128)(2,1)}, u32[]{:S(2)}, u32[]{:S(2)}) collective-permute-start(bf16[12,48,768]{2,1,0:T(8,128)(2,1)S(1)} %add.222.mine_ref), channel_id=1, source_target_pairs={{4,0},{5,1},{6,2},{7,3},{8,12},{9,13},{10,14},{11,15},{20,16},{21,... | collective-permute-start | bytes 2654216 | tf_op jit(solution)/shard_map/ppermute | solution.py:412
  288.9 26.5 %collective-permute-start.46 = (bf16[256,768]{1,0:T(8,128)(2,1)}, bf16[256,768]{1,0:T(8,128)(2,1)}, u32[]{:S(2)}, u32[]{:S(2)}) collective-permute-start(bf16[256,768]{1,0:T(8,128)(2,1)} %convolution_convert_fusion.3), channel_id=1, source_target_pairs={{0,1},{1,0},{2,3},{3,2},{4,5},{5,4},{6,7},{7,6},{8,9},{9,8},{10,11... | collective-permute-start | bytes 1179656 | tf_op jit(solution)/shard_map/ppermute | solution.py:412
  289.2 28.4 %collective-permute-start.47 = (bf16[256,768]{1,0:T(8,128)(2,1)}, bf16[256,768]{1,0:T(8,128)(2,1)}, u32[]{:S(2)}, u32[]{:S(2)}) collective-permute-start(bf16[256,768]{1,0:T(8,128)(2,1)} %convolution_convert_fusion.2), channel_id=1, source_target_pairs={{0,2},{1,3},{2,0},{3,1},{4,6},{5,7},{6,4},{7,5},{8,10},{9,11},{10,... | collective-permute-start | bytes 1179656 | tf_op jit(solution)/shard_map/ppermute | solution.py:412
  291.0 34.0 %collective-permute-start.48 = (bf16[256,768]{1,0:T(8,128)(2,1)}, bf16[256,768]{1,0:T(8,128)(2,1)}, u32[]{:S(2)}, u32[]{:S(2)}) collective-permute-start(bf16[256,768]{1,0:T(8,128)(2,1)} %convolution_convert_fusion.1), channel_id=1, source_target_pairs={{0,3},{1,2},{2,1},{3,0},{4,7},{5,6},{6,5},{7,4},{8,11},{9,10},{10,... | collective-permute-start | bytes 1179656 | tf_op jit(solution)/shard_map/ppermute | solution.py:412
  306.0 27.2 %collective-permute-start.51 = (bf16[208,768]{1,0:T(8,128)(2,1)S(1)}, bf16[208,768]{1,0:T(8,128)(2,1)}, u32[]{:S(2)}, u32[]{:S(2)}) collective-permute-start(bf16[208,768]{1,0:T(8,128)(2,1)S(1)} %add.228.mine_ref), channel_id=1, source_target_pairs={{4,0},{5,1},{6,2},{7,3},{8,12},{9,13},{10,14},{11,15},{20,16},{21,... | collective-permute-start | bytes 958472 | tf_op jit(solution)/shard_map/ppermute | solution.py:412
  308.8 19.6 %collective-permute-start.52 = (bf16[96,768]{1,0:T(8,128)(2,1)S(1)}, bf16[96,768]{1,0:T(8,128)(2,1)S(1)}, u32[]{:S(2)}, u32[]{:S(2)}) collective-permute-start(bf16[96,768]{1,0:T(8,128)(2,1)S(1)} %add_convert_fusion.2), channel_id=1, source_target_pairs={{0,4},{1,5},{2,6},{3,7},{4,0},{5,1},{6,2},{7,3},{8,12},{9,13},{10,... | collective-permute-start | bytes 442376 | tf_op jit(solution)/shard_map/ppermute | solution.py:412
  337.3 21.7 %collective-permute-start.58 = (bf16[12,48,768]{2,1,0:T(8,128)(2,1)}, bf16[12,48,768]{2,1,0:T(8,128)(2,1)S(1)}, u32[]{:S(2)}, u32[]{:S(2)}) collective-permute-start(bf16[12,48,768]{2,1,0:T(8,128)(2,1)} %join_feed.1.own_ref), channel_id=1, source_target_pairs={{0,16},{1,17},{2,18},{3,19},{12,28},{13,29},{14,30},{15,31},{16,0}... | collective-permute-start | bytes 2654216 | tf_op jit(solution)/shard_map/ppermute | solution.py:412
  341.2 17.8 %collective-permute-start.59 = (bf16[12,48,768]{2,1,0:T(8,128)(2,1)}, bf16[12,48,768]{2,1,0:T(8,128)(2,1)S(1)}, u32[]{:S(2)}, u32[]{:S(2)}) collective-permute-start(bf16[12,48,768]{2,1,0:T(8,128)(2,1)} %join_feed.1.own_ref), channel_id=1, source_target_pairs={{0,8},{1,9},{2,10},{3,11},{4,12},{5,13},{6,14},{7,15},{8,0},{9,1},... | collective-permute-start | bytes 2654216 | tf_op jit(solution)/shard_map/ppermute | solution.py:412
  341.3 17.7 %collective-permute-start.56 = (bf16[256,768]{1,0:T(8,128)(2,1)S(1)}, bf16[256,768]{1,0:T(8,128)(2,1)S(1)}, u32[]{:S(2)}, u32[]{:S(2)}) collective-permute-start(bf16[256,768]{1,0:T(8,128)(2,1)S(1)} %add_convert_fusion), channel_id=1, source_target_pairs={{0,0},{1,1},{2,2},{3,3},{4,8},{5,9},{6,10},{7,11},{8,4},{9,5},{10,... | collective-permute-start | bytes 1179656 | tf_op jit(solution)/shard_map/ppermute | solution.py:412
  (74 other events, 567.7 us)
